TPU v7x, 128 devices: a whole 4x4x4 slice. The times are simulated.
128 devices in a mesh: row: 4 (over y_lo, core), col: 32 (over x, z, y_hi).
Axes of the slice: x: 4, y: 4 (y_hi: 2, y_lo: 2; y = y_hi * 2 + y_lo), z: 4, core: 2. Of those that a mesh axis runs over, the one named last changes fastest.
Arguments:
- features: bfloat16 [65536, 256], P(('row', 'col')), may hold values from -6 to 6
- tile_values: bfloat16 [256, 64, 256, 256], P('col', 'row'), may hold values from 0 to 1, as said below
- tile_cols: int32 [256, 64], P('col', 'row'), may hold values from 0 to 63
- tile_counts: int32 [256, 4], P('col', 'row'), may hold values from 1 to 16, as said below
- weight: bfloat16 [256, 256], replicated, may hold values from -0.375 to 0.375
- bias: float32 [256], replicated, may hold values from -3 to 3
- cotangent: bfloat16 [65536, 256], P(('col', 'row')), may hold values from -6 to 6
Outputs:
- layer_out: bfloat16 [65536, 256], P(('col', 'row'))
- feature_grad: bfloat16 [65536, 256], P(('row', 'col'))
- weight_grad: float32 [256, 256], replicated
- bias_grad: float32 [256], replicated
Inputs may be any that keep to these rules, and one draw needn't show every extreme that they name: `tile_values`: nonnegative edge weights. `tile_counts`: every draw has some entry equal to 16; the loads differ between the devices' blocks.
All inputs are finite; a program needn't handle non-finite values.
Results may differ from a plain program's by a relative error of at most 0.025.
Values may be sent and summed in bfloat16 or wider, within the bound.
A program may use at most 128 MiB of HBM per device.

v0:
```python
import math

import jax
import jax.numpy as jnp
from jax import lax
from jax.sharding import PartitionSpec as P


def dense_part(hidden, weight, bias, cotangent):
    preact = jnp.dot(hidden, weight, preferred_element_type=jnp.float32) + bias
    output = jax.nn.silu(preact).astype(jnp.bfloat16)
    sigmoid_value = jax.nn.sigmoid(preact)
    slope = sigmoid_value * (1.0 + preact * (1.0 - sigmoid_value))
    preact_grad = (cotangent.astype(jnp.float32) * slope).astype(jnp.bfloat16)
    weight_grad = lax.dot_general(
        hidden, preact_grad, (((0,), (0,)), ((), ())), preferred_element_type=jnp.float32
    )
    bias_grad = jnp.sum(preact_grad.astype(jnp.float32), axis=0)
    hidden_grad = lax.dot_general(
        preact_grad, weight, (((1,), (1,)), ((), ())), preferred_element_type=jnp.float32
    ).astype(jnp.bfloat16)
    return (output, weight_grad, bias_grad, hidden_grad)


def per_device(features, tile_values, tile_cols, tile_counts, weight, bias, cotangent):
    node_dev, width = features.shape
    row_tiles, slot_count, tile_size, _ = tile_values.shape
    column_block = lax.all_gather(features, "col", axis=0, tiled=True)
    column_tiles = column_block.shape[0] // tile_size
    x_tiles = column_block.reshape(column_tiles, tile_size, width)
    live_counts = tile_counts[:, 0]
    slot_top = jnp.max(live_counts)

    def slot_data(slot):
        values = lax.dynamic_index_in_dim(tile_values, slot, 1, keepdims=False)
        columns = lax.dynamic_index_in_dim(tile_cols, slot, 1, keepdims=False)
        live = slot < live_counts
        return (values, columns, live)

    def forward_slot(slot, running):
        values, columns, live = slot_data(slot)
        picked = jnp.take(x_tiles, columns, axis=0) * live[:, None, None].astype(jnp.bfloat16)
        return running + jnp.einsum(
            "tij,tjf->tif", values, picked, preferred_element_type=jnp.float32
        )

    partial_value = lax.fori_loop(
        0, slot_top, forward_slot, jnp.zeros((row_tiles, tile_size, width), jnp.float32)
    )
    partial_value = partial_value.reshape(row_tiles * tile_size, width)
    node_total = node_dev * lax.axis_size("row") * lax.axis_size("col")
    grad_scale = 1.0 / math.sqrt(node_total)
    own_rows = lax.psum_scatter(
        partial_value.astype(jnp.bfloat16), "row", scatter_dimension=0, tiled=True
    )
    layer_out, weight_grad, bias_grad, hidden_grad = dense_part(own_rows, weight, bias, cotangent)
    weight_grad, bias_grad = lax.psum((weight_grad, bias_grad), ("row", "col"))
    grad_block = lax.all_gather(hidden_grad, "row", axis=0, tiled=True)
    grad_tiles = grad_block.reshape(row_tiles, tile_size, width)

    def backward_slot(slot, running):
        values, columns, live = slot_data(slot)
        contrib = jnp.einsum("tij,tif->tjf", values, grad_tiles, preferred_element_type=jnp.float32)
        contrib = contrib * live[:, None, None].astype(jnp.float32)
        return running.at[columns].add(contrib)

    summed = lax.fori_loop(
        0, slot_top, backward_slot, jnp.zeros((column_tiles, tile_size, width), jnp.float32)
    )
    summed = summed.reshape(column_tiles * tile_size, width)
    feature_grad = lax.psum_scatter(
        summed.astype(jnp.bfloat16), "col", scatter_dimension=0, tiled=True
    )
    return (layer_out, feature_grad, weight_grad * grad_scale, bias_grad * grad_scale)


def solution(mesh):
    placed = (
        P(("row", "col"), None),
        P("col", "row", None, None),
        P("col", "row"),
        P("col", "row"),
        P(),
        P(),
        P(("col", "row"), None),
    )
    return jax.shard_map(
        per_device,
        mesh=mesh,
        in_specs=placed,
        out_specs=(P(("col", "row"), None), P(("row", "col"), None), P(), P()),
        check_vma=False,
    )
```

profile of v0, /device:TPU:0, one launch (start us, length us, event | category | flops | bytes accessed | tf_op | source)
XLA Modules:
  0.0 641.7 jit_solution(3709168496130646856)
XLA Ops:
  7.2 0.0 copy-start
  7.2 0.0 all-gather.3.cloned.1.call-start
  7.2 0.7 all-gather.3.cloned.1.call-update
  7.9 0.0 reduce-scatter.3.cloned.1.call-start
  8.0 0.8 copy.12
  8.7 1.3 reduce_max.9
  10.0 107.7 %all-gather.3.cloned.1.call-done = bf16[16384,256]{1,0:T(8,128)(2,1)} async-done(((bf16[512,256]{1,0:T(8,128)(2,1)}), bf16[16384,256]{1,0:T(8,128)(2,1)}) %all-gather.3.cloned.1.call-update) | async-done | bytes 8388624 | tf_op jit(solution)/shard_map/all_gather | solution.py:28
  117.8 0.2 broadcast_in_dim.20
  118.0 0.0 copy-start.2
  118.0 23.1 %while.20 = (s32[]{:T(128)}, f32[8,256,256]{2,1,0:T(8,128)S(1)}, s32[]{:T(128)}, bf16[8,16,256,256]{3,2,1,0:T(8,128)(2,1)}, s32[8,16]{0,1:T(8,128)S(1)}, /*index...) while((s32[]{:T(128)}, f32[8,256,256]{2,1,0:T(8,128)S(1)}, s32[]{:T(128)}, ...), condition=%wide.region_2.3_spmd, body=%wide.region_1.2_spmd.sunk | while | flops 270009408 | bytes 8393067 | solution.py:47
  118.6 0.7 compare_convert_fusion.4
  119.3 4.0 gather_fusion
  123.3 2.1 convolution_add_fusion.3
  126.1 0.7 compare_convert_fusion.4
  126.8 4.0 gather_fusion
  130.8 2.1 convolution_add_fusion.3
  133.6 0.7 compare_convert_fusion.4
  134.3 4.0 gather_fusion
  138.3 2.1 convolution_add_fusion.3
  141.1 1.1 convert_element_type.43
  142.1 0.0 reduce-scatter.3.cloned.1.call-update
  142.2 0.0 all-gather.5.cloned.1.call-start
  142.2 113.6 %reduce-scatter.3.cloned.1.call-done = bf16[512,256]{1,0:T(8,128)(2,1)} async-done(((bf16[2048,256]{1,0:T(8,128)(2,1)}), bf16[512,256]{1,0:T(8,128)(2,1)}) %reduce-scatter.3.cloned.1.call-update) | async-done | bytes 262160 | tf_op jit(solution)/shard_map/reduce_scatter | solution.py:53
  255.8 0.0 copy-done
  255.8 0.0 copy-done.2
  255.8 2.1 convert_reduce_fusion
  257.9 1.0 convolution_convert_fusion
  258.9 0.0 all-gather.5.cloned.1.call-update
  258.9 0.0 all-reduce.2.cloned.1.call-start
  259.0 1.9 fusion.13
  260.9 0.0 all-reduce.2.cloned.1.call-update
  260.9 0.0 reduce-scatter.5.cloned.1.call-start
  261.0 20.0 %all-gather.5.cloned.1.call-done = bf16[2048,256]{1,0:T(8,128)(2,1)} async-done(((bf16[512,256]{1,0:T(8,128)(2,1)}), bf16[2048,256]{1,0:T(8,128)(2,1)}) %all-gather.5.cloned.1.call-update) | async-done | bytes 1048592 | tf_op jit(solution)/shard_map/all_gather | solution.py:58
  280.9 0.0 copy-start.1
  280.9 0.0 copy-start.3
  280.9 7.8 %broadcast_in_dim.21 = f32[64,256,256]{2,1,0:T(8,128)} broadcast(f32[]{:T(128)} %constant.49.clone.1), dimensions={} | broadcast | bytes 16777220 | tf_op jit(solution)/shard_map/broadcast_in_dim | solution.py:68
  288.7 0.0 copy-done.1
  288.7 0.0 copy-done.3
  288.7 21.3 %while.21 = (s32[]{:T(128)}, f32[64,256,256]{2,1,0:T(8,128)}, s32[]{:T(128)}, s32[8,16]{0,1:T(8,128)S(1)}, bf16[8,16,256,256]{3,2,1,0:T(8,128)(2,1)}, /*index=5*...) while((s32[]{:T(128)}, f32[64,256,256]{2,1,0:T(8,128)}, s32[]{:T(128)}, ...), condition=%wide.region_6.7_spmd, body=%wide.region_4.6_spmd.sunk | while | flops 269484064 | bytes 10486107 | solution.py:67
  289.4 1.8 convolution_multiply_fusion.2
  291.2 4.4 scatter_fusion
  296.3 1.8 convolution_multiply_fusion.2
  298.1 4.3 scatter_fusion
  303.1 1.8 convolution_multiply_fusion.2
  304.9 4.4 scatter_fusion
  310.0 9.0 %convert_element_type.49 = bf16[64,256,256]{2,1,0:T(8,128)(2,1)} convert(f32[64,256,256]{2,1,0:T(8,128)} %get-tuple-element.81) | non-fusion elementwise | flops 4194304 | bytes 25165824 | tf_op jit(solution)/shard_map/convert_element_type | solution.py:72
  319.0 0.0 reduce-scatter.5.cloned.1.call-update
  319.1 220.5 %psum.15 = f32[256]{0:T(256)S(1)} all-reduce(f32[256]{0:T(256)S(1)} %get-tuple-element.126), channel_id=1, replica_groups=mesh['row'=4,'col'=32] {'row','col'}, use_global_device_ids=true, to_apply=%region_10.11 | all-reduce | flops 256 | bytes 2048 | tf_op jit(solution)/shard_map/psum | solution.py:57
  539.6 0.6 broadcast_multiply_fusion.1
  540.1 0.0 all-reduce.2.cloned.1.call-done
  540.1 1.7 broadcast_multiply_fusion
  541.8 93.4 %reduce-scatter.5.cloned.1.call-done = bf16[512,256]{1,0:T(8,128)(2,1)} async-done(((bf16[16384,256]{1,0:T(8,128)(2,1)}), bf16[512,256]{1,0:T(8,128)(2,1)}) %reduce-scatter.5.cloned.1.call-update) | async-done | bytes 262160 | tf_op jit(solution)/shard_map/reduce_scatter | solution.py:71
  (12 shorter events, 0.1 us)
Async XLA Ops:
  7.2 248.6 %copy-start = (bf16[256,256]{1,0:T(8,128)(2,1)S(1)}, bf16[256,256]{1,0:T(8,128)(2,1)}, u32[]{:S(2)}) copy-start(bf16[256,256]{1,0:T(8,128)(2,1)} %param.15) | copy-start | bytes 393220
  7.2 110.6 %all-gather.3.cloned.1.call-start = ((), (), s32[]{:S(2)}) async-start(), calls=%async_computation.2 | async-start | bytes 8650752 | tf_op jit(solution)/shard_map/all_gather | solution.py:28
  7.9 247.9 %reduce-scatter.3.cloned.1.call-start = ((), (), s32[]{:S(2)}) async-start(), calls=%async_computation.3 | async-start | bytes 1310720 | tf_op jit(solution)/shard_map/reduce_scatter | solution.py:53
  118.0 137.8 %copy-start.2 = (f32[256]{0:T(256)S(1)}, f32[256]{0:T(256)}, u32[]{:S(2)}) copy-start(f32[256]{0:T(256)} %param.16) | copy-start | bytes 3076
  142.2 138.8 %all-gather.5.cloned.1.call-start = ((), (), s32[]{:S(2)}) async-start(), calls=%async_computation.4 | async-start | bytes 1310720 | tf_op jit(solution)/shard_map/all_gather | solution.py:58
  258.9 281.2 %all-reduce.2.cloned.1.call-start = ((), (), s32[]{:S(2)}) async-start(), calls=%async_computation.6 | async-start | bytes 524288 | tf_op jit(solution)/shard_map/psum | solution.py:57
  260.9 374.3 %reduce-scatter.5.cloned.1.call-start = ((), (), s32[]{:S(2)}) async-start(), calls=%async_computation.5 | async-start | bytes 8650752 | tf_op jit(solution)/shard_map/reduce_scatter | solution.py:71
  280.9 7.8 %copy-start.1 = (bf16[2048,256]{1,0:T(8,128)(2,1)S(1)}, bf16[2048,256]{1,0:T(8,128)(2,1)}, u32[]{:S(2)}) copy-start(bf16[2048,256]{1,0:T(8,128)(2,1)} %all-gather.5.cloned.1.call-done) | copy-start | bytes 3145732
  280.9 7.8 %copy-start.3 = (s32[8]{0:T(128)S(1)}, s32[8]{0:T(128)}, u32[]{:S(2)}) copy-start(s32[8]{0:T(128)} %get-tuple-element.303) | copy-start | bytes 100
Sparse Core Ops, SparseCore 0:
  11.0 106.7 all-gather.2
  142.3 113.4 reduce-scatter.2
  259.0 21.8 all-gather.4
  286.8 142.9 all-reduce.1
  432.7 202.4 reduce-scatter.4
where the time goes:
time: 645 us; the launch traced here: 642 us
  waiting for transfers between devices  335 us (52%)
  blocking collectives  221 us (34%)
  other arithmetic  28.9 us (4%)
  local copies, waits for them, and re-layouts  20.7 us (3%)
  matrix products  16.8 us (3%)
  between operations  13.8 us (2%)
    psum x1, blocking collectives, per_device(): weight_grad, bias_grad = lax.psum((weight_grad, bias_grad), ('row', 'col'))  221 us
    reduce_scatter x1, waiting for transfers between devices, per_device(): lax.psum_scatter(partial_value.astype(jnp.bfloat16), 'row', scatter_dimen...  114 us
    all_gather x1, waiting for transfers between devices, per_device(): column_block = lax.all_gather(features, 'col', axis=0, tiled=True)  108 us
    reduce_scatter x1, waiting for transfers between devices, per_device(): lax.psum_scatter(summed.astype(jnp.bfloat16), 'col', scatter_dimension=0,...  93.4 us
    all_gather x1, waiting for transfers between devices, per_device(): grad_block = lax.all_gather(hidden_grad, 'row', axis=0, tiled=True)  20 us
    scatter-add x3, other arithmetic, backward_slot(): return running.at[columns].add(contrib)  13.2 us
  transfers between devices with their start and end apart: 5, of which 4 were waited for; matrix products, arithmetic and copies ran while one was open for 6% of the time, Pallas kernels for 0%

commit v1 on v0

v1 whole, which is shorter than its diff:
```python
import functools
import math

import jax
import jax.numpy as jnp
from jax import lax
from jax.experimental import pallas as pl
from jax.experimental.pallas import tpu as pltpu
from jax.sharding import PartitionSpec as P

VMEM_LIMIT = 60 * 1024 * 1024


def forward_kernel(cols_ref, counts_ref, a_ref, x_ref, o_ref, acc_ref):
    t = pl.program_id(0)
    slots = a_ref.shape[1]
    last = x_ref.shape[0] - 1
    live = jnp.clip(counts_ref[t], 0, slots)
    acc_ref[...] = jnp.zeros_like(acc_ref)

    def body(s, carry):
        j = jnp.clip(cols_ref[t, s], 0, last)
        acc_ref[...] += jnp.dot(a_ref[0, s], x_ref[j], preferred_element_type=jnp.float32)
        return carry

    lax.fori_loop(0, live, body, 0)
    o_ref[0] = acc_ref[...].astype(o_ref.dtype)


def backward_kernel(cols_ref, counts_ref, a_ref, g_ref, o_ref, acc_ref):
    t = pl.program_id(0)
    slots = a_ref.shape[1]
    last = acc_ref.shape[0] - 1
    live = jnp.clip(counts_ref[t], 0, slots)

    @pl.when(t == 0)
    def _():
        acc_ref[...] = jnp.zeros_like(acc_ref)

    g = g_ref[0]

    def body(s, carry):
        j = jnp.clip(cols_ref[t, s], 0, last)
        acc_ref[j] += lax.dot_general(
            a_ref[0, s], g, (((0,), (0,)), ((), ())), preferred_element_type=jnp.float32
        )
        return carry

    lax.fori_loop(0, live, body, 0)

    @pl.when(t == pl.num_programs(0) - 1)
    def _():
        def put(j, carry):
            o_ref[j] = acc_ref[j].astype(o_ref.dtype)
            return carry

        lax.fori_loop(0, acc_ref.shape[0], put, 0)


def aggregate(tile_values, cols, counts, x_tiles):
    row_tiles, slots, tile, _ = tile_values.shape
    col_tiles, _, width = x_tiles.shape
    return pl.pallas_call(
        forward_kernel,
        out_shape=jax.ShapeDtypeStruct((row_tiles, tile, width), jnp.bfloat16),
        grid_spec=pltpu.PrefetchScalarGridSpec(
            num_scalar_prefetch=2,
            grid=(row_tiles,),
            in_specs=[
                pl.BlockSpec((1, slots, tile, tile), lambda t, c, n: (t, 0, 0, 0)),
                pl.BlockSpec(
                    (col_tiles, tile, width),
                    lambda t, c, n: (0, 0, 0),
                    pipeline_mode=pl.Buffered(1),
                ),
            ],
            out_specs=pl.BlockSpec((1, tile, width), lambda t, c, n: (t, 0, 0)),
            scratch_shapes=[pltpu.VMEM((tile, width), jnp.float32)],
        ),
        compiler_params=pltpu.CompilerParams(vmem_limit_bytes=VMEM_LIMIT),
    )(cols, counts, tile_values, x_tiles)


def aggregate_transposed(tile_values, cols, counts, g_tiles, col_tiles):
    row_tiles, slots, tile, _ = tile_values.shape
    width = g_tiles.shape[-1]
    return pl.pallas_call(
        backward_kernel,
        out_shape=jax.ShapeDtypeStruct((col_tiles, tile, width), jnp.bfloat16),
        grid_spec=pltpu.PrefetchScalarGridSpec(
            num_scalar_prefetch=2,
            grid=(row_tiles,),
            in_specs=[
                pl.BlockSpec((1, slots, tile, tile), lambda t, c, n: (t, 0, 0, 0)),
                pl.BlockSpec((1, tile, width), lambda t, c, n: (t, 0, 0)),
            ],
            out_specs=pl.BlockSpec((col_tiles, tile, width), lambda t, c, n: (0, 0, 0)),
            scratch_shapes=[pltpu.VMEM((col_tiles, tile, width), jnp.float32)],
        ),
        compiler_params=pltpu.CompilerParams(vmem_limit_bytes=VMEM_LIMIT),
    )(cols, counts, tile_values, g_tiles)


def gather_over(x, axis):
    size = lax.axis_size(axis)
    spread = jnp.broadcast_to(x[None], (size,) + x.shape)
    got = lax.all_to_all(spread, axis, 0, 0, tiled=True)
    return got.reshape((size * x.shape[0],) + x.shape[1:])


def sum_scatter_over(x, axis):
    size = lax.axis_size(axis)
    parts = x.reshape((size, x.shape[0] // size) + x.shape[1:])
    got = lax.all_to_all(parts, axis, 0, 0, tiled=True)
    return got.astype(jnp.float32).sum(axis=0)


def dense_part(hidden, weight, bias, cotangent):
    preact = jnp.dot(hidden, weight, preferred_element_type=jnp.float32) + bias
    output = jax.nn.silu(preact).astype(jnp.bfloat16)
    sigmoid_value = jax.nn.sigmoid(preact)
    slope = sigmoid_value * (1.0 + preact * (1.0 - sigmoid_value))
    preact_grad = (cotangent.astype(jnp.float32) * slope).astype(jnp.bfloat16)
    weight_grad = lax.dot_general(
        hidden, preact_grad, (((0,), (0,)), ((), ())), preferred_element_type=jnp.float32
    )
    bias_grad = jnp.sum(preact_grad.astype(jnp.float32), axis=0)
    hidden_grad = lax.dot_general(
        preact_grad, weight, (((1,), (1,)), ((), ())), preferred_element_type=jnp.float32
    ).astype(jnp.bfloat16)
    return (output, weight_grad, bias_grad, hidden_grad)


def all_sum(weight_grad, bias_grad):
    axes = ("row", "col")
    devices = lax.axis_size("row") * lax.axis_size("col")
    width = weight_grad.shape[1]
    rows = weight_grad.shape[0] + 1
    per = -(-rows // devices)
    packed = jnp.concatenate(
        [weight_grad, bias_grad[None], jnp.zeros((per * devices - rows, width), jnp.float32)]
    )
    parts = lax.all_to_all(packed.reshape(devices, per, width), axes, 0, 0, tiled=True)
    summed = parts.sum(axis=0, keepdims=True)
    spread = jnp.broadcast_to(summed, (devices, per, width))
    back = lax.all_to_all(spread, axes, 0, 0, tiled=True).reshape(devices * per, width)
    return back[: rows - 1], back[rows - 1]


def per_device(features, tile_values, tile_cols, tile_counts, weight, bias, cotangent):
    node_dev, width = features.shape
    row_tiles, slot_count, tile_size, _ = tile_values.shape
    column_block = gather_over(features, "col")
    column_tiles = column_block.shape[0] // tile_size
    x_tiles = column_block.reshape(column_tiles, tile_size, width)
    live_counts = tile_counts[:, 0]

    partial_value = aggregate(tile_values, tile_cols, live_counts, x_tiles)
    partial_value = partial_value.reshape(row_tiles * tile_size, width)
    node_total = node_dev * lax.axis_size("row") * lax.axis_size("col")
    grad_scale = 1.0 / math.sqrt(node_total)
    own_rows = sum_scatter_over(partial_value, "row").astype(jnp.bfloat16)
    layer_out, weight_grad, bias_grad, hidden_grad = dense_part(own_rows, weight, bias, cotangent)
    weight_grad, bias_grad = all_sum(weight_grad, bias_grad)
    grad_block = gather_over(hidden_grad, "row")
    grad_tiles = grad_block.reshape(row_tiles, tile_size, width)

    summed = aggregate_transposed(tile_values, tile_cols, live_counts, grad_tiles, column_tiles)
    summed = summed.reshape(column_tiles * tile_size, width)
    feature_grad = sum_scatter_over(summed, "col").astype(jnp.bfloat16)
    return (layer_out, feature_grad, weight_grad * grad_scale, bias_grad * grad_scale)


def solution(mesh):
    placed = (
        P(("row", "col"), None),
        P("col", "row", None, None),
        P("col", "row"),
        P("col", "row"),
        P(),
        P(),
        P(("col", "row"), None),
    )
    return jax.shard_map(
        per_device,
        mesh=mesh,
        in_specs=placed,
        out_specs=(P(("col", "row"), None), P(("row", "col"), None), P(), P()),
        check_vma=False,
    )
```

time: 645 us -> 381 us (0.59)
  the two profiles are of different devices: /device:TPU:0 before, /device:TPU:66 now
where the time goes in v1:
time: 381 us; the launch traced here: 380 us
  waiting for transfers between devices  178 us (47%)
  blocking collectives  105 us (28%)
  starting transfers between devices  51.2 us (13%)
  Pallas kernels  31.3 us (8%)
  other arithmetic  7.26 us (2%)
  local copies, waits for them, and re-layouts  5.16 us (1%)
    all_to_all x2, waiting for transfers between devices, sum_scatter_over(): got = lax.all_to_all(parts, axis, 0, 0, tiled=True)  154 us
    all_to_all x1, blocking collectives, gather_over(): got = lax.all_to_all(spread, axis, 0, 0, tiled=True)  105 us
    all_to_all x2, starting transfers between devices, sum_scatter_over(): got = lax.all_to_all(parts, axis, 0, 0, tiled=True)  26.2 us
    pallas_call x1, Pallas kernels, aggregate_transposed(): pl.pallas_call(backward_kernel, out_shape=jax.ShapeDtypeStruct((col_tiles...  16.8 us
    pallas_call x1, Pallas kernels, aggregate(): pl.pallas_call(forward_kernel, out_shape=jax.ShapeDtypeStruct((row_tiles,...  14.5 us
    all_to_all x1, waiting for transfers between devices, gather_over(): got = lax.all_to_all(spread, axis, 0, 0, tiled=True)  14.3 us
    all_to_all x1, starting transfers between devices, all_sum(): lax.all_to_all(packed.reshape(devices, per, width), axes, 0, 0, tiled=True)  13.1 us
    all_to_all x1, waiting for transfers between devices, all_sum(): lax.all_to_all(packed.reshape(devices, per, width), axes, 0, 0, tiled=True)  9.53 us
  transfers between devices with their start and end apart: 5, of which 4 were waited for; matrix products, arithmetic and copies ran while one was open for 1% of the time, Pallas kernels for 4%

profile of v1, /device:TPU:66, one launch (start us, length us, event | category | flops | bytes accessed | tf_op | source)
XLA Modules:
  0.0 380.3 jit_solution(10692689697359914087)
XLA Ops:
  0.6 0.0 copy-start
  0.6 1.9 broadcast_in_dim.10
  2.6 105.0 %all_to_all.30 = bf16[32,512,256]{2,1,0:T(8,128)(2,1)} all-to-all(bf16[32,512,256]{2,1,0:T(8,128)(2,1)S(1)} %broadcast_in_dim.10), channel_id=1, replica_groups=mesh['row'=4,'col'=32] {'col'}, dimensions={0} | all-to-all | bytes 16777216 | tf_op jit(solution)/shard_map/all_to_all | solution.py:107
  107.6 0.0 copy-start.2
  107.6 0.0 copy-start.3
  107.6 14.5 %shard_map.102 = bf16[8,256,256]{2,1,0:T(8,128)(2,1)} custom-call(s32[8,16]{1,0:T(8,128)} %cols_ref.3, s32[8]{0:T(128)} %bitcast.17, bf16[8,16,256,256]{3,2,1,0:T(8,128)(2,1)} %a_ref.3, bf16[64,256,256]{2,1,0:T(8,128)(2,1)} %bitcast.14), custom_call_target="tpu_custom_call" | custom-call | tf_op jit(solution)/shard_map/pallas_call | solution.py:63
  122.0 6.7 %all-to-all-start.1 = ((bf16[4,512,256]{2,1,0:T(8,128)(2,1)}), bf16[4,512,256]{2,1,0:T(8,128)(2,1)S(1)}, u32[]{:S(2)}, u32[]{:S(2)}) async-start(bf16[4,512,256]{2,1,0:T(8,128)(2,1)} %bitcast.16), calls=%async_computation.1 | async-start | bytes 2097152 | tf_op jit(solution)/shard_map/all_to_all | solution.py:114
  128.8 0.1 pad.2.clone
  128.8 14.8 %all-to-all-done.1 = bf16[4,512,256]{2,1,0:T(8,128)(2,1)S(1)} async-done(((bf16[4,512,256]{2,1,0:T(8,128)(2,1)}), bf16[4,512,256]{2,1,0:T(8,128)(2,1)S(1)}, u32[]{:S(2)}, u32[]{:S(2)}) %all-to-all-start.1) | async-done | bytes 1048608 | tf_op jit(solution)/shard_map/all_to_all | solution.py:114
  143.7 0.3 reduce_sum.42
  143.9 0.0 copy-done
  143.9 0.0 copy-done.2
  143.9 0.0 copy-done.3
  144.0 1.1 convert_reduce_fusion
  145.1 0.3 fusion
  145.3 0.1 maximum_maximum_fusion
  145.5 1.0 reshape.20
  146.4 13.1 %all-to-all-start.4 = ((f32[128,3,256]{2,1,0:T(4,128)}), f32[128,3,256]{2,1,0:T(4,128)S(1)}, u32[]{:S(2)}, u32[]{:S(2)}) async-start(f32[128,3,256]{2,1,0:T(4,128)} %reshape.20), calls=%async_computation.4 | async-start | bytes 1048576 | tf_op jit(solution)/shard_map/all_to_all | solution.py:143
  159.5 0.3 convolution_convert_fusion
  159.8 9.5 %all-to-all-done.4 = f32[128,3,256]{2,1,0:T(4,128)S(1)} async-done(((f32[128,3,256]{2,1,0:T(4,128)}), f32[128,3,256]{2,1,0:T(4,128)S(1)}, u32[]{:S(2)}, u32[]{:S(2)}) %all-to-all-start.4) | async-done | bytes 393248 | tf_op jit(solution)/shard_map/all_to_all | solution.py:143
  169.3 1.0 broadcast_in_dim.11
  170.3 3.5 all-to-all-start.2
  173.8 0.1 reduce_sum.45
  174.0 14.3 %all-to-all-done.2 = bf16[4,512,256]{2,1,0:T(8,128)(2,1)S(1)} async-done(((bf16[4,512,256]{2,1,0:T(8,128)(2,1)}), bf16[4,512,256]{2,1,0:T(8,128)(2,1)S(1)}, u32[]{:S(2)}, u32[]{:S(2)}) %all-to-all-start.2) | async-done | bytes 1048608 | tf_op jit(solution)/shard_map/all_to_all | solution.py:107
  188.3 0.0 copy-start.1
  188.3 1.0 broadcast_in_dim.14
  189.2 8.4 %all-to-all-start.5 = ((f32[128,3,256]{2,1,0:T(4,128)}), f32[128,3,256]{2,1,0:T(4,128)S(1)}, u32[]{:S(2)}, u32[]{:S(2)}) async-start(f32[128,3,256]{2,1,0:T(4,128)} %broadcast_in_dim.14), calls=%async_computation.5 | async-start | bytes 1048576 | tf_op jit(solution)/shard_map/all_to_all | solution.py:146
  197.7 0.0 copy-done.1
  197.7 16.8 %shard_map.103 = bf16[64,256,256]{2,1,0:T(8,128)(2,1)} custom-call(s32[8,16]{1,0:T(8,128)} %cols_ref.3, s32[8]{0:T(128)} %bitcast.18, bf16[8,16,256,256]{3,2,1,0:T(8,128)(2,1)} %a_ref.3, bf16[8,256,256]{2,1,0:T(8,128)(2,1)} %bitcast.15), custom_call_target="tpu_custom_call" | custom-call | tf_op jit(solution)/shard_map/pallas_call | solution.py:87
  214.5 0.0 all-to-all-done.5
  214.5 19.5 %all-to-all-start.3 = ((bf16[32,512,256]{2,1,0:T(8,128)(2,1)}), bf16[32,512,256]{2,1,0:T(8,128)(2,1)}, u32[]{:S(2)}, u32[]{:S(2)}) async-start(bf16[32,512,256]{2,1,0:T(8,128)(2,1)} %bitcast.13), calls=%async_computation.3 | async-start | bytes 16777216 | tf_op jit(solution)/shard_map/all_to_all | solution.py:114
  234.0 0.2 reshape.21
  234.2 0.6 slice_multiply_fusion.1
  234.8 0.7 slice_multiply_fusion
  235.5 139.4 %all-to-all-done.3 = bf16[32,512,256]{2,1,0:T(8,128)(2,1)} async-done(((bf16[32,512,256]{2,1,0:T(8,128)(2,1)}), bf16[32,512,256]{2,1,0:T(8,128)(2,1)}, u32[]{:S(2)}, u32[]{:S(2)}) %all-to-all-start.3) | async-done | bytes 8388640 | tf_op jit(solution)/shard_map/all_to_all | solution.py:114
  374.9 5.5 %reduce_sum.43 = bf16[512,256]{1,0:T(8,128)(2,1)} reduce(bf16[32,512,256]{2,1,0:T(8,128)(2,1)} %all-to-all-done.3, bf16[]{:T(256)} %constant.4.clone.1), dimensions={0}, to_apply=%region_1.2 | reduce | flops 4063232 | bytes 8650754 | tf_op jit(solution)/shard_map/reduce_sum | solution.py:115
  (1 shorter events, 0.0 us)
Async XLA Ops:
  0.6 143.3 %copy-start = (bf16[256,256]{1,0:T(8,128)(2,1)S(1)}, bf16[256,256]{1,0:T(8,128)(2,1)}, u32[]{:S(2)}) copy-start(bf16[256,256]{1,0:T(8,128)(2,1)} %param.11) | copy-start | bytes 393220
  107.6 36.3 %copy-start.2 = (bf16[512,256]{1,0:T(8,128)(2,1)S(1)}, bf16[512,256]{1,0:T(8,128)(2,1)}, u32[]{:S(2)}) copy-start(bf16[512,256]{1,0:T(8,128)(2,1)} %param.13) | copy-start | bytes 786436
  107.6 36.4 %copy-start.3 = (f32[256]{0:T(256)S(1)}, f32[256]{0:T(256)}, u32[]{:S(2)}) copy-start(f32[256]{0:T(256)} %param.12) | copy-start | bytes 3076
  122.0 21.6 %all-to-all-start.1 = ((bf16[4,512,256]{2,1,0:T(8,128)(2,1)}), bf16[4,512,256]{2,1,0:T(8,128)(2,1)S(1)}, u32[]{:S(2)}, u32[]{:S(2)}) async-start(bf16[4,512,256]{2,1,0:T(8,128)(2,1)} %bitcast.16), calls=%async_computation.1 | async-start | bytes 2097152 | tf_op jit(solution)/shard_map/all_to_all | solution.py:114
  146.4 22.9 %all-to-all-start.4 = ((f32[128,3,256]{2,1,0:T(4,128)}), f32[128,3,256]{2,1,0:T(4,128)S(1)}, u32[]{:S(2)}, u32[]{:S(2)}) async-start(f32[128,3,256]{2,1,0:T(4,128)} %reshape.20), calls=%async_computation.4 | async-start | bytes 1048576 | tf_op jit(solution)/shard_map/all_to_all | solution.py:143
  170.3 18.0 %all-to-all-start.2 = ((bf16[4,512,256]{2,1,0:T(8,128)(2,1)}), bf16[4,512,256]{2,1,0:T(8,128)(2,1)S(1)}, u32[]{:S(2)}, u32[]{:S(2)}) async-start(bf16[4,512,256]{2,1,0:T(8,128)(2,1)} %broadcast_in_dim.11), calls=%async_computation.2 | async-start | bytes 2097152 | tf_op jit(solution)/shard_map/all_to_all | solution.py:107
  188.3 9.4 %copy-start.1 = (bf16[4,512,256]{2,1,0:T(8,128)(2,1)}, bf16[4,512,256]{2,1,0:T(8,128)(2,1)S(1)}, u32[]{:S(2)}) copy-start(bf16[4,512,256]{2,1,0:T(8,128)(2,1)S(1)} %all-to-all-done.2) | copy-start | bytes 3145732
  189.2 25.3 %all-to-all-start.5 = ((f32[128,3,256]{2,1,0:T(4,128)}), f32[128,3,256]{2,1,0:T(4,128)S(1)}, u32[]{:S(2)}, u32[]{:S(2)}) async-start(f32[128,3,256]{2,1,0:T(4,128)} %broadcast_in_dim.14), calls=%async_computation.5 | async-start | bytes 1048576 | tf_op jit(solution)/shard_map/all_to_all | solution.py:146
  214.5 160.4 %all-to-all-start.3 = ((bf16[32,512,256]{2,1,0:T(8,128)(2,1)}), bf16[32,512,256]{2,1,0:T(8,128)(2,1)}, u32[]{:S(2)}, u32[]{:S(2)}) async-start(bf16[32,512,256]{2,1,0:T(8,128)(2,1)} %bitcast.13), calls=%async_computation.3 | async-start | bytes 16777216 | tf_op jit(solution)/shard_map/all_to_all | solution.py:114

commit v2 on v1

--- a/solution.py
+++ b/solution.py
@@ -131,22 +131,6 @@
     return (output, weight_grad, bias_grad, hidden_grad)
 
 
-def all_sum(weight_grad, bias_grad):
-    axes = ("row", "col")
-    devices = lax.axis_size("row") * lax.axis_size("col")
-    width = weight_grad.shape[1]
-    rows = weight_grad.shape[0] + 1
-    per = -(-rows // devices)
-    packed = jnp.concatenate(
-        [weight_grad, bias_grad[None], jnp.zeros((per * devices - rows, width), jnp.float32)]
-    )
-    parts = lax.all_to_all(packed.reshape(devices, per, width), axes, 0, 0, tiled=True)
-    summed = parts.sum(axis=0, keepdims=True)
-    spread = jnp.broadcast_to(summed, (devices, per, width))
-    back = lax.all_to_all(spread, axes, 0, 0, tiled=True).reshape(devices * per, width)
-    return back[: rows - 1], back[rows - 1]
-
-
 def per_device(features, tile_values, tile_cols, tile_counts, weight, bias, cotangent):
     node_dev, width = features.shape
     row_tiles, slot_count, tile_size, _ = tile_values.shape
@@ -161,7 +145,8 @@
     grad_scale = 1.0 / math.sqrt(node_total)
     own_rows = sum_scatter_over(partial_value, "row").astype(jnp.bfloat16)
     layer_out, weight_grad, bias_grad, hidden_grad = dense_part(own_rows, weight, bias, cotangent)
-    weight_grad, bias_grad = all_sum(weight_grad, bias_grad)
+    packed = lax.psum(jnp.concatenate([weight_grad, bias_grad[None]]), ("row", "col"))
+    weight_grad, bias_grad = packed[:-1], packed[-1]
     grad_block = gather_over(hidden_grad, "row")
     grad_tiles = grad_block.reshape(row_tiles, tile_size, width)
 

time: 381 us -> 456 us (1.20)
  waiting for transfers between devices: 178 us -> 226 us
  blocking collectives: 105 us -> 150 us
  starting transfers between devices: 51.2 us -> 21.1 us
  between operations: 0.75 us -> 14.1 us
    psum x0 -> x1, waiting for transfers between devices: none -> 226 us  [per_device(): lax.psum(jnp.concatenate([weight_grad, bias_grad[None]]), ('row', 'col'))]
    all_to_all x2 -> x1, waiting for transfers between devices: 154 us -> 0.01 us  [sum_scatter_over(): got = lax.all_to_all(parts, axis, 0, 0, tiled=True)]
    all_to_all x0 -> x1, blocking collectives: none -> 27.4 us  [sum_scatter_over(): got = lax.all_to_all(parts, axis, 0, 0, tiled=True)]
    all_to_all x3 -> x0, starting transfers between devices: 25 us -> none  [the longest x1 13.1 us: all_sum(): lax.all_to_all(packed.reshape(devices, per, width), axes, 0, 0, tiled=True)]
    all_to_all x3 -> x0, waiting for transfers between devices: 23.8 us -> none  [the longest x1 14.3 us: gather_over(): got = lax.all_to_all(spread, axis, 0, 0, tiled=True)]
    all_to_all x1 -> x2, blocking collectives: 105 us -> 123 us  [gather_over(): got = lax.all_to_all(spread, axis, 0, 0, tiled=True)]
    all_to_all x2 -> x1, starting transfers between devices: 26.2 us -> 21.1 us  [sum_scatter_over(): got = lax.all_to_all(parts, axis, 0, 0, tiled=True)]
  transfers between devices with their start and end apart: 5 -> 2, of which waited for: 4 -> 1; matrix products, arithmetic and copies ran while one was open for 1% -> 1% of each run, Pallas kernels for 4% -> 0%
where the time goes in v2:
time: 456 us; the launch traced here: 452 us
  waiting for transfers between devices  226 us (50%)
  blocking collectives  150 us (33%)
  Pallas kernels  28.3 us (6%)
  starting transfers between devices  21.1 us (5%)
  between operations  14.1 us (3%)
  other arithmetic  9.35 us (2%)
    psum x1, waiting for transfers between devices, per_device(): lax.psum(jnp.concatenate([weight_grad, bias_grad[None]]), ('row', 'col'))  226 us
    all_to_all x2, blocking collectives, gather_over(): got = lax.all_to_all(spread, axis, 0, 0, tiled=True)  123 us
    all_to_all x1, blocking collectives, sum_scatter_over(): got = lax.all_to_all(parts, axis, 0, 0, tiled=True)  27.4 us
    all_to_all x1, starting transfers between devices, sum_scatter_over(): got = lax.all_to_all(parts, axis, 0, 0, tiled=True)  21.1 us
    pallas_call x1, Pallas kernels, aggregate_transposed(): pl.pallas_call(backward_kernel, out_shape=jax.ShapeDtypeStruct((col_tiles...  15.2 us
    pallas_call x1, Pallas kernels, aggregate(): pl.pallas_call(forward_kernel, out_shape=jax.ShapeDtypeStruct((row_tiles,...  13.1 us
  transfers between devices with their start and end apart: 2, of which 1 were waited for; matrix products, arithmetic and copies ran while one was open for 1% of the time, Pallas kernels for 0%

profile of v2, /device:TPU:66, one launch (start us, length us, event | category | flops | bytes accessed | tf_op | source)
XLA Modules:
  0.0 452.2 jit_solution(7950717460916434919)
XLA Ops:
  7.2 0.0 copy-start
  7.2 1.9 broadcast_in_dim.6
  9.1 105.0 %all_to_all.20 = bf16[32,512,256]{2,1,0:T(8,128)(2,1)} all-to-all(bf16[32,512,256]{2,1,0:T(8,128)(2,1)S(1)} %broadcast_in_dim.6), channel_id=1, replica_groups=mesh['row'=4,'col'=32] {'col'}, dimensions={0} | all-to-all | bytes 16777216 | tf_op jit(solution)/shard_map/all_to_all | solution.py:107
  114.1 0.0 copy-start.1
  114.1 0.0 copy-start.2
  114.1 13.1 %shard_map.102 = bf16[8,256,256]{2,1,0:T(8,128)(2,1)} custom-call(s32[8,16]{1,0:T(8,128)} %cols_ref.3, s32[8]{0:T(128)} %bitcast.17, bf16[8,16,256,256]{3,2,1,0:T(8,128)(2,1)} %a_ref.3, bf16[64,256,256]{2,1,0:T(8,128)(2,1)} %bitcast.14), custom_call_target="tpu_custom_call" | custom-call | tf_op jit(solution)/shard_map/pallas_call | solution.py:63
  127.2 27.4 %all_to_all.21 = bf16[4,512,256]{2,1,0:T(8,128)(2,1)S(1)} all-to-all(bf16[4,512,256]{2,1,0:T(8,128)(2,1)} %bitcast.15), channel_id=1, replica_groups=mesh['row'=4,'col'=32] {'row'}, dimensions={0} | all-to-all | bytes 2097152 | tf_op jit(solution)/shard_map/all_to_all | solution.py:114
  154.6 0.3 reduce_sum.33
  154.9 0.0 copy-done
  154.9 0.0 copy-done.1
  154.9 0.0 copy-done.2
  154.9 1.1 convert_reduce_fusion
  156.0 0.3 convolution_convert_fusion
  156.3 0.1 broadcast_in_dim.7
  156.4 17.6 %all_to_all.22 = bf16[4,512,256]{2,1,0:T(8,128)(2,1)} all-to-all(bf16[4,512,256]{2,1,0:T(8,128)(2,1)S(1)} %broadcast_in_dim.7), channel_id=1, replica_groups=mesh['row'=4,'col'=32] {'row'}, dimensions={0} | all-to-all | bytes 2097152 | tf_op jit(solution)/shard_map/all_to_all | solution.py:107
  174.0 15.2 %shard_map.103 = bf16[64,256,256]{2,1,0:T(8,128)(2,1)} custom-call(s32[8,16]{1,0:T(8,128)} %cols_ref.3, s32[8]{0:T(128)} %bitcast.18, bf16[8,16,256,256]{3,2,1,0:T(8,128)(2,1)} %a_ref.3, bf16[8,256,256]{2,1,0:T(8,128)(2,1)} %bitcast.16), custom_call_target="tpu_custom_call" | custom-call | tf_op jit(solution)/shard_map/pallas_call | solution.py:87
  189.1 21.1 %all-to-all-start.3 = ((bf16[32,512,256]{2,1,0:T(8,128)(2,1)}), bf16[32,512,256]{2,1,0:T(8,128)(2,1)}, u32[]{:S(2)}, u32[]{:S(2)}) async-start(bf16[32,512,256]{2,1,0:T(8,128)(2,1)} %bitcast.13), calls=%async_computation.3 | async-start | bytes 16777216 | tf_op jit(solution)/shard_map/all_to_all | solution.py:114
  210.2 0.0 all-reduce.2.cloned.1.call-start
  210.3 0.3 fusion
  210.5 0.7 pad_maximum_fusion
  211.2 0.0 all-reduce.2.cloned.1.call-update
  211.3 225.7 %all-reduce.2.cloned.1.call-done = f32[257,256]{1,0:T(8,128)} async-done(((f32[257,256]{1,0:T(8,128)}), f32[257,256]{1,0:T(8,128)}) %all-reduce.2.cloned.1.call-update) | async-done | bytes 263184 | tf_op jit(solution)/shard_map/psum | solution.py:148
  437.0 1.3 slice_multiply_fusion.1
  438.2 1.7 slice_multiply_fusion
  439.9 0.0 all-to-all-done.3
  439.9 5.5 %reduce_sum.34 = bf16[512,256]{1,0:T(8,128)(2,1)} reduce(bf16[32,512,256]{2,1,0:T(8,128)(2,1)} %all-to-all-done.3, bf16[]{:T(256)} %constant.4.clone.1), dimensions={0}, to_apply=%region_1.2 | reduce | flops 4063232 | bytes 8650754 | tf_op jit(solution)/shard_map/reduce_sum | solution.py:115
Async XLA Ops:
  7.2 147.7 %copy-start = (bf16[256,256]{1,0:T(8,128)(2,1)S(1)}, bf16[256,256]{1,0:T(8,128)(2,1)}, u32[]{:S(2)}) copy-start(bf16[256,256]{1,0:T(8,128)(2,1)} %param.11) | copy-start | bytes 393220
  114.1 40.7 %copy-start.1 = (bf16[512,256]{1,0:T(8,128)(2,1)S(1)}, bf16[512,256]{1,0:T(8,128)(2,1)}, u32[]{:S(2)}) copy-start(bf16[512,256]{1,0:T(8,128)(2,1)} %param.13) | copy-start | bytes 786436
  114.1 40.8 %copy-start.2 = (f32[256]{0:T(256)S(1)}, f32[256]{0:T(256)}, u32[]{:S(2)}) copy-start(f32[256]{0:T(256)} %param.12) | copy-start | bytes 3076
  189.1 250.7 %all-to-all-start.3 = ((bf16[32,512,256]{2,1,0:T(8,128)(2,1)}), bf16[32,512,256]{2,1,0:T(8,128)(2,1)}, u32[]{:S(2)}, u32[]{:S(2)}) async-start(bf16[32,512,256]{2,1,0:T(8,128)(2,1)} %bitcast.13), calls=%async_computation.3 | async-start | bytes 16777216 | tf_op jit(solution)/shard_map/all_to_all | solution.py:114
  210.2 226.7 %all-reduce.2.cloned.1.call-start = ((), (), s32[]{:S(2)}) async-start(), calls=%async_computation.4 | async-start | bytes 540672 | tf_op jit(solution)/shard_map/psum | solution.py:148
Sparse Core Ops, SparseCore 0:
  215.8 221.1 all-reduce.1

commit v3 on v1

--- a/solution.py
+++ b/solution.py
@@ -11,42 +11,37 @@
 VMEM_LIMIT = 60 * 1024 * 1024
 
 
-def forward_kernel(cols_ref, counts_ref, a_ref, x_ref, o_ref, acc_ref):
+def forward_kernel(cols_ref, counts_ref, a_ref, x_ref, o_ref):
     t = pl.program_id(0)
     slots = a_ref.shape[1]
     last = x_ref.shape[0] - 1
-    live = jnp.clip(counts_ref[t], 0, slots)
-    acc_ref[...] = jnp.zeros_like(acc_ref)
-
-    def body(s, carry):
+    live = counts_ref[t]
+    acc = None
+    for s in range(slots):
         j = jnp.clip(cols_ref[t, s], 0, last)
-        acc_ref[...] += jnp.dot(a_ref[0, s], x_ref[j], preferred_element_type=jnp.float32)
-        return carry
-
-    lax.fori_loop(0, live, body, 0)
-    o_ref[0] = acc_ref[...].astype(o_ref.dtype)
+        term = jnp.dot(a_ref[0, s], x_ref[j], preferred_element_type=jnp.float32)
+        term = jnp.where(s < live, term, 0.0)
+        acc = term if acc is None else acc + term
+    o_ref[0] = acc.astype(o_ref.dtype)
 
 
 def backward_kernel(cols_ref, counts_ref, a_ref, g_ref, o_ref, acc_ref):
     t = pl.program_id(0)
     slots = a_ref.shape[1]
     last = acc_ref.shape[0] - 1
-    live = jnp.clip(counts_ref[t], 0, slots)
+    live = counts_ref[t]
 
     @pl.when(t == 0)
     def _():
         acc_ref[...] = jnp.zeros_like(acc_ref)
 
     g = g_ref[0]
-
-    def body(s, carry):
+    for s in range(slots):
         j = jnp.clip(cols_ref[t, s], 0, last)
-        acc_ref[j] += lax.dot_general(
+        term = lax.dot_general(
             a_ref[0, s], g, (((0,), (0,)), ((), ())), preferred_element_type=jnp.float32
         )
-        return carry
-
-    lax.fori_loop(0, live, body, 0)
+        acc_ref[j] += jnp.where(s < live, term, 0.0)
 
     @pl.when(t == pl.num_programs(0) - 1)
     def _():
@@ -75,7 +70,6 @@
                 ),
             ],
             out_specs=pl.BlockSpec((1, tile, width), lambda t, c, n: (t, 0, 0)),
-            scratch_shapes=[pltpu.VMEM((tile, width), jnp.float32)],
         ),
         compiler_params=pltpu.CompilerParams(vmem_limit_bytes=VMEM_LIMIT),
     )(cols, counts, tile_values, x_tiles)

time: 381 us -> 359 us (0.942); the launches traced: 380 us -> 354 us
  starting transfers between devices: 51.2 us -> 33.4 us
  waiting for transfers between devices: 178 us -> 169 us
    all_to_all x2, starting transfers between devices: 26.2 us -> 13.5 us  [sum_scatter_over(): got = lax.all_to_all(parts, axis, 0, 0, tiled=True)]
    all_to_all x2, waiting for transfers between devices: 154 us -> 145 us  [sum_scatter_over(): got = lax.all_to_all(parts, axis, 0, 0, tiled=True)]
    all_to_all x1, starting transfers between devices: 13.1 us -> 7.92 us  [all_sum(): lax.all_to_all(packed.reshape(devices, per, width), axes, 0, 0, tiled=True)]
  transfers between devices with their start and end apart: 5 -> 5, of which waited for: 4 -> 4; matrix products, arithmetic and copies ran while one was open for 1% -> 1% of each run, Pallas kernels for 4% -> 5%
where the time goes in v3:
time: 359 us; the launch traced here: 354 us
  waiting for transfers between devices  169 us (47%)
  blocking collectives  105 us (29%)
  starting transfers between devices  33.4 us (9%)
  Pallas kernels  31.6 us (9%)
  other arithmetic  7.26 us (2%)
  local copies, waits for them, and re-layouts  5.16 us (1%)
    all_to_all x2, waiting for transfers between devices, sum_scatter_over(): got = lax.all_to_all(parts, axis, 0, 0, tiled=True)  145 us
    all_to_all x1, blocking collectives, gather_over(): got = lax.all_to_all(spread, axis, 0, 0, tiled=True)  105 us
    pallas_call x1, Pallas kernels, aggregate_transposed(): pl.pallas_call(backward_kernel, out_shape=jax.ShapeDtypeStruct((col_tiles...  17 us
    pallas_call x1, Pallas kernels, aggregate(): pl.pallas_call(forward_kernel, out_shape=jax.ShapeDtypeStruct((row_tiles,...  14.6 us
    all_to_all x1, waiting for transfers between devices, gather_over(): got = lax.all_to_all(spread, axis, 0, 0, tiled=True)  14.3 us
    all_to_all x2, starting transfers between devices, sum_scatter_over(): got = lax.all_to_all(parts, axis, 0, 0, tiled=True)  13.5 us
    all_to_all x1, waiting for transfers between devices, all_sum(): lax.all_to_all(packed.reshape(devices, per, width), axes, 0, 0, tiled=True)  9.53 us
    all_to_all x1, starting transfers between devices, all_sum(): lax.all_to_all(spread, axes, 0, 0, tiled=True).reshape(devices * per, width)  8.43 us
  transfers between devices with their start and end apart: 5, of which 4 were waited for; matrix products, arithmetic and copies ran while one was open for 1% of the time, Pallas kernels for 5%

profile of v3, /device:TPU:66, one launch (start us, length us, event | category | flops | bytes accessed | tf_op | source)
XLA Modules:
  0.0 353.7 jit_solution(9861943149688660831)
XLA Ops:
  0.6 0.0 copy-start
  0.6 1.9 broadcast_in_dim.10
  2.6 105.0 %all_to_all.30 = bf16[32,512,256]{2,1,0:T(8,128)(2,1)} all-to-all(bf16[32,512,256]{2,1,0:T(8,128)(2,1)S(1)} %broadcast_in_dim.10), channel_id=1, replica_groups=mesh['row'=4,'col'=32] {'col'}, dimensions={0} | all-to-all | bytes 16777216 | tf_op jit(solution)/shard_map/all_to_all | solution.py:101
  107.6 0.0 copy-start.2
  107.6 0.0 copy-start.3
  107.6 14.6 %shard_map.102 = bf16[8,256,256]{2,1,0:T(8,128)(2,1)} custom-call(s32[8,16]{1,0:T(8,128)} %cols_ref.3, s32[8]{0:T(128)} %bitcast.17, bf16[8,16,256,256]{3,2,1,0:T(8,128)(2,1)} %a_ref.3, bf16[64,256,256]{2,1,0:T(8,128)(2,1)} %bitcast.14), custom_call_target="tpu_custom_call" | custom-call | tf_op jit(solution)/shard_map/pallas_call | solution.py:58
  122.2 3.5 all-to-all-start.1
  125.7 0.1 pad.2.clone
  125.8 14.3 %all-to-all-done.1 = bf16[4,512,256]{2,1,0:T(8,128)(2,1)S(1)} async-done(((bf16[4,512,256]{2,1,0:T(8,128)(2,1)}), bf16[4,512,256]{2,1,0:T(8,128)(2,1)S(1)}, u32[]{:S(2)}, u32[]{:S(2)}) %all-to-all-start.1) | async-done | bytes 1048608 | tf_op jit(solution)/shard_map/all_to_all | solution.py:108
  140.1 0.3 reduce_sum.42
  140.4 0.0 copy-done
  140.4 0.0 copy-done.2
  140.4 0.0 copy-done.3
  140.4 1.1 convert_reduce_fusion
  141.5 0.3 fusion
  141.8 0.1 maximum_maximum_fusion
  141.9 1.0 reshape.20
  142.9 7.9 %all-to-all-start.4 = ((f32[128,3,256]{2,1,0:T(4,128)}), f32[128,3,256]{2,1,0:T(4,128)S(1)}, u32[]{:S(2)}, u32[]{:S(2)}) async-start(f32[128,3,256]{2,1,0:T(4,128)} %reshape.20), calls=%async_computation.4 | async-start | bytes 1048576 | tf_op jit(solution)/shard_map/all_to_all | solution.py:137
  150.8 0.3 convolution_convert_fusion
  151.1 9.5 %all-to-all-done.4 = f32[128,3,256]{2,1,0:T(4,128)S(1)} async-done(((f32[128,3,256]{2,1,0:T(4,128)}), f32[128,3,256]{2,1,0:T(4,128)S(1)}, u32[]{:S(2)}, u32[]{:S(2)}) %all-to-all-start.4) | async-done | bytes 393248 | tf_op jit(solution)/shard_map/all_to_all | solution.py:137
  160.6 1.0 broadcast_in_dim.11
  161.6 3.5 all-to-all-start.2
  165.2 0.1 reduce_sum.45
  165.3 14.3 %all-to-all-done.2 = bf16[4,512,256]{2,1,0:T(8,128)(2,1)S(1)} async-done(((bf16[4,512,256]{2,1,0:T(8,128)(2,1)}), bf16[4,512,256]{2,1,0:T(8,128)(2,1)S(1)}, u32[]{:S(2)}, u32[]{:S(2)}) %all-to-all-start.2) | async-done | bytes 1048608 | tf_op jit(solution)/shard_map/all_to_all | solution.py:101
  179.6 0.0 copy-start.1
  179.6 1.0 broadcast_in_dim.14
  180.6 8.4 %all-to-all-start.5 = ((f32[128,3,256]{2,1,0:T(4,128)}), f32[128,3,256]{2,1,0:T(4,128)S(1)}, u32[]{:S(2)}, u32[]{:S(2)}) async-start(f32[128,3,256]{2,1,0:T(4,128)} %broadcast_in_dim.14), calls=%async_computation.5 | async-start | bytes 1048576 | tf_op jit(solution)/shard_map/all_to_all | solution.py:140
  189.0 0.0 copy-done.1
  189.0 17.0 %shard_map.103 = bf16[64,256,256]{2,1,0:T(8,128)(2,1)} custom-call(s32[8,16]{1,0:T(8,128)} %cols_ref.3, s32[8]{0:T(128)} %bitcast.18, bf16[8,16,256,256]{3,2,1,0:T(8,128)(2,1)} %a_ref.3, bf16[8,256,256]{2,1,0:T(8,128)(2,1)} %bitcast.15), custom_call_target="tpu_custom_call" | custom-call | tf_op jit(solution)/shard_map/pallas_call | solution.py:81
  206.0 0.0 all-to-all-done.5
  206.0 10.0 %all-to-all-start.3 = ((bf16[32,512,256]{2,1,0:T(8,128)(2,1)}), bf16[32,512,256]{2,1,0:T(8,128)(2,1)}, u32[]{:S(2)}, u32[]{:S(2)}) async-start(bf16[32,512,256]{2,1,0:T(8,128)(2,1)} %bitcast.13), calls=%async_computation.3 | async-start | bytes 16777216 | tf_op jit(solution)/shard_map/all_to_all | solution.py:108
  216.0 0.2 reshape.21
  216.2 0.6 slice_multiply_fusion.1
  216.8 0.7 slice_multiply_fusion
  217.5 130.7 %all-to-all-done.3 = bf16[32,512,256]{2,1,0:T(8,128)(2,1)} async-done(((bf16[32,512,256]{2,1,0:T(8,128)(2,1)}), bf16[32,512,256]{2,1,0:T(8,128)(2,1)}, u32[]{:S(2)}, u32[]{:S(2)}) %all-to-all-start.3) | async-done | bytes 8388640 | tf_op jit(solution)/shard_map/all_to_all | solution.py:108
  348.2 5.5 %reduce_sum.43 = bf16[512,256]{1,0:T(8,128)(2,1)} reduce(bf16[32,512,256]{2,1,0:T(8,128)(2,1)} %all-to-all-done.3, bf16[]{:T(256)} %constant.4.clone.1), dimensions={0}, to_apply=%region_1.2 | reduce | flops 4063232 | bytes 8650754 | tf_op jit(solution)/shard_map/reduce_sum | solution.py:109
  (1 shorter events, 0.0 us)
Async XLA Ops:
  0.6 139.8 %copy-start = (bf16[256,256]{1,0:T(8,128)(2,1)S(1)}, bf16[256,256]{1,0:T(8,128)(2,1)}, u32[]{:S(2)}) copy-start(bf16[256,256]{1,0:T(8,128)(2,1)} %param.11) | copy-start | bytes 393220
  107.6 32.8 %copy-start.2 = (bf16[512,256]{1,0:T(8,128)(2,1)S(1)}, bf16[512,256]{1,0:T(8,128)(2,1)}, u32[]{:S(2)}) copy-start(bf16[512,256]{1,0:T(8,128)(2,1)} %param.13) | copy-start | bytes 786436
  107.6 32.8 %copy-start.3 = (f32[256]{0:T(256)S(1)}, f32[256]{0:T(256)}, u32[]{:S(2)}) copy-start(f32[256]{0:T(256)} %param.12) | copy-start | bytes 3076
  122.2 18.0 %all-to-all-start.1 = ((bf16[4,512,256]{2,1,0:T(8,128)(2,1)}), bf16[4,512,256]{2,1,0:T(8,128)(2,1)S(1)}, u32[]{:S(2)}, u32[]{:S(2)}) async-start(bf16[4,512,256]{2,1,0:T(8,128)(2,1)} %bitcast.16), calls=%async_computation.1 | async-start | bytes 2097152 | tf_op jit(solution)/shard_map/all_to_all | solution.py:108
  142.9 17.7 %all-to-all-start.4 = ((f32[128,3,256]{2,1,0:T(4,128)}), f32[128,3,256]{2,1,0:T(4,128)S(1)}, u32[]{:S(2)}, u32[]{:S(2)}) async-start(f32[128,3,256]{2,1,0:T(4,128)} %reshape.20), calls=%async_computation.4 | async-start | bytes 1048576 | tf_op jit(solution)/shard_map/all_to_all | solution.py:137
  161.6 18.0 %all-to-all-start.2 = ((bf16[4,512,256]{2,1,0:T(8,128)(2,1)}), bf16[4,512,256]{2,1,0:T(8,128)(2,1)S(1)}, u32[]{:S(2)}, u32[]{:S(2)}) async-start(bf16[4,512,256]{2,1,0:T(8,128)(2,1)} %broadcast_in_dim.11), calls=%async_computation.2 | async-start | bytes 2097152 | tf_op jit(solution)/shard_map/all_to_all | solution.py:101
  179.6 9.4 %copy-start.1 = (bf16[4,512,256]{2,1,0:T(8,128)(2,1)}, bf16[4,512,256]{2,1,0:T(8,128)(2,1)S(1)}, u32[]{:S(2)}) copy-start(bf16[4,512,256]{2,1,0:T(8,128)(2,1)S(1)} %all-to-all-done.2) | copy-start | bytes 3145732
  180.6 25.5 %all-to-all-start.5 = ((f32[128,3,256]{2,1,0:T(4,128)}), f32[128,3,256]{2,1,0:T(4,128)S(1)}, u32[]{:S(2)}, u32[]{:S(2)}) async-start(f32[128,3,256]{2,1,0:T(4,128)} %broadcast_in_dim.14), calls=%async_computation.5 | async-start | bytes 1048576 | tf_op jit(solution)/shard_map/all_to_all | solution.py:140
  206.0 142.2 %all-to-all-start.3 = ((bf16[32,512,256]{2,1,0:T(8,128)(2,1)}), bf16[32,512,256]{2,1,0:T(8,128)(2,1)}, u32[]{:S(2)}, u32[]{:S(2)}) async-start(bf16[32,512,256]{2,1,0:T(8,128)(2,1)} %bitcast.13), calls=%async_computation.3 | async-start | bytes 16777216 | tf_op jit(solution)/shard_map/all_to_all | solution.py:108

commit v4 on v3

--- a/solution.py
+++ b/solution.py
@@ -157,6 +157,7 @@
     layer_out, weight_grad, bias_grad, hidden_grad = dense_part(own_rows, weight, bias, cotangent)
     weight_grad, bias_grad = all_sum(weight_grad, bias_grad)
     grad_block = gather_over(hidden_grad, "row")
+    grad_block, weight_grad, bias_grad = lax.optimization_barrier((grad_block, weight_grad, bias_grad))
     grad_tiles = grad_block.reshape(row_tiles, tile_size, width)
 
     summed = aggregate_transposed(tile_values, tile_cols, live_counts, grad_tiles, column_tiles)

time: 359 us -> 367 us (1.022)
  blocking collectives: 105 us -> 123 us
  starting transfers between devices: 33.4 us -> 24.7 us
    all_to_all x0 -> x1, blocking collectives: none -> 17.5 us  [all_sum(): lax.all_to_all(packed.reshape(devices, per, width), axes, 0, 0, tiled=True)]
    all_to_all x1 -> x0, waiting for transfers between devices: 9.53 us -> none  [all_sum(): lax.all_to_all(packed.reshape(devices, per, width), axes, 0, 0, tiled=True)]
    all_to_all x1, waiting for transfers between devices: 0.01 us -> 9.53 us  [all_sum(): lax.all_to_all(spread, axes, 0, 0, tiled=True).reshape(devices * per, width)]
    all_to_all x1 -> x0, starting transfers between devices: 7.92 us -> none  [all_sum(): lax.all_to_all(packed.reshape(devices, per, width), axes, 0, 0, tiled=True)]
  transfers between devices with their start and end apart: 5 -> 4, of which waited for: 4 -> 4; matrix products, arithmetic and copies ran while one was open for 1% -> 1% of each run, Pallas kernels for 5% -> 0%
where the time goes in v4:
time: 367 us; the launch traced here: 360 us
  waiting for transfers between devices  166 us (45%)
  blocking collectives  123 us (34%)
  Pallas kernels  31.6 us (9%)
  starting transfers between devices  24.7 us (7%)
  other arithmetic  7.26 us (2%)
  local copies, waits for them, and re-layouts  5.34 us (1%)
    all_to_all x2, waiting for transfers between devices, sum_scatter_over(): got = lax.all_to_all(parts, axis, 0, 0, tiled=True)  142 us
    all_to_all x1, blocking collectives, gather_over(): got = lax.all_to_all(spread, axis, 0, 0, tiled=True)  105 us
    all_to_all x1, blocking collectives, all_sum(): lax.all_to_all(packed.reshape(devices, per, width), axes, 0, 0, tiled=True)  17.5 us
    pallas_call x1, Pallas kernels, aggregate_transposed(): pl.pallas_call(backward_kernel, out_shape=jax.ShapeDtypeStruct((col_tiles...  17 us
    pallas_call x1, Pallas kernels, aggregate(): pl.pallas_call(forward_kernel, out_shape=jax.ShapeDtypeStruct((row_tiles,...  14.6 us
    all_to_all x1, waiting for transfers between devices, gather_over(): got = lax.all_to_all(spread, axis, 0, 0, tiled=True)  14.2 us
    all_to_all x2, starting transfers between devices, sum_scatter_over(): got = lax.all_to_all(parts, axis, 0, 0, tiled=True)  12.8 us
    all_to_all x1, waiting for transfers between devices, all_sum(): lax.all_to_all(spread, axes, 0, 0, tiled=True).reshape(devices * per, width)  9.53 us
  transfers between devices with their start and end apart: 4, of which 4 were waited for; matrix products, arithmetic and copies ran while one was open for 1% of the time, Pallas kernels for 0%

profile of v4, /device:TPU:66, one launch (start us, length us, event | category | flops | bytes accessed | tf_op | source)
XLA Modules:
  0.0 359.6 jit_solution(12884964934926743523)
XLA Ops:
  0.6 0.0 copy-start
  0.6 1.9 broadcast_in_dim.10
  2.6 105.0 %all_to_all.30 = bf16[32,512,256]{2,1,0:T(8,128)(2,1)} all-to-all(bf16[32,512,256]{2,1,0:T(8,128)(2,1)S(1)} %broadcast_in_dim.10), channel_id=1, replica_groups=mesh['row'=4,'col'=32] {'col'}, dimensions={0} | all-to-all | bytes 16777216 | tf_op jit(solution)/shard_map/all_to_all | solution.py:101
  107.6 0.0 copy-start.3
  107.6 0.0 copy-start.4
  107.6 14.6 %shard_map.102 = bf16[8,256,256]{2,1,0:T(8,128)(2,1)} custom-call(s32[8,16]{1,0:T(8,128)} %cols_ref.3, s32[8]{0:T(128)} %bitcast.19, bf16[8,16,256,256]{3,2,1,0:T(8,128)(2,1)} %a_ref.3, bf16[64,256,256]{2,1,0:T(8,128)(2,1)} %bitcast.15), custom_call_target="tpu_custom_call" | custom-call | tf_op jit(solution)/shard_map/pallas_call | solution.py:58
  122.2 3.5 all-to-all-start.1
  125.7 0.1 pad.2.clone
  125.8 14.3 %all-to-all-done.1 = bf16[4,512,256]{2,1,0:T(8,128)(2,1)S(1)} async-done(((bf16[4,512,256]{2,1,0:T(8,128)(2,1)}), bf16[4,512,256]{2,1,0:T(8,128)(2,1)S(1)}, u32[]{:S(2)}, u32[]{:S(2)}) %all-to-all-start.1) | async-done | bytes 1048608 | tf_op jit(solution)/shard_map/all_to_all | solution.py:108
  140.1 0.3 reduce_sum.42
  140.4 0.0 copy-done
  140.4 0.0 copy-done.3
  140.4 0.0 copy-done.4
  140.4 1.1 convert_reduce_fusion
  141.5 0.3 fusion
  141.8 0.1 maximum_maximum_fusion
  141.9 0.2 reshape.25
  142.1 17.5 %all_to_all.31 = f32[128,3,256]{2,1,0:T(4,128)S(1)} all-to-all(f32[128,3,256]{2,1,0:T(4,128)S(1)} %reshape.25), channel_id=1, replica_groups=mesh['row'=4,'col'=32] {'row','col'}, dimensions={0} | all-to-all | bytes 786432 | tf_op jit(solution)/shard_map/all_to_all | solution.py:137
  159.6 0.1 reduce_sum.44
  159.8 0.9 broadcast_in_dim.14
  160.6 8.4 %all-to-all-start.4 = ((f32[128,3,256]{2,1,0:T(4,128)}), f32[128,3,256]{2,1,0:T(4,128)S(1)}, u32[]{:S(2)}, u32[]{:S(2)}) async-start(f32[128,3,256]{2,1,0:T(4,128)} %broadcast_in_dim.14), calls=%async_computation.4 | async-start | bytes 1048576 | tf_op jit(solution)/shard_map/all_to_all | solution.py:140
  169.1 0.3 convolution_convert_fusion
  169.3 9.5 %all-to-all-done.4 = f32[128,3,256]{2,1,0:T(4,128)S(1)} async-done(((f32[128,3,256]{2,1,0:T(4,128)}), f32[128,3,256]{2,1,0:T(4,128)S(1)}, u32[]{:S(2)}, u32[]{:S(2)}) %all-to-all-start.4) | async-done | bytes 393248 | tf_op jit(solution)/shard_map/all_to_all | solution.py:140
  178.9 1.0 broadcast_in_dim.11
  179.9 3.5 all-to-all-start.2
  183.4 0.2 reshape.26
  183.6 0.0 copy-start.2
  183.6 14.2 %all-to-all-done.2 = bf16[4,512,256]{2,1,0:T(8,128)(2,1)S(1)} async-done(((bf16[4,512,256]{2,1,0:T(8,128)(2,1)}), bf16[4,512,256]{2,1,0:T(8,128)(2,1)S(1)}, u32[]{:S(2)}, u32[]{:S(2)}) %all-to-all-start.2) | async-done | bytes 1048608 | tf_op jit(solution)/shard_map/all_to_all | solution.py:101
  197.9 0.0 copy-start.1
  197.9 1.0 copy-done.1
  198.9 17.0 %shard_map.103 = bf16[64,256,256]{2,1,0:T(8,128)(2,1)} custom-call(s32[8,16]{1,0:T(8,128)} %cols_ref.3, s32[8]{0:T(128)} %bitcast.20, bf16[8,16,256,256]{3,2,1,0:T(8,128)(2,1)} %a_ref.3, bf16[8,256,256]{2,1,0:T(8,128)(2,1)} %bitcast.16), custom_call_target="tpu_custom_call" | custom-call | tf_op jit(solution)/shard_map/pallas_call | solution.py:81
  215.9 0.0 copy-done.2
  215.9 0.0 slice-start
  215.9 0.0 slice-start.1
  215.9 9.2 %all-to-all-start.5 = ((bf16[32,512,256]{2,1,0:T(8,128)(2,1)}), bf16[32,512,256]{2,1,0:T(8,128)(2,1)}, u32[]{:S(2)}, u32[]{:S(2)}) async-start(bf16[32,512,256]{2,1,0:T(8,128)(2,1)} %bitcast.14), calls=%async_computation.5 | async-start | bytes 16777216 | tf_op jit(solution)/shard_map/all_to_all | solution.py:108
  225.2 0.0 slice-done
  225.2 0.6 broadcast_multiply_fusion.1
  225.8 0.0 slice-done.1
  225.8 0.7 broadcast_multiply_fusion
  226.5 127.7 %all-to-all-done.5 = bf16[32,512,256]{2,1,0:T(8,128)(2,1)} async-done(((bf16[32,512,256]{2,1,0:T(8,128)(2,1)}), bf16[32,512,256]{2,1,0:T(8,128)(2,1)}, u32[]{:S(2)}, u32[]{:S(2)}) %all-to-all-start.5) | async-done | bytes 8388640 | tf_op jit(solution)/shard_map/all_to_all | solution.py:108
  354.2 5.5 %reduce_sum.45 = bf16[512,256]{1,0:T(8,128)(2,1)} reduce(bf16[32,512,256]{2,1,0:T(8,128)(2,1)} %all-to-all-done.5, bf16[]{:T(256)} %constant.4.clone.1), dimensions={0}, to_apply=%region_3.4 | reduce | flops 4063232 | bytes 8650754 | tf_op jit(solution)/shard_map/reduce_sum | solution.py:109
  (1 shorter events, 0.0 us)
Async XLA Ops:
  0.6 139.8 %copy-start = (bf16[256,256]{1,0:T(8,128)(2,1)S(1)}, bf16[256,256]{1,0:T(8,128)(2,1)}, u32[]{:S(2)}) copy-start(bf16[256,256]{1,0:T(8,128)(2,1)} %param.11) | copy-start | bytes 393220
  107.6 32.8 %copy-start.3 = (bf16[512,256]{1,0:T(8,128)(2,1)S(1)}, bf16[512,256]{1,0:T(8,128)(2,1)}, u32[]{:S(2)}) copy-start(bf16[512,256]{1,0:T(8,128)(2,1)} %param.13) | copy-start | bytes 786436
  107.6 32.8 %copy-start.4 = (f32[256]{0:T(256)S(1)}, f32[256]{0:T(256)}, u32[]{:S(2)}) copy-start(f32[256]{0:T(256)} %param.12) | copy-start | bytes 3076
  122.2 18.0 %all-to-all-start.1 = ((bf16[4,512,256]{2,1,0:T(8,128)(2,1)}), bf16[4,512,256]{2,1,0:T(8,128)(2,1)S(1)}, u32[]{:S(2)}, u32[]{:S(2)}) async-start(bf16[4,512,256]{2,1,0:T(8,128)(2,1)} %bitcast.17), calls=%async_computation.1 | async-start | bytes 2097152 | tf_op jit(solution)/shard_map/all_to_all | solution.py:108
  160.6 18.2 %all-to-all-start.4 = ((f32[128,3,256]{2,1,0:T(4,128)}), f32[128,3,256]{2,1,0:T(4,128)S(1)}, u32[]{:S(2)}, u32[]{:S(2)}) async-start(f32[128,3,256]{2,1,0:T(4,128)} %broadcast_in_dim.14), calls=%async_computation.4 | async-start | bytes 1048576 | tf_op jit(solution)/shard_map/all_to_all | solution.py:140
  179.9 18.0 %all-to-all-start.2 = ((bf16[4,512,256]{2,1,0:T(8,128)(2,1)}), bf16[4,512,256]{2,1,0:T(8,128)(2,1)S(1)}, u32[]{:S(2)}, u32[]{:S(2)}) async-start(bf16[4,512,256]{2,1,0:T(8,128)(2,1)} %broadcast_in_dim.11), calls=%async_computation.2 | async-start | bytes 2097152 | tf_op jit(solution)/shard_map/all_to_all | solution.py:101
  183.6 32.3 %copy-start.2 = (f32[384,256]{1,0:T(8,128)}, f32[384,256]{1,0:T(8,128)S(1)}, u32[]{:S(2)}) copy-start(f32[384,256]{1,0:T(8,128)S(1)} %reshape.26) | copy-start | bytes 1179652
  197.9 1.1 copy-start.1
  215.9 9.3 %slice-start = ((f32[384,256]{1,0:T(8,128)}), f32[1,256]{1,0:T(1,128)S(1)}, s32[]{:S(2)}) async-start(f32[384,256]{1,0:T(8,128)} %copy-done.2), calls=%async_computation.6 | async-start | bytes 2048 | tf_op jit(solution)/shard_map/slice | solution.py:141
  215.9 9.8 %slice-start.1 = ((f32[384,256]{1,0:T(8,128)}), f32[256,256]{1,0:T(8,128)S(1)}, s32[]{:S(2)}) async-start(f32[384,256]{1,0:T(8,128)} %copy-done.2), calls=%async_computation.7 | async-start | bytes 524288 | tf_op jit(solution)/shard_map/slice | solution.py:141
  215.9 138.2 %all-to-all-start.5 = ((bf16[32,512,256]{2,1,0:T(8,128)(2,1)}), bf16[32,512,256]{2,1,0:T(8,128)(2,1)}, u32[]{:S(2)}, u32[]{:S(2)}) async-start(bf16[32,512,256]{2,1,0:T(8,128)(2,1)} %bitcast.14), calls=%async_computation.5 | async-start | bytes 16777216 | tf_op jit(solution)/shard_map/all_to_all | solution.py:108

commit v5 on v3

--- a/solution.py
+++ b/solution.py
@@ -155,14 +155,14 @@
     grad_scale = 1.0 / math.sqrt(node_total)
     own_rows = sum_scatter_over(partial_value, "row").astype(jnp.bfloat16)
     layer_out, weight_grad, bias_grad, hidden_grad = dense_part(own_rows, weight, bias, cotangent)
-    weight_grad, bias_grad = all_sum(weight_grad, bias_grad)
+    weight_grad, bias_grad = all_sum(weight_grad * grad_scale, bias_grad * grad_scale)
     grad_block = gather_over(hidden_grad, "row")
     grad_tiles = grad_block.reshape(row_tiles, tile_size, width)
 
     summed = aggregate_transposed(tile_values, tile_cols, live_counts, grad_tiles, column_tiles)
     summed = summed.reshape(column_tiles * tile_size, width)
     feature_grad = sum_scatter_over(summed, "col").astype(jnp.bfloat16)
-    return (layer_out, feature_grad, weight_grad * grad_scale, bias_grad * grad_scale)
+    return (layer_out, feature_grad, weight_grad, bias_grad)
 
 
 def solution(mesh):

time: 359 us -> 359 us (level)
  no operation moved by 1% of the time
where the time goes in v5:
time: 359 us; the launch traced here: 354 us
  waiting for transfers between devices  169 us (47%)
  blocking collectives  105 us (29%)
  starting transfers between devices  33.4 us (9%)
  Pallas kernels  31.6 us (9%)
  local copies, waits for them, and re-layouts  6.45 us (2%)
  other arithmetic  5.98 us (2%)
    all_to_all x2, waiting for transfers between devices, sum_scatter_over(): got = lax.all_to_all(parts, axis, 0, 0, tiled=True)  145 us
    all_to_all x1, blocking collectives, gather_over(): got = lax.all_to_all(spread, axis, 0, 0, tiled=True)  105 us
    pallas_call x1, Pallas kernels, aggregate_transposed(): pl.pallas_call(backward_kernel, out_shape=jax.ShapeDtypeStruct((col_tiles...  17 us
    pallas_call x1, Pallas kernels, aggregate(): pl.pallas_call(forward_kernel, out_shape=jax.ShapeDtypeStruct((row_tiles,...  14.6 us
    all_to_all x1, waiting for transfers between devices, gather_over(): got = lax.all_to_all(spread, axis, 0, 0, tiled=True)  14.3 us
    all_to_all x2, starting transfers between devices, sum_scatter_over(): got = lax.all_to_all(parts, axis, 0, 0, tiled=True)  13.5 us
    all_to_all x1, waiting for transfers between devices, all_sum(): lax.all_to_all(packed.reshape(devices, per, width), axes, 0, 0, tiled=True)  9.54 us
    all_to_all x1, starting transfers between devices, all_sum(): lax.all_to_all(spread, axes, 0, 0, tiled=True).reshape(devices * per, width)  8.43 us
  transfers between devices with their start and end apart: 5, of which 4 were waited for; matrix products, arithmetic and copies ran while one was open for 1% of the time, Pallas kernels for 5%

profile of v5, /device:TPU:66, one launch (start us, length us, event | category | flops | bytes accessed | tf_op | source)
XLA Modules:
  0.0 353.6 jit_solution(4255569341021137590)
XLA Ops:
  0.6 0.0 copy-start
  0.6 1.9 broadcast_in_dim.8
  2.6 105.0 %all_to_all.30 = bf16[32,512,256]{2,1,0:T(8,128)(2,1)} all-to-all(bf16[32,512,256]{2,1,0:T(8,128)(2,1)S(1)} %broadcast_in_dim.8), channel_id=1, replica_groups=mesh['row'=4,'col'=32] {'col'}, dimensions={0} | all-to-all | bytes 16777216 | tf_op jit(solution)/shard_map/all_to_all | solution.py:101
  107.6 0.0 copy-start.2
  107.6 0.0 copy-start.3
  107.6 14.6 %shard_map.102 = bf16[8,256,256]{2,1,0:T(8,128)(2,1)} custom-call(s32[8,16]{1,0:T(8,128)} %cols_ref.3, s32[8]{0:T(128)} %bitcast.18, bf16[8,16,256,256]{3,2,1,0:T(8,128)(2,1)} %a_ref.3, bf16[64,256,256]{2,1,0:T(8,128)(2,1)} %bitcast.14), custom_call_target="tpu_custom_call" | custom-call | tf_op jit(solution)/shard_map/pallas_call | solution.py:58
  122.2 3.5 all-to-all-start.1
  125.7 0.1 pad.2.clone
  125.8 14.3 %all-to-all-done.1 = bf16[4,512,256]{2,1,0:T(8,128)(2,1)S(1)} async-done(((bf16[4,512,256]{2,1,0:T(8,128)(2,1)}), bf16[4,512,256]{2,1,0:T(8,128)(2,1)S(1)}, u32[]{:S(2)}, u32[]{:S(2)}) %all-to-all-start.1) | async-done | bytes 1048608 | tf_op jit(solution)/shard_map/all_to_all | solution.py:108
  140.1 0.3 reduce_sum.42
  140.4 0.0 copy-done
  140.4 0.0 copy-done.2
  140.4 0.0 copy-done.3
  140.4 1.1 convert_reduce_fusion
  141.5 0.3 convolution_multiply_fusion
  141.8 0.1 maximum_maximum_fusion
  141.9 1.0 reshape.27
  142.9 7.9 %all-to-all-start.4 = ((f32[128,3,256]{2,1,0:T(4,128)}), f32[128,3,256]{2,1,0:T(4,128)S(1)}, u32[]{:S(2)}, u32[]{:S(2)}) async-start(f32[128,3,256]{2,1,0:T(4,128)} %reshape.27), calls=%async_computation.4 | async-start | bytes 1048576 | tf_op jit(solution)/shard_map/all_to_all | solution.py:137
  150.8 0.3 convolution_convert_fusion
  151.1 9.5 %all-to-all-done.4 = f32[128,3,256]{2,1,0:T(4,128)S(1)} async-done(((f32[128,3,256]{2,1,0:T(4,128)}), f32[128,3,256]{2,1,0:T(4,128)S(1)}, u32[]{:S(2)}, u32[]{:S(2)}) %all-to-all-start.4) | async-done | bytes 393248 | tf_op jit(solution)/shard_map/all_to_all | solution.py:137
  160.6 1.0 broadcast_in_dim.9
  161.7 3.5 all-to-all-start.2
  165.2 0.1 reduce_sum.45
  165.3 14.3 %all-to-all-done.2 = bf16[4,512,256]{2,1,0:T(8,128)(2,1)S(1)} async-done(((bf16[4,512,256]{2,1,0:T(8,128)(2,1)}), bf16[4,512,256]{2,1,0:T(8,128)(2,1)S(1)}, u32[]{:S(2)}, u32[]{:S(2)}) %all-to-all-start.2) | async-done | bytes 1048608 | tf_op jit(solution)/shard_map/all_to_all | solution.py:101
  179.6 0.0 copy-start.1
  179.6 1.0 broadcast_in_dim.11
  180.6 8.4 %all-to-all-start.5 = ((f32[128,3,256]{2,1,0:T(4,128)}), f32[128,3,256]{2,1,0:T(4,128)S(1)}, u32[]{:S(2)}, u32[]{:S(2)}) async-start(f32[128,3,256]{2,1,0:T(4,128)} %broadcast_in_dim.11), calls=%async_computation.5 | async-start | bytes 1048576 | tf_op jit(solution)/shard_map/all_to_all | solution.py:140
  189.0 0.0 copy-done.1
  189.0 17.0 %shard_map.103 = bf16[64,256,256]{2,1,0:T(8,128)(2,1)} custom-call(s32[8,16]{1,0:T(8,128)} %cols_ref.3, s32[8]{0:T(128)} %bitcast.19, bf16[8,16,256,256]{3,2,1,0:T(8,128)(2,1)} %a_ref.3, bf16[8,256,256]{2,1,0:T(8,128)(2,1)} %bitcast.15), custom_call_target="tpu_custom_call" | custom-call | tf_op jit(solution)/shard_map/pallas_call | solution.py:81
  206.0 0.0 all-to-all-done.5
  206.0 10.0 %all-to-all-start.3 = ((bf16[32,512,256]{2,1,0:T(8,128)(2,1)}), bf16[32,512,256]{2,1,0:T(8,128)(2,1)}, u32[]{:S(2)}, u32[]{:S(2)}) async-start(bf16[32,512,256]{2,1,0:T(8,128)(2,1)} %bitcast.13), calls=%async_computation.3 | async-start | bytes 16777216 | tf_op jit(solution)/shard_map/all_to_all | solution.py:108
  216.0 0.2 reshape.28
  216.2 0.6 slice.9
  216.8 0.7 slice.8
  217.5 130.6 %all-to-all-done.3 = bf16[32,512,256]{2,1,0:T(8,128)(2,1)} async-done(((bf16[32,512,256]{2,1,0:T(8,128)(2,1)}), bf16[32,512,256]{2,1,0:T(8,128)(2,1)}, u32[]{:S(2)}, u32[]{:S(2)}) %all-to-all-start.3) | async-done | bytes 8388640 | tf_op jit(solution)/shard_map/all_to_all | solution.py:108
  348.1 5.5 %reduce_sum.43 = bf16[512,256]{1,0:T(8,128)(2,1)} reduce(bf16[32,512,256]{2,1,0:T(8,128)(2,1)} %all-to-all-done.3, bf16[]{:T(256)} %constant.4.clone.1), dimensions={0}, to_apply=%region_1.2 | reduce | flops 4063232 | bytes 8650754 | tf_op jit(solution)/shard_map/reduce_sum | solution.py:109
  (2 shorter events, 0.0 us)
Async XLA Ops:
  0.6 139.8 %copy-start = (bf16[256,256]{1,0:T(8,128)(2,1)S(1)}, bf16[256,256]{1,0:T(8,128)(2,1)}, u32[]{:S(2)}) copy-start(bf16[256,256]{1,0:T(8,128)(2,1)} %param.11) | copy-start | bytes 393220
  107.6 32.8 %copy-start.2 = (bf16[512,256]{1,0:T(8,128)(2,1)S(1)}, bf16[512,256]{1,0:T(8,128)(2,1)}, u32[]{:S(2)}) copy-start(bf16[512,256]{1,0:T(8,128)(2,1)} %param.13) | copy-start | bytes 786436
  107.6 32.8 %copy-start.3 = (f32[256]{0:T(256)S(1)}, f32[256]{0:T(256)}, u32[]{:S(2)}) copy-start(f32[256]{0:T(256)} %param.12) | copy-start | bytes 3076
  122.2 18.0 %all-to-all-start.1 = ((bf16[4,512,256]{2,1,0:T(8,128)(2,1)}), bf16[4,512,256]{2,1,0:T(8,128)(2,1)S(1)}, u32[]{:S(2)}, u32[]{:S(2)}) async-start(bf16[4,512,256]{2,1,0:T(8,128)(2,1)} %bitcast.16), calls=%async_computation.1 | async-start | bytes 2097152 | tf_op jit(solution)/shard_map/all_to_all | solution.py:108
  142.9 17.7 %all-to-all-start.4 = ((f32[128,3,256]{2,1,0:T(4,128)}), f32[128,3,256]{2,1,0:T(4,128)S(1)}, u32[]{:S(2)}, u32[]{:S(2)}) async-start(f32[128,3,256]{2,1,0:T(4,128)} %reshape.27), calls=%async_computation.4 | async-start | bytes 1048576 | tf_op jit(solution)/shard_map/all_to_all | solution.py:137
  161.7 18.0 %all-to-all-start.2 = ((bf16[4,512,256]{2,1,0:T(8,128)(2,1)}), bf16[4,512,256]{2,1,0:T(8,128)(2,1)S(1)}, u32[]{:S(2)}, u32[]{:S(2)}) async-start(bf16[4,512,256]{2,1,0:T(8,128)(2,1)} %broadcast_in_dim.9), calls=%async_computation.2 | async-start | bytes 2097152 | tf_op jit(solution)/shard_map/all_to_all | solution.py:101
  179.6 9.4 %copy-start.1 = (bf16[4,512,256]{2,1,0:T(8,128)(2,1)}, bf16[4,512,256]{2,1,0:T(8,128)(2,1)S(1)}, u32[]{:S(2)}) copy-start(bf16[4,512,256]{2,1,0:T(8,128)(2,1)S(1)} %all-to-all-done.2) | copy-start | bytes 3145732
  180.6 25.5 %all-to-all-start.5 = ((f32[128,3,256]{2,1,0:T(4,128)}), f32[128,3,256]{2,1,0:T(4,128)S(1)}, u32[]{:S(2)}, u32[]{:S(2)}) async-start(f32[128,3,256]{2,1,0:T(4,128)} %broadcast_in_dim.11), calls=%async_computation.5 | async-start | bytes 1048576 | tf_op jit(solution)/shard_map/all_to_all | solution.py:140
  206.0 142.1 %all-to-all-start.3 = ((bf16[32,512,256]{2,1,0:T(8,128)(2,1)}), bf16[32,512,256]{2,1,0:T(8,128)(2,1)}, u32[]{:S(2)}, u32[]{:S(2)}) async-start(bf16[32,512,256]{2,1,0:T(8,128)(2,1)} %bitcast.13), calls=%async_computation.3 | async-start | bytes 16777216 | tf_op jit(solution)/shard_map/all_to_all | solution.py:108

commit v6 on v5

--- a/solution.py
+++ b/solution.py
@@ -11,18 +11,22 @@
 VMEM_LIMIT = 60 * 1024 * 1024
 
 
-def forward_kernel(cols_ref, counts_ref, a_ref, x_ref, o_ref):
+def forward_kernel(cols_ref, counts_ref, a_ref, x_ref, o_ref, acc_ref):
     t = pl.program_id(0)
     slots = a_ref.shape[1]
     last = x_ref.shape[0] - 1
     live = counts_ref[t]
-    acc = None
-    for s in range(slots):
-        j = jnp.clip(cols_ref[t, s], 0, last)
-        term = jnp.dot(a_ref[0, s], x_ref[j], preferred_element_type=jnp.float32)
-        term = jnp.where(s < live, term, 0.0)
-        acc = term if acc is None else acc + term
-    o_ref[0] = acc.astype(o_ref.dtype)
+    j = jnp.clip(cols_ref[t, 0], 0, last)
+    first = jnp.dot(a_ref[0, 0], x_ref[j], preferred_element_type=jnp.float32)
+    acc_ref[...] = jnp.where(live > 0, first, 0.0)
+    for s in range(1, slots):
+
+        @pl.when(s < live)
+        def _():
+            k = jnp.clip(cols_ref[t, s], 0, last)
+            acc_ref[...] += jnp.dot(a_ref[0, s], x_ref[k], preferred_element_type=jnp.float32)
+
+    o_ref[0] = acc_ref[...].astype(o_ref.dtype)
 
 
 def backward_kernel(cols_ref, counts_ref, a_ref, g_ref, o_ref, acc_ref):
@@ -37,11 +41,13 @@
 
     g = g_ref[0]
     for s in range(slots):
-        j = jnp.clip(cols_ref[t, s], 0, last)
-        term = lax.dot_general(
-            a_ref[0, s], g, (((0,), (0,)), ((), ())), preferred_element_type=jnp.float32
-        )
-        acc_ref[j] += jnp.where(s < live, term, 0.0)
+
+        @pl.when(s < live)
+        def _():
+            j = jnp.clip(cols_ref[t, s], 0, last)
+            acc_ref[j] += lax.dot_general(
+                a_ref[0, s], g, (((0,), (0,)), ((), ())), preferred_element_type=jnp.float32
+            )
 
     @pl.when(t == pl.num_programs(0) - 1)
     def _():
@@ -70,6 +76,7 @@
                 ),
             ],
             out_specs=pl.BlockSpec((1, tile, width), lambda t, c, n: (t, 0, 0)),
+            scratch_shapes=[pltpu.VMEM((tile, width), jnp.float32)],
         ),
         compiler_params=pltpu.CompilerParams(vmem_limit_bytes=VMEM_LIMIT),
     )(cols, counts, tile_values, x_tiles)

time: 359 us -> 374 us (1.042)
  the two profiles are of different devices: /device:TPU:66 before, /device:TPU:1 now
where the time goes in v6:
time: 374 us; the launch traced here: 373 us
  waiting for transfers between devices  166 us (44%)
  blocking collectives  107 us (29%)
  Pallas kernels  48.9 us (13%)
  starting transfers between devices  35.7 us (10%)
  local copies, waits for them, and re-layouts  6.45 us (2%)
  other arithmetic  5.98 us (2%)
    all_to_all x2, waiting for transfers between devices, sum_scatter_over(): got = lax.all_to_all(parts, axis, 0, 0, tiled=True)  139 us
    all_to_all x1, blocking collectives, gather_over(): got = lax.all_to_all(spread, axis, 0, 0, tiled=True)  107 us
    pallas_call x1, Pallas kernels, aggregate_transposed(): pl.pallas_call(backward_kernel, out_shape=jax.ShapeDtypeStruct((col_tiles...  26.6 us
    pallas_call x1, Pallas kernels, aggregate(): pl.pallas_call(forward_kernel, out_shape=jax.ShapeDtypeStruct((row_tiles,...  22.3 us
    all_to_all x2, starting transfers between devices, sum_scatter_over(): got = lax.all_to_all(parts, axis, 0, 0, tiled=True)  16.7 us
    all_to_all x1, waiting for transfers between devices, gather_over(): got = lax.all_to_all(spread, axis, 0, 0, tiled=True)  13.4 us
    all_to_all x1, waiting for transfers between devices, all_sum(): lax.all_to_all(packed.reshape(devices, per, width), axes, 0, 0, tiled=True)  13.2 us
    all_to_all x1, starting transfers between devices, all_sum(): lax.all_to_all(packed.reshape(devices, per, width), axes, 0, 0, tiled=True)  9.85 us
  transfers between devices with their start and end apart: 5, of which 4 were waited for; matrix products, arithmetic and copies ran while one was open for 1% of the time, Pallas kernels for 7%

profile of v6, /device:TPU:1, one launch (start us, length us, event | category | flops | bytes accessed | tf_op | source)
XLA Modules:
  0.0 372.7 jit_solution(15981800812293568343)
XLA Ops:
  0.6 0.0 copy-start
  0.6 1.9 broadcast_in_dim.8
  2.6 107.5 %all_to_all.30 = bf16[32,512,256]{2,1,0:T(8,128)(2,1)} all-to-all(bf16[32,512,256]{2,1,0:T(8,128)(2,1)S(1)} %broadcast_in_dim.8), channel_id=1, replica_groups=mesh['row'=4,'col'=32] {'col'}, dimensions={0} | all-to-all | bytes 16777216 | tf_op jit(solution)/shard_map/all_to_all | solution.py:108
  110.0 0.0 copy-start.2
  110.0 0.0 copy-start.3
  110.0 22.3 %shard_map.102 = bf16[8,256,256]{2,1,0:T(8,128)(2,1)} custom-call(s32[8,16]{1,0:T(8,128)} %cols_ref.3, s32[8]{0:T(128)} %bitcast.18, bf16[8,16,256,256]{3,2,1,0:T(8,128)(2,1)} %a_ref.3, bf16[64,256,256]{2,1,0:T(8,128)(2,1)} %bitcast.14), custom_call_target="tpu_custom_call" | custom-call | tf_op jit(solution)/shard_map/pallas_call | solution.py:64
  132.3 3.5 all-to-all-start.1
  135.8 0.1 pad.2.clone
  135.9 11.8 %all-to-all-done.1 = bf16[4,512,256]{2,1,0:T(8,128)(2,1)S(1)} async-done(((bf16[4,512,256]{2,1,0:T(8,128)(2,1)}), bf16[4,512,256]{2,1,0:T(8,128)(2,1)S(1)}, u32[]{:S(2)}, u32[]{:S(2)}) %all-to-all-start.1) | async-done | bytes 1048608 | tf_op jit(solution)/shard_map/all_to_all | solution.py:115
  147.7 0.3 reduce_sum.42
  147.9 0.0 copy-done
  147.9 0.0 copy-done.2
  148.0 0.0 copy-done.3
  148.0 1.1 convert_reduce_fusion
  149.1 0.3 convolution_multiply_fusion
  149.4 0.1 maximum_maximum_fusion
  149.5 1.0 reshape.27
  150.4 9.8 %all-to-all-start.4 = ((f32[128,3,256]{2,1,0:T(4,128)}), f32[128,3,256]{2,1,0:T(4,128)S(1)}, u32[]{:S(2)}, u32[]{:S(2)}) async-start(f32[128,3,256]{2,1,0:T(4,128)} %reshape.27), calls=%async_computation.4 | async-start | bytes 1048576 | tf_op jit(solution)/shard_map/all_to_all | solution.py:144
  160.3 0.3 convolution_convert_fusion
  160.6 13.2 %all-to-all-done.4 = f32[128,3,256]{2,1,0:T(4,128)S(1)} async-done(((f32[128,3,256]{2,1,0:T(4,128)}), f32[128,3,256]{2,1,0:T(4,128)S(1)}, u32[]{:S(2)}, u32[]{:S(2)}) %all-to-all-start.4) | async-done | bytes 393248 | tf_op jit(solution)/shard_map/all_to_all | solution.py:144
  173.8 1.0 broadcast_in_dim.9
  174.8 4.7 %all-to-all-start.2 = ((bf16[4,512,256]{2,1,0:T(8,128)(2,1)}), bf16[4,512,256]{2,1,0:T(8,128)(2,1)S(1)}, u32[]{:S(2)}, u32[]{:S(2)}) async-start(bf16[4,512,256]{2,1,0:T(8,128)(2,1)} %broadcast_in_dim.9), calls=%async_computation.2 | async-start | bytes 2097152 | tf_op jit(solution)/shard_map/all_to_all | solution.py:108
  179.5 0.1 reduce_sum.45
  179.6 13.4 %all-to-all-done.2 = bf16[4,512,256]{2,1,0:T(8,128)(2,1)S(1)} async-done(((bf16[4,512,256]{2,1,0:T(8,128)(2,1)}), bf16[4,512,256]{2,1,0:T(8,128)(2,1)S(1)}, u32[]{:S(2)}, u32[]{:S(2)}) %all-to-all-start.2) | async-done | bytes 1048608 | tf_op jit(solution)/shard_map/all_to_all | solution.py:108
  193.1 0.0 copy-start.1
  193.1 1.0 broadcast_in_dim.11
  194.0 4.4 %all-to-all-start.5 = ((f32[128,3,256]{2,1,0:T(4,128)}), f32[128,3,256]{2,1,0:T(4,128)S(1)}, u32[]{:S(2)}, u32[]{:S(2)}) async-start(f32[128,3,256]{2,1,0:T(4,128)} %broadcast_in_dim.11), calls=%async_computation.5 | async-start | bytes 1048576 | tf_op jit(solution)/shard_map/all_to_all | solution.py:147
  198.5 0.0 copy-done.1
  198.5 26.6 %shard_map.103 = bf16[64,256,256]{2,1,0:T(8,128)(2,1)} custom-call(s32[8,16]{1,0:T(8,128)} %cols_ref.3, s32[8]{0:T(128)} %bitcast.19, bf16[8,16,256,256]{3,2,1,0:T(8,128)(2,1)} %a_ref.3, bf16[8,256,256]{2,1,0:T(8,128)(2,1)} %bitcast.15), custom_call_target="tpu_custom_call" | custom-call | tf_op jit(solution)/shard_map/pallas_call | solution.py:88
  225.1 0.0 all-to-all-done.5
  225.1 13.2 %all-to-all-start.3 = ((bf16[32,512,256]{2,1,0:T(8,128)(2,1)}), bf16[32,512,256]{2,1,0:T(8,128)(2,1)}, u32[]{:S(2)}, u32[]{:S(2)}) async-start(bf16[32,512,256]{2,1,0:T(8,128)(2,1)} %bitcast.13), calls=%async_computation.3 | async-start | bytes 16777216 | tf_op jit(solution)/shard_map/all_to_all | solution.py:115
  238.3 0.2 reshape.28
  238.5 0.6 slice.9
  239.1 0.7 slice.8
  239.8 127.5 %all-to-all-done.3 = bf16[32,512,256]{2,1,0:T(8,128)(2,1)} async-done(((bf16[32,512,256]{2,1,0:T(8,128)(2,1)}), bf16[32,512,256]{2,1,0:T(8,128)(2,1)}, u32[]{:S(2)}, u32[]{:S(2)}) %all-to-all-start.3) | async-done | bytes 8388640 | tf_op jit(solution)/shard_map/all_to_all | solution.py:115
  367.3 5.5 %reduce_sum.43 = bf16[512,256]{1,0:T(8,128)(2,1)} reduce(bf16[32,512,256]{2,1,0:T(8,128)(2,1)} %all-to-all-done.3, bf16[]{:T(256)} %constant.4.clone.1), dimensions={0}, to_apply=%region_1.2 | reduce | flops 4063232 | bytes 8650754 | tf_op jit(solution)/shard_map/reduce_sum | solution.py:116
  (2 shorter events, 0.0 us)
Async XLA Ops:
  0.6 147.3 %copy-start = (bf16[256,256]{1,0:T(8,128)(2,1)S(1)}, bf16[256,256]{1,0:T(8,128)(2,1)}, u32[]{:S(2)}) copy-start(bf16[256,256]{1,0:T(8,128)(2,1)} %param.11) | copy-start | bytes 393220
  110.0 37.9 %copy-start.2 = (bf16[512,256]{1,0:T(8,128)(2,1)S(1)}, bf16[512,256]{1,0:T(8,128)(2,1)}, u32[]{:S(2)}) copy-start(bf16[512,256]{1,0:T(8,128)(2,1)} %param.13) | copy-start | bytes 786436
  110.0 37.9 %copy-start.3 = (f32[256]{0:T(256)S(1)}, f32[256]{0:T(256)}, u32[]{:S(2)}) copy-start(f32[256]{0:T(256)} %param.12) | copy-start | bytes 3076
  132.3 15.4 %all-to-all-start.1 = ((bf16[4,512,256]{2,1,0:T(8,128)(2,1)}), bf16[4,512,256]{2,1,0:T(8,128)(2,1)S(1)}, u32[]{:S(2)}, u32[]{:S(2)}) async-start(bf16[4,512,256]{2,1,0:T(8,128)(2,1)} %bitcast.16), calls=%async_computation.1 | async-start | bytes 2097152 | tf_op jit(solution)/shard_map/all_to_all | solution.py:115
  150.4 23.3 %all-to-all-start.4 = ((f32[128,3,256]{2,1,0:T(4,128)}), f32[128,3,256]{2,1,0:T(4,128)S(1)}, u32[]{:S(2)}, u32[]{:S(2)}) async-start(f32[128,3,256]{2,1,0:T(4,128)} %reshape.27), calls=%async_computation.4 | async-start | bytes 1048576 | tf_op jit(solution)/shard_map/all_to_all | solution.py:144
  174.8 18.3 %all-to-all-start.2 = ((bf16[4,512,256]{2,1,0:T(8,128)(2,1)}), bf16[4,512,256]{2,1,0:T(8,128)(2,1)S(1)}, u32[]{:S(2)}, u32[]{:S(2)}) async-start(bf16[4,512,256]{2,1,0:T(8,128)(2,1)} %broadcast_in_dim.9), calls=%async_computation.2 | async-start | bytes 2097152 | tf_op jit(solution)/shard_map/all_to_all | solution.py:108
  193.1 5.4 %copy-start.1 = (bf16[4,512,256]{2,1,0:T(8,128)(2,1)}, bf16[4,512,256]{2,1,0:T(8,128)(2,1)S(1)}, u32[]{:S(2)}) copy-start(bf16[4,512,256]{2,1,0:T(8,128)(2,1)S(1)} %all-to-all-done.2) | copy-start | bytes 3145732
  194.0 31.1 %all-to-all-start.5 = ((f32[128,3,256]{2,1,0:T(4,128)}), f32[128,3,256]{2,1,0:T(4,128)S(1)}, u32[]{:S(2)}, u32[]{:S(2)}) async-start(f32[128,3,256]{2,1,0:T(4,128)} %broadcast_in_dim.11), calls=%async_computation.5 | async-start | bytes 1048576 | tf_op jit(solution)/shard_map/all_to_all | solution.py:147
  225.1 142.2 %all-to-all-start.3 = ((bf16[32,512,256]{2,1,0:T(8,128)(2,1)}), bf16[32,512,256]{2,1,0:T(8,128)(2,1)}, u32[]{:S(2)}, u32[]{:S(2)}) async-start(bf16[32,512,256]{2,1,0:T(8,128)(2,1)} %bitcast.13), calls=%async_computation.3 | async-start | bytes 16777216 | tf_op jit(solution)/shard_map/all_to_all | solution.py:115

commit v7 on v5

--- a/solution.py
+++ b/solution.py
@@ -9,41 +9,49 @@
 from jax.sharding import PartitionSpec as P
 
 VMEM_LIMIT = 60 * 1024 * 1024
+GROUP = 2
 
 
 def forward_kernel(cols_ref, counts_ref, a_ref, x_ref, o_ref):
-    t = pl.program_id(0)
-    slots = a_ref.shape[1]
+    step = pl.program_id(0)
+    group, slots = a_ref.shape[:2]
     last = x_ref.shape[0] - 1
-    live = counts_ref[t]
-    acc = None
-    for s in range(slots):
-        j = jnp.clip(cols_ref[t, s], 0, last)
-        term = jnp.dot(a_ref[0, s], x_ref[j], preferred_element_type=jnp.float32)
-        term = jnp.where(s < live, term, 0.0)
-        acc = term if acc is None else acc + term
-    o_ref[0] = acc.astype(o_ref.dtype)
+    for u in range(group):
+        t = step * group + u
+        live = counts_ref[t]
+        acc = None
+        for s in range(slots):
+            j = jnp.clip(cols_ref[t, s], 0, last)
+            term = jnp.dot(a_ref[u, s], x_ref[j], preferred_element_type=jnp.float32)
+            term = jnp.where(s < live, term, 0.0)
+            acc = term if acc is None else acc + term
+        o_ref[u] = acc.astype(o_ref.dtype)
 
 
 def backward_kernel(cols_ref, counts_ref, a_ref, g_ref, o_ref, acc_ref):
-    t = pl.program_id(0)
-    slots = a_ref.shape[1]
+    step = pl.program_id(0)
+    group, slots = a_ref.shape[:2]
     last = acc_ref.shape[0] - 1
-    live = counts_ref[t]
 
-    @pl.when(t == 0)
+    @pl.when(step == 0)
     def _():
         acc_ref[...] = jnp.zeros_like(acc_ref)
 
-    g = g_ref[0]
-    for s in range(slots):
-        j = jnp.clip(cols_ref[t, s], 0, last)
-        term = lax.dot_general(
-            a_ref[0, s], g, (((0,), (0,)), ((), ())), preferred_element_type=jnp.float32
-        )
-        acc_ref[j] += jnp.where(s < live, term, 0.0)
+    for u in range(group):
+        t = step * group + u
+        live = counts_ref[t]
+        g = g_ref[u]
+        terms = [
+            lax.dot_general(
+                a_ref[u, s], g, (((0,), (0,)), ((), ())), preferred_element_type=jnp.float32
+            )
+            for s in range(slots)
+        ]
+        for s in range(slots):
+            j = jnp.clip(cols_ref[t, s], 0, last)
+            acc_ref[j] += jnp.where(s < live, terms[s], 0.0)
 
-    @pl.when(t == pl.num_programs(0) - 1)
+    @pl.when(step == pl.num_programs(0) - 1)
     def _():
         def put(j, carry):
             o_ref[j] = acc_ref[j].astype(o_ref.dtype)
@@ -60,16 +68,16 @@
         out_shape=jax.ShapeDtypeStruct((row_tiles, tile, width), jnp.bfloat16),
         grid_spec=pltpu.PrefetchScalarGridSpec(
             num_scalar_prefetch=2,
-            grid=(row_tiles,),
+            grid=(row_tiles // GROUP,),
             in_specs=[
-                pl.BlockSpec((1, slots, tile, tile), lambda t, c, n: (t, 0, 0, 0)),
+                pl.BlockSpec((GROUP, slots, tile, tile), lambda t, c, n: (t, 0, 0, 0)),
                 pl.BlockSpec(
                     (col_tiles, tile, width),
                     lambda t, c, n: (0, 0, 0),
                     pipeline_mode=pl.Buffered(1),
                 ),
             ],
-            out_specs=pl.BlockSpec((1, tile, width), lambda t, c, n: (t, 0, 0)),
+            out_specs=pl.BlockSpec((GROUP, tile, width), lambda t, c, n: (t, 0, 0)),
         ),
         compiler_params=pltpu.CompilerParams(vmem_limit_bytes=VMEM_LIMIT),
     )(cols, counts, tile_values, x_tiles)
@@ -83,10 +91,10 @@
         out_shape=jax.ShapeDtypeStruct((col_tiles, tile, width), jnp.bfloat16),
         grid_spec=pltpu.PrefetchScalarGridSpec(
             num_scalar_prefetch=2,
-            grid=(row_tiles,),
+            grid=(row_tiles // GROUP,),
             in_specs=[
-                pl.BlockSpec((1, slots, tile, tile), lambda t, c, n: (t, 0, 0, 0)),
-                pl.BlockSpec((1, tile, width), lambda t, c, n: (t, 0, 0)),
+                pl.BlockSpec((GROUP, slots, tile, tile), lambda t, c, n: (t, 0, 0, 0)),
+                pl.BlockSpec((GROUP, tile, width), lambda t, c, n: (t, 0, 0)),
             ],
             out_specs=pl.BlockSpec((col_tiles, tile, width), lambda t, c, n: (0, 0, 0)),
             scratch_shapes=[pltpu.VMEM((col_tiles, tile, width), jnp.float32)],

time: 359 us -> 355 us (0.989)
  Pallas kernels: 31.6 us -> 27.7 us
  transfers between devices with their start and end apart: 5 -> 5, of which waited for: 4 -> 4; matrix products, arithmetic and copies ran while one was open for 1% -> 1% of each run, Pallas kernels for 5% -> 4%
where the time goes in v7:
time: 355 us; the launch traced here: 350 us
  waiting for transfers between devices  169 us (48%)
  blocking collectives  105 us (30%)
  starting transfers between devices  33.4 us (9%)
  Pallas kernels  27.7 us (8%)
  local copies, waits for them, and re-layouts  6.45 us (2%)
  other arithmetic  5.98 us (2%)
    all_to_all x2, waiting for transfers between devices, sum_scatter_over(): got = lax.all_to_all(parts, axis, 0, 0, tiled=True)  145 us
    all_to_all x1, blocking collectives, gather_over(): got = lax.all_to_all(spread, axis, 0, 0, tiled=True)  105 us
    pallas_call x1, Pallas kernels, aggregate_transposed(): pl.pallas_call(backward_kernel, out_shape=jax.ShapeDtypeStruct((col_tiles...  15 us
    all_to_all x1, waiting for transfers between devices, gather_over(): got = lax.all_to_all(spread, axis, 0, 0, tiled=True)  14.3 us
    all_to_all x2, starting transfers between devices, sum_scatter_over(): got = lax.all_to_all(parts, axis, 0, 0, tiled=True)  13.5 us
    pallas_call x1, Pallas kernels, aggregate(): pl.pallas_call(forward_kernel, out_shape=jax.ShapeDtypeStruct((row_tiles,...  12.7 us
    all_to_all x1, waiting for transfers between devices, all_sum(): lax.all_to_all(packed.reshape(devices, per, width), axes, 0, 0, tiled=True)  9.54 us
    all_to_all x1, starting transfers between devices, all_sum(): lax.all_to_all(spread, axes, 0, 0, tiled=True).reshape(devices * per, width)  8.43 us
  transfers between devices with their start and end apart: 5, of which 4 were waited for; matrix products, arithmetic and copies ran while one was open for 1% of the time, Pallas kernels for 4%

profile of v7, /device:TPU:66, one launch (start us, length us, event | category | flops | bytes accessed | tf_op | source)
XLA Modules:
  0.0 349.7 jit_solution(12636852009916264059)
XLA Ops:
  0.6 0.0 copy-start
  0.6 1.9 broadcast_in_dim.8
  2.6 105.0 %all_to_all.30 = bf16[32,512,256]{2,1,0:T(8,128)(2,1)} all-to-all(bf16[32,512,256]{2,1,0:T(8,128)(2,1)S(1)} %broadcast_in_dim.8), channel_id=1, replica_groups=mesh['row'=4,'col'=32] {'col'}, dimensions={0} | all-to-all | bytes 16777216 | tf_op jit(solution)/shard_map/all_to_all | solution.py:109
  107.6 0.0 copy-start.2
  107.6 0.0 copy-start.3
  107.6 12.7 %shard_map.102 = bf16[8,256,256]{2,1,0:T(8,128)(2,1)} custom-call(s32[8,16]{1,0:T(8,128)} %cols_ref.3, s32[8]{0:T(128)} %bitcast.18, bf16[8,16,256,256]{3,2,1,0:T(8,128)(2,1)} %a_ref.3, bf16[64,256,256]{2,1,0:T(8,128)(2,1)} %bitcast.14), custom_call_target="tpu_custom_call" | custom-call | tf_op jit(solution)/shard_map/pallas_call | solution.py:66
  120.3 3.5 %all-to-all-start.1 = ((bf16[4,512,256]{2,1,0:T(8,128)(2,1)}), bf16[4,512,256]{2,1,0:T(8,128)(2,1)S(1)}, u32[]{:S(2)}, u32[]{:S(2)}) async-start(bf16[4,512,256]{2,1,0:T(8,128)(2,1)} %bitcast.16), calls=%async_computation.1 | async-start | bytes 2097152 | tf_op jit(solution)/shard_map/all_to_all | solution.py:116
  123.8 0.1 pad.2.clone
  123.9 14.3 %all-to-all-done.1 = bf16[4,512,256]{2,1,0:T(8,128)(2,1)S(1)} async-done(((bf16[4,512,256]{2,1,0:T(8,128)(2,1)}), bf16[4,512,256]{2,1,0:T(8,128)(2,1)S(1)}, u32[]{:S(2)}, u32[]{:S(2)}) %all-to-all-start.1) | async-done | bytes 1048608 | tf_op jit(solution)/shard_map/all_to_all | solution.py:116
  138.2 0.3 reduce_sum.42
  138.5 0.0 copy-done
  138.5 0.0 copy-done.2
  138.5 0.0 copy-done.3
  138.5 1.1 convert_reduce_fusion
  139.6 0.3 convolution_multiply_fusion
  139.9 0.1 maximum_maximum_fusion
  140.1 1.0 reshape.27
  141.0 7.9 %all-to-all-start.4 = ((f32[128,3,256]{2,1,0:T(4,128)}), f32[128,3,256]{2,1,0:T(4,128)S(1)}, u32[]{:S(2)}, u32[]{:S(2)}) async-start(f32[128,3,256]{2,1,0:T(4,128)} %reshape.27), calls=%async_computation.4 | async-start | bytes 1048576 | tf_op jit(solution)/shard_map/all_to_all | solution.py:145
  148.9 0.3 convolution_convert_fusion
  149.2 9.5 %all-to-all-done.4 = f32[128,3,256]{2,1,0:T(4,128)S(1)} async-done(((f32[128,3,256]{2,1,0:T(4,128)}), f32[128,3,256]{2,1,0:T(4,128)S(1)}, u32[]{:S(2)}, u32[]{:S(2)}) %all-to-all-start.4) | async-done | bytes 393248 | tf_op jit(solution)/shard_map/all_to_all | solution.py:145
  158.7 1.0 broadcast_in_dim.9
  159.8 3.5 %all-to-all-start.2 = ((bf16[4,512,256]{2,1,0:T(8,128)(2,1)}), bf16[4,512,256]{2,1,0:T(8,128)(2,1)S(1)}, u32[]{:S(2)}, u32[]{:S(2)}) async-start(bf16[4,512,256]{2,1,0:T(8,128)(2,1)} %broadcast_in_dim.9), calls=%async_computation.2 | async-start | bytes 2097152 | tf_op jit(solution)/shard_map/all_to_all | solution.py:109
  163.3 0.1 reduce_sum.45
  163.4 14.3 %all-to-all-done.2 = bf16[4,512,256]{2,1,0:T(8,128)(2,1)S(1)} async-done(((bf16[4,512,256]{2,1,0:T(8,128)(2,1)}), bf16[4,512,256]{2,1,0:T(8,128)(2,1)S(1)}, u32[]{:S(2)}, u32[]{:S(2)}) %all-to-all-start.2) | async-done | bytes 1048608 | tf_op jit(solution)/shard_map/all_to_all | solution.py:109
  177.7 0.0 copy-start.1
  177.7 1.0 broadcast_in_dim.11
  178.7 8.4 %all-to-all-start.5 = ((f32[128,3,256]{2,1,0:T(4,128)}), f32[128,3,256]{2,1,0:T(4,128)S(1)}, u32[]{:S(2)}, u32[]{:S(2)}) async-start(f32[128,3,256]{2,1,0:T(4,128)} %broadcast_in_dim.11), calls=%async_computation.5 | async-start | bytes 1048576 | tf_op jit(solution)/shard_map/all_to_all | solution.py:148
  187.1 0.0 copy-done.1
  187.1 15.0 %shard_map.103 = bf16[64,256,256]{2,1,0:T(8,128)(2,1)} custom-call(s32[8,16]{1,0:T(8,128)} %cols_ref.3, s32[8]{0:T(128)} %bitcast.19, bf16[8,16,256,256]{3,2,1,0:T(8,128)(2,1)} %a_ref.3, bf16[8,256,256]{2,1,0:T(8,128)(2,1)} %bitcast.15), custom_call_target="tpu_custom_call" | custom-call | tf_op jit(solution)/shard_map/pallas_call | solution.py:89
  202.1 0.0 all-to-all-done.5
  202.1 10.0 %all-to-all-start.3 = ((bf16[32,512,256]{2,1,0:T(8,128)(2,1)}), bf16[32,512,256]{2,1,0:T(8,128)(2,1)}, u32[]{:S(2)}, u32[]{:S(2)}) async-start(bf16[32,512,256]{2,1,0:T(8,128)(2,1)} %bitcast.13), calls=%async_computation.3 | async-start | bytes 16777216 | tf_op jit(solution)/shard_map/all_to_all | solution.py:116
  212.1 0.2 reshape.28
  212.3 0.6 slice.9
  212.9 0.7 slice.8
  213.6 130.6 %all-to-all-done.3 = bf16[32,512,256]{2,1,0:T(8,128)(2,1)} async-done(((bf16[32,512,256]{2,1,0:T(8,128)(2,1)}), bf16[32,512,256]{2,1,0:T(8,128)(2,1)}, u32[]{:S(2)}, u32[]{:S(2)}) %all-to-all-start.3) | async-done | bytes 8388640 | tf_op jit(solution)/shard_map/all_to_all | solution.py:116
  344.2 5.5 %reduce_sum.43 = bf16[512,256]{1,0:T(8,128)(2,1)} reduce(bf16[32,512,256]{2,1,0:T(8,128)(2,1)} %all-to-all-done.3, bf16[]{:T(256)} %constant.4.clone.1), dimensions={0}, to_apply=%region_1.2 | reduce | flops 4063232 | bytes 8650754 | tf_op jit(solution)/shard_map/reduce_sum | solution.py:117
  (2 shorter events, 0.0 us)
Async XLA Ops:
  0.6 137.9 %copy-start = (bf16[256,256]{1,0:T(8,128)(2,1)S(1)}, bf16[256,256]{1,0:T(8,128)(2,1)}, u32[]{:S(2)}) copy-start(bf16[256,256]{1,0:T(8,128)(2,1)} %param.11) | copy-start | bytes 393220
  107.6 30.9 %copy-start.2 = (bf16[512,256]{1,0:T(8,128)(2,1)S(1)}, bf16[512,256]{1,0:T(8,128)(2,1)}, u32[]{:S(2)}) copy-start(bf16[512,256]{1,0:T(8,128)(2,1)} %param.13) | copy-start | bytes 786436
  107.6 30.9 %copy-start.3 = (f32[256]{0:T(256)S(1)}, f32[256]{0:T(256)}, u32[]{:S(2)}) copy-start(f32[256]{0:T(256)} %param.12) | copy-start | bytes 3076
  120.3 18.0 %all-to-all-start.1 = ((bf16[4,512,256]{2,1,0:T(8,128)(2,1)}), bf16[4,512,256]{2,1,0:T(8,128)(2,1)S(1)}, u32[]{:S(2)}, u32[]{:S(2)}) async-start(bf16[4,512,256]{2,1,0:T(8,128)(2,1)} %bitcast.16), calls=%async_computation.1 | async-start | bytes 2097152 | tf_op jit(solution)/shard_map/all_to_all | solution.py:116
  141.0 17.7 %all-to-all-start.4 = ((f32[128,3,256]{2,1,0:T(4,128)}), f32[128,3,256]{2,1,0:T(4,128)S(1)}, u32[]{:S(2)}, u32[]{:S(2)}) async-start(f32[128,3,256]{2,1,0:T(4,128)} %reshape.27), calls=%async_computation.4 | async-start | bytes 1048576 | tf_op jit(solution)/shard_map/all_to_all | solution.py:145
  159.8 18.0 %all-to-all-start.2 = ((bf16[4,512,256]{2,1,0:T(8,128)(2,1)}), bf16[4,512,256]{2,1,0:T(8,128)(2,1)S(1)}, u32[]{:S(2)}, u32[]{:S(2)}) async-start(bf16[4,512,256]{2,1,0:T(8,128)(2,1)} %broadcast_in_dim.9), calls=%async_computation.2 | async-start | bytes 2097152 | tf_op jit(solution)/shard_map/all_to_all | solution.py:109
  177.7 9.4 %copy-start.1 = (bf16[4,512,256]{2,1,0:T(8,128)(2,1)}, bf16[4,512,256]{2,1,0:T(8,128)(2,1)S(1)}, u32[]{:S(2)}) copy-start(bf16[4,512,256]{2,1,0:T(8,128)(2,1)S(1)} %all-to-all-done.2) | copy-start | bytes 3145732
  178.7 23.4 %all-to-all-start.5 = ((f32[128,3,256]{2,1,0:T(4,128)}), f32[128,3,256]{2,1,0:T(4,128)S(1)}, u32[]{:S(2)}, u32[]{:S(2)}) async-start(f32[128,3,256]{2,1,0:T(4,128)} %broadcast_in_dim.11), calls=%async_computation.5 | async-start | bytes 1048576 | tf_op jit(solution)/shard_map/all_to_all | solution.py:148
  202.1 142.1 %all-to-all-start.3 = ((bf16[32,512,256]{2,1,0:T(8,128)(2,1)}), bf16[32,512,256]{2,1,0:T(8,128)(2,1)}, u32[]{:S(2)}, u32[]{:S(2)}) async-start(bf16[32,512,256]{2,1,0:T(8,128)(2,1)} %bitcast.13), calls=%async_computation.3 | async-start | bytes 16777216 | tf_op jit(solution)/shard_map/all_to_all | solution.py:116

commit v8 on v7

--- a/solution.py
+++ b/solution.py
@@ -9,7 +9,7 @@
 from jax.sharding import PartitionSpec as P
 
 VMEM_LIMIT = 60 * 1024 * 1024
-GROUP = 2
+GROUP = 4
 
 
 def forward_kernel(cols_ref, counts_ref, a_ref, x_ref, o_ref):

time: 355 us -> 355 us (level)
  no operation moved by 1% of the time
where the time goes in v8:
time: 355 us; the launch traced here: 349 us
  waiting for transfers between devices  169 us (48%)
  blocking collectives  105 us (30%)
  starting transfers between devices  33.4 us (9%)
  Pallas kernels  27.2 us (8%)
  local copies, waits for them, and re-layouts  6.45 us (2%)
  other arithmetic  5.98 us (2%)
    all_to_all x2, waiting for transfers between devices, sum_scatter_over(): got = lax.all_to_all(parts, axis, 0, 0, tiled=True)  145 us
    all_to_all x1, blocking collectives, gather_over(): got = lax.all_to_all(spread, axis, 0, 0, tiled=True)  105 us
    pallas_call x1, Pallas kernels, aggregate_transposed(): pl.pallas_call(backward_kernel, out_shape=jax.ShapeDtypeStruct((col_tiles...  15 us
    all_to_all x1, waiting for transfers between devices, gather_over(): got = lax.all_to_all(spread, axis, 0, 0, tiled=True)  14.3 us
    all_to_all x2, starting transfers between devices, sum_scatter_over(): got = lax.all_to_all(parts, axis, 0, 0, tiled=True)  13.5 us
    pallas_call x1, Pallas kernels, aggregate(): pl.pallas_call(forward_kernel, out_shape=jax.ShapeDtypeStruct((row_tiles,...  12.2 us
    all_to_all x1, waiting for transfers between devices, all_sum(): lax.all_to_all(packed.reshape(devices, per, width), axes, 0, 0, tiled=True)  9.53 us
    all_to_all x1, starting transfers between devices, all_sum(): lax.all_to_all(spread, axes, 0, 0, tiled=True).reshape(devices * per, width)  8.43 us
  transfers between devices with their start and end apart: 5, of which 4 were waited for; matrix products, arithmetic and copies ran while one was open for 1% of the time, Pallas kernels for 4%

profile of v8, /device:TPU:66, one launch (start us, length us, event | category | flops | bytes accessed | tf_op | source)
XLA Modules:
  0.0 349.3 jit_solution(1241762625331607485)
XLA Ops:
  0.6 0.0 copy-start
  0.6 1.9 broadcast_in_dim.8
  2.6 105.0 %all_to_all.30 = bf16[32,512,256]{2,1,0:T(8,128)(2,1)} all-to-all(bf16[32,512,256]{2,1,0:T(8,128)(2,1)S(1)} %broadcast_in_dim.8), channel_id=1, replica_groups=mesh['row'=4,'col'=32] {'col'}, dimensions={0} | all-to-all | bytes 16777216 | tf_op jit(solution)/shard_map/all_to_all | solution.py:109
  107.6 0.0 copy-start.2
  107.6 0.0 copy-start.3
  107.6 12.2 %shard_map.102 = bf16[8,256,256]{2,1,0:T(8,128)(2,1)} custom-call(s32[8,16]{1,0:T(8,128)} %cols_ref.3, s32[8]{0:T(128)} %bitcast.18, bf16[8,16,256,256]{3,2,1,0:T(8,128)(2,1)} %a_ref.3, bf16[64,256,256]{2,1,0:T(8,128)(2,1)} %bitcast.14), custom_call_target="tpu_custom_call" | custom-call | tf_op jit(solution)/shard_map/pallas_call | solution.py:66
  119.8 3.5 %all-to-all-start.1 = ((bf16[4,512,256]{2,1,0:T(8,128)(2,1)}), bf16[4,512,256]{2,1,0:T(8,128)(2,1)S(1)}, u32[]{:S(2)}, u32[]{:S(2)}) async-start(bf16[4,512,256]{2,1,0:T(8,128)(2,1)} %bitcast.16), calls=%async_computation.1 | async-start | bytes 2097152 | tf_op jit(solution)/shard_map/all_to_all | solution.py:116
  123.4 0.1 pad.2.clone
  123.4 14.3 %all-to-all-done.1 = bf16[4,512,256]{2,1,0:T(8,128)(2,1)S(1)} async-done(((bf16[4,512,256]{2,1,0:T(8,128)(2,1)}), bf16[4,512,256]{2,1,0:T(8,128)(2,1)S(1)}, u32[]{:S(2)}, u32[]{:S(2)}) %all-to-all-start.1) | async-done | bytes 1048608 | tf_op jit(solution)/shard_map/all_to_all | solution.py:116
  137.8 0.3 reduce_sum.42
  138.0 0.0 copy-done
  138.0 0.0 copy-done.2
  138.1 0.0 copy-done.3
  138.1 1.1 convert_reduce_fusion
  139.2 0.3 convolution_multiply_fusion
  139.5 0.1 maximum_maximum_fusion
  139.6 1.0 reshape.27
  140.5 7.9 %all-to-all-start.4 = ((f32[128,3,256]{2,1,0:T(4,128)}), f32[128,3,256]{2,1,0:T(4,128)S(1)}, u32[]{:S(2)}, u32[]{:S(2)}) async-start(f32[128,3,256]{2,1,0:T(4,128)} %reshape.27), calls=%async_computation.4 | async-start | bytes 1048576 | tf_op jit(solution)/shard_map/all_to_all | solution.py:145
  148.5 0.3 convolution_convert_fusion
  148.7 9.5 %all-to-all-done.4 = f32[128,3,256]{2,1,0:T(4,128)S(1)} async-done(((f32[128,3,256]{2,1,0:T(4,128)}), f32[128,3,256]{2,1,0:T(4,128)S(1)}, u32[]{:S(2)}, u32[]{:S(2)}) %all-to-all-start.4) | async-done | bytes 393248 | tf_op jit(solution)/shard_map/all_to_all | solution.py:145
  158.3 1.0 broadcast_in_dim.9
  159.3 3.5 %all-to-all-start.2 = ((bf16[4,512,256]{2,1,0:T(8,128)(2,1)}), bf16[4,512,256]{2,1,0:T(8,128)(2,1)S(1)}, u32[]{:S(2)}, u32[]{:S(2)}) async-start(bf16[4,512,256]{2,1,0:T(8,128)(2,1)} %broadcast_in_dim.9), calls=%async_computation.2 | async-start | bytes 2097152 | tf_op jit(solution)/shard_map/all_to_all | solution.py:109
  162.8 0.1 reduce_sum.45
  163.0 14.3 %all-to-all-done.2 = bf16[4,512,256]{2,1,0:T(8,128)(2,1)S(1)} async-done(((bf16[4,512,256]{2,1,0:T(8,128)(2,1)}), bf16[4,512,256]{2,1,0:T(8,128)(2,1)S(1)}, u32[]{:S(2)}, u32[]{:S(2)}) %all-to-all-start.2) | async-done | bytes 1048608 | tf_op jit(solution)/shard_map/all_to_all | solution.py:109
  177.3 0.0 copy-start.1
  177.3 1.0 broadcast_in_dim.11
  178.2 8.4 %all-to-all-start.5 = ((f32[128,3,256]{2,1,0:T(4,128)}), f32[128,3,256]{2,1,0:T(4,128)S(1)}, u32[]{:S(2)}, u32[]{:S(2)}) async-start(f32[128,3,256]{2,1,0:T(4,128)} %broadcast_in_dim.11), calls=%async_computation.5 | async-start | bytes 1048576 | tf_op jit(solution)/shard_map/all_to_all | solution.py:148
  186.7 0.0 copy-done.1
  186.7 15.0 %shard_map.103 = bf16[64,256,256]{2,1,0:T(8,128)(2,1)} custom-call(s32[8,16]{1,0:T(8,128)} %cols_ref.3, s32[8]{0:T(128)} %bitcast.19, bf16[8,16,256,256]{3,2,1,0:T(8,128)(2,1)} %a_ref.3, bf16[8,256,256]{2,1,0:T(8,128)(2,1)} %bitcast.15), custom_call_target="tpu_custom_call" | custom-call | tf_op jit(solution)/shard_map/pallas_call | solution.py:89
  201.6 0.0 all-to-all-done.5
  201.6 10.0 %all-to-all-start.3 = ((bf16[32,512,256]{2,1,0:T(8,128)(2,1)}), bf16[32,512,256]{2,1,0:T(8,128)(2,1)}, u32[]{:S(2)}, u32[]{:S(2)}) async-start(bf16[32,512,256]{2,1,0:T(8,128)(2,1)} %bitcast.13), calls=%async_computation.3 | async-start | bytes 16777216 | tf_op jit(solution)/shard_map/all_to_all | solution.py:116
  211.6 0.2 reshape.28
  211.8 0.6 slice.9
  212.4 0.7 slice.8
  213.1 130.7 %all-to-all-done.3 = bf16[32,512,256]{2,1,0:T(8,128)(2,1)} async-done(((bf16[32,512,256]{2,1,0:T(8,128)(2,1)}), bf16[32,512,256]{2,1,0:T(8,128)(2,1)}, u32[]{:S(2)}, u32[]{:S(2)}) %all-to-all-start.3) | async-done | bytes 8388640 | tf_op jit(solution)/shard_map/all_to_all | solution.py:116
  343.8 5.5 %reduce_sum.43 = bf16[512,256]{1,0:T(8,128)(2,1)} reduce(bf16[32,512,256]{2,1,0:T(8,128)(2,1)} %all-to-all-done.3, bf16[]{:T(256)} %constant.4.clone.1), dimensions={0}, to_apply=%region_1.2 | reduce | flops 4063232 | bytes 8650754 | tf_op jit(solution)/shard_map/reduce_sum | solution.py:117
  (2 shorter events, 0.0 us)
Async XLA Ops:
  0.6 137.4 %copy-start = (bf16[256,256]{1,0:T(8,128)(2,1)S(1)}, bf16[256,256]{1,0:T(8,128)(2,1)}, u32[]{:S(2)}) copy-start(bf16[256,256]{1,0:T(8,128)(2,1)} %param.11) | copy-start | bytes 393220
  107.6 30.5 %copy-start.2 = (bf16[512,256]{1,0:T(8,128)(2,1)S(1)}, bf16[512,256]{1,0:T(8,128)(2,1)}, u32[]{:S(2)}) copy-start(bf16[512,256]{1,0:T(8,128)(2,1)} %param.13) | copy-start | bytes 786436
  107.6 30.5 %copy-start.3 = (f32[256]{0:T(256)S(1)}, f32[256]{0:T(256)}, u32[]{:S(2)}) copy-start(f32[256]{0:T(256)} %param.12) | copy-start | bytes 3076
  119.8 18.0 %all-to-all-start.1 = ((bf16[4,512,256]{2,1,0:T(8,128)(2,1)}), bf16[4,512,256]{2,1,0:T(8,128)(2,1)S(1)}, u32[]{:S(2)}, u32[]{:S(2)}) async-start(bf16[4,512,256]{2,1,0:T(8,128)(2,1)} %bitcast.16), calls=%async_computation.1 | async-start | bytes 2097152 | tf_op jit(solution)/shard_map/all_to_all | solution.py:116
  140.5 17.7 %all-to-all-start.4 = ((f32[128,3,256]{2,1,0:T(4,128)}), f32[128,3,256]{2,1,0:T(4,128)S(1)}, u32[]{:S(2)}, u32[]{:S(2)}) async-start(f32[128,3,256]{2,1,0:T(4,128)} %reshape.27), calls=%async_computation.4 | async-start | bytes 1048576 | tf_op jit(solution)/shard_map/all_to_all | solution.py:145
  159.3 18.0 %all-to-all-start.2 = ((bf16[4,512,256]{2,1,0:T(8,128)(2,1)}), bf16[4,512,256]{2,1,0:T(8,128)(2,1)S(1)}, u32[]{:S(2)}, u32[]{:S(2)}) async-start(bf16[4,512,256]{2,1,0:T(8,128)(2,1)} %broadcast_in_dim.9), calls=%async_computation.2 | async-start | bytes 2097152 | tf_op jit(solution)/shard_map/all_to_all | solution.py:109
  177.3 9.4 %copy-start.1 = (bf16[4,512,256]{2,1,0:T(8,128)(2,1)}, bf16[4,512,256]{2,1,0:T(8,128)(2,1)S(1)}, u32[]{:S(2)}) copy-start(bf16[4,512,256]{2,1,0:T(8,128)(2,1)S(1)} %all-to-all-done.2) | copy-start | bytes 3145732
  178.2 23.4 %all-to-all-start.5 = ((f32[128,3,256]{2,1,0:T(4,128)}), f32[128,3,256]{2,1,0:T(4,128)S(1)}, u32[]{:S(2)}, u32[]{:S(2)}) async-start(f32[128,3,256]{2,1,0:T(4,128)} %broadcast_in_dim.11), calls=%async_computation.5 | async-start | bytes 1048576 | tf_op jit(solution)/shard_map/all_to_all | solution.py:148
  201.6 142.2 %all-to-all-start.3 = ((bf16[32,512,256]{2,1,0:T(8,128)(2,1)}), bf16[32,512,256]{2,1,0:T(8,128)(2,1)}, u32[]{:S(2)}, u32[]{:S(2)}) async-start(bf16[32,512,256]{2,1,0:T(8,128)(2,1)} %bitcast.13), calls=%async_computation.3 | async-start | bytes 16777216 | tf_op jit(solution)/shard_map/all_to_all | solution.py:116

commit v9 on v8

--- a/solution.py
+++ b/solution.py
@@ -117,6 +117,21 @@
     return got.astype(jnp.float32).sum(axis=0)
 
 
+def sum_kernel(x_ref, o_ref):
+    o_ref[...] = jnp.sum(x_ref[...].astype(jnp.float32), axis=0).astype(o_ref.dtype)
+
+
+def sum_parts(parts, rows_per_step=128):
+    count, rows, width = parts.shape
+    return pl.pallas_call(
+        sum_kernel,
+        out_shape=jax.ShapeDtypeStruct((rows, width), jnp.bfloat16),
+        grid=(rows // rows_per_step,),
+        in_specs=[pl.BlockSpec((count, rows_per_step, width), lambda i: (0, i, 0))],
+        out_specs=pl.BlockSpec((rows_per_step, width), lambda i: (i, 0)),
+    )(parts)
+
+
 def dense_part(hidden, weight, bias, cotangent):
     preact = jnp.dot(hidden, weight, preferred_element_type=jnp.float32) + bias
     output = jax.nn.silu(preact).astype(jnp.bfloat16)
@@ -169,7 +184,8 @@
 
     summed = aggregate_transposed(tile_values, tile_cols, live_counts, grad_tiles, column_tiles)
     summed = summed.reshape(column_tiles * tile_size, width)
-    feature_grad = sum_scatter_over(summed, "col").astype(jnp.bfloat16)
+    col_parts = summed.reshape((lax.axis_size("col"), -1, width))
+    feature_grad = sum_parts(lax.all_to_all(col_parts, "col", 0, 0, tiled=True))
     return (layer_out, feature_grad, weight_grad, bias_grad)
 
 

time: 355 us -> 354 us (level)
  other arithmetic: 5.98 us -> 0.53 us
  Pallas kernels: 27.2 us -> 32.4 us
    all_to_all x2 -> x1, waiting for transfers between devices: 145 us -> 14.3 us  [sum_scatter_over(): got = lax.all_to_all(parts, axis, 0, 0, tiled=True)]
    all_to_all x0 -> x1, waiting for transfers between devices: none -> 131 us  [per_device(): feature_grad = sum_parts(lax.all_to_all(col_parts, 'col', 0, 0, tiled=True))]
    all_to_all x2 -> x1, starting transfers between devices: 13.5 us -> 3.51 us  [sum_scatter_over(): got = lax.all_to_all(parts, axis, 0, 0, tiled=True)]
    all_to_all x0 -> x1, starting transfers between devices: none -> 9.98 us  [per_device(): feature_grad = sum_parts(lax.all_to_all(col_parts, 'col', 0, 0, tiled=True))]
    reduce_sum x2 -> x1, other arithmetic: 5.71 us -> 0.26 us  [sum_scatter_over(): return got.astype(jnp.float32).sum(axis=0)]
    pallas_call x0 -> x1, Pallas kernels: none -> 5.2 us  [sum_parts(): pl.pallas_call(sum_kernel, out_shape=jax.ShapeDtypeStruct((rows, width),...]
where the time goes in v9:
time: 354 us; the launch traced here: 349 us
  waiting for transfers between devices  169 us (48%)
  blocking collectives  105 us (30%)
  starting transfers between devices  33.4 us (9%)
  Pallas kernels  32.4 us (9%)
  local copies, waits for them, and re-layouts  6.46 us (2%)
    all_to_all x1, waiting for transfers between devices, per_device(): feature_grad = sum_parts(lax.all_to_all(col_parts, 'col', 0, 0, tiled=True))  131 us
    all_to_all x1, blocking collectives, gather_over(): got = lax.all_to_all(spread, axis, 0, 0, tiled=True)  105 us
    pallas_call x1, Pallas kernels, aggregate_transposed(): pl.pallas_call(backward_kernel, out_shape=jax.ShapeDtypeStruct((col_tiles...  15 us
    all_to_all x1, waiting for transfers between devices, sum_scatter_over(): got = lax.all_to_all(parts, axis, 0, 0, tiled=True)  14.3 us
    all_to_all x1, waiting for transfers between devices, gather_over(): got = lax.all_to_all(spread, axis, 0, 0, tiled=True)  14.3 us
    pallas_call x1, Pallas kernels, aggregate(): pl.pallas_call(forward_kernel, out_shape=jax.ShapeDtypeStruct((row_tiles,...  12.2 us
    all_to_all x1, starting transfers between devices, per_device(): feature_grad = sum_parts(lax.all_to_all(col_parts, 'col', 0, 0, tiled=True))  9.98 us
    all_to_all x1, waiting for transfers between devices, all_sum(): lax.all_to_all(packed.reshape(devices, per, width), axes, 0, 0, tiled=True)  9.54 us
  transfers between devices with their start and end apart: 5, of which 4 were waited for; matrix products, arithmetic and copies ran while one was open for 1% of the time, Pallas kernels for 4%

profile of v9, /device:TPU:66, one launch (start us, length us, event | category | flops | bytes accessed | tf_op | source)
XLA Modules:
  0.0 348.9 jit_solution(3169170865252803888)
XLA Ops:
  0.6 0.0 copy-start
  0.6 1.9 broadcast_in_dim.8
  2.6 105.0 %all_to_all.30 = bf16[32,512,256]{2,1,0:T(8,128)(2,1)} all-to-all(bf16[32,512,256]{2,1,0:T(8,128)(2,1)S(1)} %broadcast_in_dim.8), channel_id=1, replica_groups=mesh['row'=4,'col'=32] {'col'}, dimensions={0} | all-to-all | bytes 16777216 | tf_op jit(solution)/shard_map/all_to_all | solution.py:109
  107.6 0.0 copy-start.2
  107.6 0.0 copy-start.3
  107.6 12.2 %shard_map.102 = bf16[8,256,256]{2,1,0:T(8,128)(2,1)} custom-call(s32[8,16]{1,0:T(8,128)} %cols_ref.3, s32[8]{0:T(128)} %bitcast.18, bf16[8,16,256,256]{3,2,1,0:T(8,128)(2,1)} %a_ref.3, bf16[64,256,256]{2,1,0:T(8,128)(2,1)} %bitcast.14), custom_call_target="tpu_custom_call" | custom-call | tf_op jit(solution)/shard_map/pallas_call | solution.py:66
  119.8 3.5 %all-to-all-start.1 = ((bf16[4,512,256]{2,1,0:T(8,128)(2,1)}), bf16[4,512,256]{2,1,0:T(8,128)(2,1)S(1)}, u32[]{:S(2)}, u32[]{:S(2)}) async-start(bf16[4,512,256]{2,1,0:T(8,128)(2,1)} %bitcast.16), calls=%async_computation.1 | async-start | bytes 2097152 | tf_op jit(solution)/shard_map/all_to_all | solution.py:116
  123.3 0.1 pad.2.clone
  123.4 14.3 %all-to-all-done.1 = bf16[4,512,256]{2,1,0:T(8,128)(2,1)S(1)} async-done(((bf16[4,512,256]{2,1,0:T(8,128)(2,1)}), bf16[4,512,256]{2,1,0:T(8,128)(2,1)S(1)}, u32[]{:S(2)}, u32[]{:S(2)}) %all-to-all-start.1) | async-done | bytes 1048608 | tf_op jit(solution)/shard_map/all_to_all | solution.py:116
  137.8 0.3 reduce_sum.30
  138.0 0.0 copy-done
  138.0 0.0 copy-done.2
  138.0 0.0 copy-done.3
  138.1 1.1 convert_reduce_fusion
  139.2 0.3 convolution_multiply_fusion
  139.5 0.1 maximum_maximum_fusion
  139.6 1.0 reshape.27
  140.5 7.9 %all-to-all-start.4 = ((f32[128,3,256]{2,1,0:T(4,128)}), f32[128,3,256]{2,1,0:T(4,128)S(1)}, u32[]{:S(2)}, u32[]{:S(2)}) async-start(f32[128,3,256]{2,1,0:T(4,128)} %reshape.27), calls=%async_computation.4 | async-start | bytes 1048576 | tf_op jit(solution)/shard_map/all_to_all | solution.py:160
  148.5 0.3 convolution_convert_fusion
  148.7 9.5 %all-to-all-done.4 = f32[128,3,256]{2,1,0:T(4,128)S(1)} async-done(((f32[128,3,256]{2,1,0:T(4,128)}), f32[128,3,256]{2,1,0:T(4,128)S(1)}, u32[]{:S(2)}, u32[]{:S(2)}) %all-to-all-start.4) | async-done | bytes 393248 | tf_op jit(solution)/shard_map/all_to_all | solution.py:160
  158.3 1.0 broadcast_in_dim.9
  159.3 3.5 %all-to-all-start.2 = ((bf16[4,512,256]{2,1,0:T(8,128)(2,1)}), bf16[4,512,256]{2,1,0:T(8,128)(2,1)S(1)}, u32[]{:S(2)}, u32[]{:S(2)}) async-start(bf16[4,512,256]{2,1,0:T(8,128)(2,1)} %broadcast_in_dim.9), calls=%async_computation.2 | async-start | bytes 2097152 | tf_op jit(solution)/shard_map/all_to_all | solution.py:109
  162.8 0.1 reduce_sum.32
  163.0 14.3 %all-to-all-done.2 = bf16[4,512,256]{2,1,0:T(8,128)(2,1)S(1)} async-done(((bf16[4,512,256]{2,1,0:T(8,128)(2,1)}), bf16[4,512,256]{2,1,0:T(8,128)(2,1)S(1)}, u32[]{:S(2)}, u32[]{:S(2)}) %all-to-all-start.2) | async-done | bytes 1048608 | tf_op jit(solution)/shard_map/all_to_all | solution.py:109
  177.3 0.0 copy-start.1
  177.3 1.0 broadcast_in_dim.11
  178.2 8.4 %all-to-all-start.5 = ((f32[128,3,256]{2,1,0:T(4,128)}), f32[128,3,256]{2,1,0:T(4,128)S(1)}, u32[]{:S(2)}, u32[]{:S(2)}) async-start(f32[128,3,256]{2,1,0:T(4,128)} %broadcast_in_dim.11), calls=%async_computation.5 | async-start | bytes 1048576 | tf_op jit(solution)/shard_map/all_to_all | solution.py:163
  186.7 0.0 copy-done.1
  186.7 15.0 %shard_map.103 = bf16[64,256,256]{2,1,0:T(8,128)(2,1)} custom-call(s32[8,16]{1,0:T(8,128)} %cols_ref.3, s32[8]{0:T(128)} %bitcast.19, bf16[8,16,256,256]{3,2,1,0:T(8,128)(2,1)} %a_ref.3, bf16[8,256,256]{2,1,0:T(8,128)(2,1)} %bitcast.15), custom_call_target="tpu_custom_call" | custom-call | tf_op jit(solution)/shard_map/pallas_call | solution.py:89
  201.6 0.0 all-to-all-done.5
  201.7 10.0 %all-to-all-start.3 = ((bf16[32,512,256]{2,1,0:T(8,128)(2,1)}), bf16[32,512,256]{2,1,0:T(8,128)(2,1)}, u32[]{:S(2)}, u32[]{:S(2)}) async-start(bf16[32,512,256]{2,1,0:T(8,128)(2,1)} %bitcast.13), calls=%async_computation.3 | async-start | bytes 16777216 | tf_op jit(solution)/shard_map/all_to_all | solution.py:188
  211.6 0.2 reshape.28
  211.8 0.6 slice.9
  212.4 0.7 slice.8
  213.1 130.6 %all-to-all-done.3.x_ref = bf16[32,512,256]{2,1,0:T(8,128)(2,1)} async-done(((bf16[32,512,256]{2,1,0:T(8,128)(2,1)}), bf16[32,512,256]{2,1,0:T(8,128)(2,1)}, u32[]{:S(2)}, u32[]{:S(2)}) %all-to-all-start.3) | async-done | bytes 8388640 | tf_op jit(solution)/shard_map/all_to_all | solution.py:188
  343.7 5.2 %shard_map.104 = bf16[512,256]{1,0:T(8,128)(2,1)} custom-call(bf16[32,512,256]{2,1,0:T(8,128)(2,1)} %all-to-all-done.3.x_ref), custom_call_target="tpu_custom_call" | custom-call | tf_op jit(solution)/shard_map/pallas_call | solution.py:126
  (2 shorter events, 0.0 us)
Async XLA Ops:
  0.6 137.4 %copy-start = (bf16[256,256]{1,0:T(8,128)(2,1)S(1)}, bf16[256,256]{1,0:T(8,128)(2,1)}, u32[]{:S(2)}) copy-start(bf16[256,256]{1,0:T(8,128)(2,1)} %param.11) | copy-start | bytes 393220
  107.6 30.4 %copy-start.2 = (bf16[512,256]{1,0:T(8,128)(2,1)S(1)}, bf16[512,256]{1,0:T(8,128)(2,1)}, u32[]{:S(2)}) copy-start(bf16[512,256]{1,0:T(8,128)(2,1)} %param.13) | copy-start | bytes 786436
  107.6 30.5 %copy-start.3 = (f32[256]{0:T(256)S(1)}, f32[256]{0:T(256)}, u32[]{:S(2)}) copy-start(f32[256]{0:T(256)} %param.12) | copy-start | bytes 3076
  119.8 18.0 %all-to-all-start.1 = ((bf16[4,512,256]{2,1,0:T(8,128)(2,1)}), bf16[4,512,256]{2,1,0:T(8,128)(2,1)S(1)}, u32[]{:S(2)}, u32[]{:S(2)}) async-start(bf16[4,512,256]{2,1,0:T(8,128)(2,1)} %bitcast.16), calls=%async_computation.1 | async-start | bytes 2097152 | tf_op jit(solution)/shard_map/all_to_all | solution.py:116
  140.5 17.7 %all-to-all-start.4 = ((f32[128,3,256]{2,1,0:T(4,128)}), f32[128,3,256]{2,1,0:T(4,128)S(1)}, u32[]{:S(2)}, u32[]{:S(2)}) async-start(f32[128,3,256]{2,1,0:T(4,128)} %reshape.27), calls=%async_computation.4 | async-start | bytes 1048576 | tf_op jit(solution)/shard_map/all_to_all | solution.py:160
  159.3 18.0 %all-to-all-start.2 = ((bf16[4,512,256]{2,1,0:T(8,128)(2,1)}), bf16[4,512,256]{2,1,0:T(8,128)(2,1)S(1)}, u32[]{:S(2)}, u32[]{:S(2)}) async-start(bf16[4,512,256]{2,1,0:T(8,128)(2,1)} %broadcast_in_dim.9), calls=%async_computation.2 | async-start | bytes 2097152 | tf_op jit(solution)/shard_map/all_to_all | solution.py:109
  177.3 9.4 %copy-start.1 = (bf16[4,512,256]{2,1,0:T(8,128)(2,1)}, bf16[4,512,256]{2,1,0:T(8,128)(2,1)S(1)}, u32[]{:S(2)}) copy-start(bf16[4,512,256]{2,1,0:T(8,128)(2,1)S(1)} %all-to-all-done.2) | copy-start | bytes 3145732
  178.2 23.4 %all-to-all-start.5 = ((f32[128,3,256]{2,1,0:T(4,128)}), f32[128,3,256]{2,1,0:T(4,128)S(1)}, u32[]{:S(2)}, u32[]{:S(2)}) async-start(f32[128,3,256]{2,1,0:T(4,128)} %broadcast_in_dim.11), calls=%async_computation.5 | async-start | bytes 1048576 | tf_op jit(solution)/shard_map/all_to_all | solution.py:163
  201.7 142.1 %all-to-all-start.3 = ((bf16[32,512,256]{2,1,0:T(8,128)(2,1)}), bf16[32,512,256]{2,1,0:T(8,128)(2,1)}, u32[]{:S(2)}, u32[]{:S(2)}) async-start(bf16[32,512,256]{2,1,0:T(8,128)(2,1)} %bitcast.13), calls=%async_computation.3 | async-start | bytes 16777216 | tf_op jit(solution)/shard_map/all_to_all | solution.py:188

commit v10 on v8

--- a/solution.py
+++ b/solution.py
@@ -165,6 +165,7 @@
     layer_out, weight_grad, bias_grad, hidden_grad = dense_part(own_rows, weight, bias, cotangent)
     weight_grad, bias_grad = all_sum(weight_grad * grad_scale, bias_grad * grad_scale)
     grad_block = gather_over(hidden_grad, "row")
+    grad_block, weight_grad, bias_grad = lax.optimization_barrier((grad_block, weight_grad, bias_grad))
     grad_tiles = grad_block.reshape(row_tiles, tile_size, width)
 
     summed = aggregate_transposed(tile_values, tile_cols, live_counts, grad_tiles, column_tiles)

time: 355 us -> 333 us (0.938)
  the two profiles are of different devices: /device:TPU:66 before, /device:TPU:8 now
where the time goes in v10:
time: 333 us; the launch traced here: 332 us
  blocking collectives  240 us (72%)
  waiting for transfers between devices  36.8 us (11%)
  Pallas kernels  27.2 us (8%)
  starting transfers between devices  13.4 us (4%)
  local copies, waits for them, and re-layouts  6.65 us (2%)
  other arithmetic  5.98 us (2%)
    all_to_all x1, blocking collectives, sum_scatter_over(): got = lax.all_to_all(parts, axis, 0, 0, tiled=True)  112 us
    all_to_all x1, blocking collectives, gather_over(): got = lax.all_to_all(spread, axis, 0, 0, tiled=True)  110 us
    all_to_all x1, blocking collectives, all_sum(): lax.all_to_all(packed.reshape(devices, per, width), axes, 0, 0, tiled=True)  18.5 us
    pallas_call x1, Pallas kernels, aggregate_transposed(): pl.pallas_call(backward_kernel, out_shape=jax.ShapeDtypeStruct((col_tiles...  15 us
    all_to_all x1, waiting for transfers between devices, all_sum(): lax.all_to_all(spread, axes, 0, 0, tiled=True).reshape(devices * per, width)  13 us
    all_to_all x1, waiting for transfers between devices, sum_scatter_over(): got = lax.all_to_all(parts, axis, 0, 0, tiled=True)  12.5 us
    pallas_call x1, Pallas kernels, aggregate(): pl.pallas_call(forward_kernel, out_shape=jax.ShapeDtypeStruct((row_tiles,...  12.3 us
    all_to_all x1, waiting for transfers between devices, gather_over(): got = lax.all_to_all(spread, axis, 0, 0, tiled=True)  11.3 us
  transfers between devices with their start and end apart: 3, of which 3 were waited for; matrix products, arithmetic and copies ran while one was open for 1% of the time, Pallas kernels for 0%

profile of v10, /device:TPU:8, one launch (start us, length us, event | category | flops | bytes accessed | tf_op | source)
XLA Modules:
  0.0 332.2 jit_solution(2338854356442504935)
XLA Ops:
  0.6 0.0 copy-start
  0.6 1.9 broadcast_in_dim.8
  2.6 109.8 %all_to_all.30 = bf16[32,512,256]{2,1,0:T(8,128)(2,1)} all-to-all(bf16[32,512,256]{2,1,0:T(8,128)(2,1)S(1)} %broadcast_in_dim.8), channel_id=1, replica_groups=mesh['row'=4,'col'=32] {'col'}, dimensions={0} | all-to-all | bytes 16777216 | tf_op jit(solution)/shard_map/all_to_all | solution.py:109
  112.4 0.0 copy-start.2
  112.4 0.0 copy-start.3
  112.4 12.3 %shard_map.102 = bf16[8,256,256]{2,1,0:T(8,128)(2,1)} custom-call(s32[8,16]{1,0:T(8,128)} %cols_ref.3, s32[8]{0:T(128)} %bitcast.19, bf16[8,16,256,256]{3,2,1,0:T(8,128)(2,1)} %a_ref.3, bf16[64,256,256]{2,1,0:T(8,128)(2,1)} %bitcast.14), custom_call_target="tpu_custom_call" | custom-call | tf_op jit(solution)/shard_map/pallas_call | solution.py:66
  124.6 3.5 %all-to-all-start.1 = ((bf16[4,512,256]{2,1,0:T(8,128)(2,1)}), bf16[4,512,256]{2,1,0:T(8,128)(2,1)S(1)}, u32[]{:S(2)}, u32[]{:S(2)}) async-start(bf16[4,512,256]{2,1,0:T(8,128)(2,1)} %bitcast.17), calls=%async_computation.1 | async-start | bytes 2097152 | tf_op jit(solution)/shard_map/all_to_all | solution.py:116
  128.1 0.1 pad.2.clone
  128.2 12.5 %all-to-all-done.1 = bf16[4,512,256]{2,1,0:T(8,128)(2,1)S(1)} async-done(((bf16[4,512,256]{2,1,0:T(8,128)(2,1)}), bf16[4,512,256]{2,1,0:T(8,128)(2,1)S(1)}, u32[]{:S(2)}, u32[]{:S(2)}) %all-to-all-start.1) | async-done | bytes 1048608 | tf_op jit(solution)/shard_map/all_to_all | solution.py:116
  140.7 0.3 reduce_sum.42
  141.0 0.0 copy-done
  141.0 0.0 copy-done.2
  141.0 0.0 copy-done.3
  141.0 1.1 convert_reduce_fusion
  142.1 0.3 convolution_multiply_fusion
  142.4 0.1 maximum_maximum_fusion
  142.5 0.2 reshape.34
  142.7 18.5 %all_to_all.31 = f32[128,3,256]{2,1,0:T(4,128)S(1)} all-to-all(f32[128,3,256]{2,1,0:T(4,128)S(1)} %reshape.34), channel_id=1, replica_groups=mesh['row'=4,'col'=32] {'row','col'}, dimensions={0} | all-to-all | bytes 786432 | tf_op jit(solution)/shard_map/all_to_all | solution.py:145
  161.2 0.1 reduce_sum.44
  161.3 0.9 broadcast_in_dim.11
  162.2 5.0 %all-to-all-start.4 = ((f32[128,3,256]{2,1,0:T(4,128)}), f32[128,3,256]{2,1,0:T(4,128)S(1)}, u32[]{:S(2)}, u32[]{:S(2)}) async-start(f32[128,3,256]{2,1,0:T(4,128)} %broadcast_in_dim.11), calls=%async_computation.4 | async-start | bytes 1048576 | tf_op jit(solution)/shard_map/all_to_all | solution.py:148
  167.2 0.3 convolution_convert_fusion
  167.4 13.0 %all-to-all-done.4 = f32[128,3,256]{2,1,0:T(4,128)S(1)} async-done(((f32[128,3,256]{2,1,0:T(4,128)}), f32[128,3,256]{2,1,0:T(4,128)S(1)}, u32[]{:S(2)}, u32[]{:S(2)}) %all-to-all-start.4) | async-done | bytes 393248 | tf_op jit(solution)/shard_map/all_to_all | solution.py:148
  180.4 1.1 broadcast_in_dim.9
  181.5 4.9 %all-to-all-start.2 = ((bf16[4,512,256]{2,1,0:T(8,128)(2,1)}), bf16[4,512,256]{2,1,0:T(8,128)(2,1)S(1)}, u32[]{:S(2)}, u32[]{:S(2)}) async-start(bf16[4,512,256]{2,1,0:T(8,128)(2,1)} %broadcast_in_dim.9), calls=%async_computation.2 | async-start | bytes 2097152 | tf_op jit(solution)/shard_map/all_to_all | solution.py:109
  186.4 0.2 reshape.35
  186.6 0.6 slice.9
  187.1 0.7 slice.8
  187.9 11.3 %all-to-all-done.2 = bf16[4,512,256]{2,1,0:T(8,128)(2,1)S(1)} async-done(((bf16[4,512,256]{2,1,0:T(8,128)(2,1)}), bf16[4,512,256]{2,1,0:T(8,128)(2,1)S(1)}, u32[]{:S(2)}, u32[]{:S(2)}) %all-to-all-start.2) | async-done | bytes 1048608 | tf_op jit(solution)/shard_map/all_to_all | solution.py:109
  199.2 0.0 copy-start.1
  199.2 1.1 copy-done.1
  200.2 15.0 %shard_map.103 = bf16[64,256,256]{2,1,0:T(8,128)(2,1)} custom-call(s32[8,16]{1,0:T(8,128)} %cols_ref.3, s32[8]{0:T(128)} %bitcast.20, bf16[8,16,256,256]{3,2,1,0:T(8,128)(2,1)} %a_ref.3, bf16[8,256,256]{2,1,0:T(8,128)(2,1)} %bitcast.16), custom_call_target="tpu_custom_call" | custom-call | tf_op jit(solution)/shard_map/pallas_call | solution.py:89
  215.2 111.5 %all_to_all.32 = bf16[32,512,256]{2,1,0:T(8,128)(2,1)} all-to-all(bf16[32,512,256]{2,1,0:T(8,128)(2,1)} %bitcast.15), channel_id=1, replica_groups=mesh['row'=4,'col'=32] {'col'}, dimensions={0} | all-to-all | bytes 16777216 | tf_op jit(solution)/shard_map/all_to_all | solution.py:116
  326.7 5.5 %reduce_sum.45 = bf16[512,256]{1,0:T(8,128)(2,1)} reduce(bf16[32,512,256]{2,1,0:T(8,128)(2,1)} %all_to_all.32, bf16[]{:T(256)} %constant.4.clone.1), dimensions={0}, to_apply=%region_3.4 | reduce | flops 4063232 | bytes 8650754 | tf_op jit(solution)/shard_map/reduce_sum | solution.py:117
  (2 shorter events, 0.0 us)
Async XLA Ops:
  0.6 140.3 %copy-start = (bf16[256,256]{1,0:T(8,128)(2,1)S(1)}, bf16[256,256]{1,0:T(8,128)(2,1)}, u32[]{:S(2)}) copy-start(bf16[256,256]{1,0:T(8,128)(2,1)} %param.11) | copy-start | bytes 393220
  112.4 28.6 %copy-start.2 = (bf16[512,256]{1,0:T(8,128)(2,1)S(1)}, bf16[512,256]{1,0:T(8,128)(2,1)}, u32[]{:S(2)}) copy-start(bf16[512,256]{1,0:T(8,128)(2,1)} %param.13) | copy-start | bytes 786436
  112.4 28.6 %copy-start.3 = (f32[256]{0:T(256)S(1)}, f32[256]{0:T(256)}, u32[]{:S(2)}) copy-start(f32[256]{0:T(256)} %param.12) | copy-start | bytes 3076
  124.6 16.1 %all-to-all-start.1 = ((bf16[4,512,256]{2,1,0:T(8,128)(2,1)}), bf16[4,512,256]{2,1,0:T(8,128)(2,1)S(1)}, u32[]{:S(2)}, u32[]{:S(2)}) async-start(bf16[4,512,256]{2,1,0:T(8,128)(2,1)} %bitcast.17), calls=%async_computation.1 | async-start | bytes 2097152 | tf_op jit(solution)/shard_map/all_to_all | solution.py:116
  162.2 18.2 %all-to-all-start.4 = ((f32[128,3,256]{2,1,0:T(4,128)}), f32[128,3,256]{2,1,0:T(4,128)S(1)}, u32[]{:S(2)}, u32[]{:S(2)}) async-start(f32[128,3,256]{2,1,0:T(4,128)} %broadcast_in_dim.11), calls=%async_computation.4 | async-start | bytes 1048576 | tf_op jit(solution)/shard_map/all_to_all | solution.py:148
  181.5 17.7 %all-to-all-start.2 = ((bf16[4,512,256]{2,1,0:T(8,128)(2,1)}), bf16[4,512,256]{2,1,0:T(8,128)(2,1)S(1)}, u32[]{:S(2)}, u32[]{:S(2)}) async-start(bf16[4,512,256]{2,1,0:T(8,128)(2,1)} %broadcast_in_dim.9), calls=%async_computation.2 | async-start | bytes 2097152 | tf_op jit(solution)/shard_map/all_to_all | solution.py:109
  199.2 1.1 copy-start.1

commit v11 on v8

--- a/solution.py
+++ b/solution.py
@@ -133,25 +133,16 @@
     return (output, weight_grad, bias_grad, hidden_grad)
 
 
-def all_sum(weight_grad, bias_grad):
-    axes = ("row", "col")
-    devices = lax.axis_size("row") * lax.axis_size("col")
-    width = weight_grad.shape[1]
-    rows = weight_grad.shape[0] + 1
-    per = -(-rows // devices)
-    packed = jnp.concatenate(
-        [weight_grad, bias_grad[None], jnp.zeros((per * devices - rows, width), jnp.float32)]
-    )
-    parts = lax.all_to_all(packed.reshape(devices, per, width), axes, 0, 0, tiled=True)
-    summed = parts.sum(axis=0, keepdims=True)
-    spread = jnp.broadcast_to(summed, (devices, per, width))
-    back = lax.all_to_all(spread, axes, 0, 0, tiled=True).reshape(devices * per, width)
-    return back[: rows - 1], back[rows - 1]
+def split_wide(v):
+    high = v.astype(jnp.bfloat16)
+    low = (v - high.astype(jnp.float32)).astype(jnp.bfloat16)
+    return high, low
 
 
 def per_device(features, tile_values, tile_cols, tile_counts, weight, bias, cotangent):
     node_dev, width = features.shape
     row_tiles, slot_count, tile_size, _ = tile_values.shape
+    n_row, n_col = lax.axis_size("row"), lax.axis_size("col")
     column_block = gather_over(features, "col")
     column_tiles = column_block.shape[0] // tile_size
     x_tiles = column_block.reshape(column_tiles, tile_size, width)
@@ -159,18 +150,45 @@
 
     partial_value = aggregate(tile_values, tile_cols, live_counts, x_tiles)
     partial_value = partial_value.reshape(row_tiles * tile_size, width)
-    node_total = node_dev * lax.axis_size("row") * lax.axis_size("col")
+    node_total = node_dev * n_row * n_col
     grad_scale = 1.0 / math.sqrt(node_total)
     own_rows = sum_scatter_over(partial_value, "row").astype(jnp.bfloat16)
     layer_out, weight_grad, bias_grad, hidden_grad = dense_part(own_rows, weight, bias, cotangent)
-    weight_grad, bias_grad = all_sum(weight_grad * grad_scale, bias_grad * grad_scale)
-    grad_block = gather_over(hidden_grad, "row")
+
+    terms = jnp.concatenate([weight_grad, bias_grad[None]]) * grad_scale
+    rows = terms.shape[0]
+    piece = -(-rows // n_col)
+    terms = jnp.concatenate([terms, jnp.zeros((piece * n_col - rows, width), jnp.float32)])
+    high, low = split_wide(terms)
+    payload = jnp.concatenate([hidden_grad, high, low])
+    got = lax.all_to_all(
+        jnp.broadcast_to(payload[None], (n_row,) + payload.shape), "row", 0, 0, tiled=True
+    )
+    grad_block = got[:, :node_dev].reshape(n_row * node_dev, width)
+    kept = piece * n_col
+    row_sum = (
+        got[:, node_dev : node_dev + kept].astype(jnp.float32)
+        + got[:, node_dev + kept :].astype(jnp.float32)
+    ).sum(axis=0)
     grad_tiles = grad_block.reshape(row_tiles, tile_size, width)
 
     summed = aggregate_transposed(tile_values, tile_cols, live_counts, grad_tiles, column_tiles)
-    summed = summed.reshape(column_tiles * tile_size, width)
-    feature_grad = sum_scatter_over(summed, "col").astype(jnp.bfloat16)
-    return (layer_out, feature_grad, weight_grad, bias_grad)
+    parts = summed.reshape(n_col, -1, width)
+    chunk = parts.shape[1]
+    high, low = split_wide(row_sum)
+    payload = jnp.concatenate(
+        [parts, high.reshape(n_col, piece, width), low.reshape(n_col, piece, width)], axis=1
+    )
+    got = lax.all_to_all(payload, "col", 0, 0, tiled=True)
+    feature_grad = got[:, :chunk].astype(jnp.float32).sum(axis=0).astype(jnp.bfloat16)
+    own_piece = (
+        got[:, chunk : chunk + piece].astype(jnp.float32)
+        + got[:, chunk + piece :].astype(jnp.float32)
+    ).sum(axis=0)
+    total = lax.all_to_all(
+        jnp.broadcast_to(own_piece[None], (n_col, piece, width)), "col", 0, 0, tiled=True
+    ).reshape(n_col * piece, width)
+    return (layer_out, feature_grad, total[: rows - 1], total[rows - 1])
 
 
 def solution(mesh):

time: 355 us -> 327 us (0.921)
  waiting for transfers between devices: 169 us -> 4.55 us
  blocking collectives: 105 us -> 259 us
  starting transfers between devices: 33.4 us -> 7.8 us
  other arithmetic: 5.98 us -> 10.9 us
    all_to_all x5 -> x1, waiting for transfers between devices: 169 us -> 4.55 us  [per_device(): lax.all_to_all(jnp.broadcast_to(own_piece[None], (n_col, piece, width)),...]
    all_to_all x0 -> x3, blocking collectives: none -> 154 us  [the longest x1 107 us: per_device(): got = lax.all_to_all(payload, 'col', 0, 0, tiled=True)]
    all_to_all x5 -> x1, starting transfers between devices: 33.4 us -> 7.8 us  [per_device(): lax.all_to_all(jnp.broadcast_to(own_piece[None], (n_col, piece, width)),...]
    reduce_sum x1 -> x3, other arithmetic: 0.15 us -> 5.74 us  [the longest x1 5.46 us: per_device(): got[:, :chunk].astype(jnp.float32).sum(axis=0).astype(jnp.bfloat16)]
    reduce_sum x2 -> x1, other arithmetic: 5.71 us -> 0.26 us  [sum_scatter_over(): return got.astype(jnp.float32).sum(axis=0)]
    concatenate x1 -> x2, other arithmetic: 0.12 us -> 4.76 us  [the longest x1 4.72 us: per_device(): jnp.concatenate([parts, high.reshape(n_col, piece, width), low.reshape(n_...]
  transfers between devices with their start and end apart: 5 -> 1, of which waited for: 4 -> 1; matrix products, arithmetic and copies ran while one was open for 1% -> 2% of each run, Pallas kernels for 4% -> 0%
where the time goes in v11:
time: 327 us; the launch traced here: 321 us
  blocking collectives  259 us (79%)
  Pallas kernels  27.2 us (8%)
  other arithmetic  10.9 us (3%)
  local copies, waits for them, and re-layouts  8.91 us (3%)
  starting transfers between devices  7.8 us (2%)
  waiting for transfers between devices  4.55 us (1%)
    all_to_all x1, blocking collectives, per_device(): got = lax.all_to_all(payload, 'col', 0, 0, tiled=True)  107 us
    all_to_all x1, blocking collectives, gather_over(): got = lax.all_to_all(spread, axis, 0, 0, tiled=True)  105 us
    all_to_all x1, blocking collectives, per_device(): lax.all_to_all(jnp.broadcast_to(payload[None], (n_row,) + payload.shape),...  29.6 us
    all_to_all x1, blocking collectives, sum_scatter_over(): got = lax.all_to_all(parts, axis, 0, 0, tiled=True)  17.9 us
    pallas_call x1, Pallas kernels, aggregate_transposed(): pl.pallas_call(backward_kernel, out_shape=jax.ShapeDtypeStruct((col_tiles...  15 us
    pallas_call x1, Pallas kernels, aggregate(): pl.pallas_call(forward_kernel, out_shape=jax.ShapeDtypeStruct((row_tiles,...  12.3 us
    all_to_all x1, starting transfers between devices, per_device(): lax.all_to_all(jnp.broadcast_to(own_piece[None], (n_col, piece, width)),...  7.8 us
  transfers between devices with their start and end apart: 1, of which 1 were waited for; matrix products, arithmetic and copies ran while one was open for 2% of the time, Pallas kernels for 0%

profile of v11, /device:TPU:66, one launch (start us, length us, event | category | flops | bytes accessed | tf_op | source)
XLA Modules:
  0.0 321.2 jit_solution(17879487690715329820)
XLA Ops:
  0.6 0.0 copy-start
  0.6 1.9 broadcast_in_dim.8
  2.6 105.0 %all_to_all.25 = bf16[32,512,256]{2,1,0:T(8,128)(2,1)} all-to-all(bf16[32,512,256]{2,1,0:T(8,128)(2,1)S(1)} %broadcast_in_dim.8), channel_id=1, replica_groups=mesh['row'=4,'col'=32] {'col'}, dimensions={0} | all-to-all | bytes 16777216 | tf_op jit(solution)/shard_map/all_to_all | solution.py:109
  107.6 0.0 copy-start.3
  107.6 0.0 copy-start.4
  107.6 12.3 %shard_map.102 = bf16[8,256,256]{2,1,0:T(8,128)(2,1)} custom-call(s32[8,16]{1,0:T(8,128)} %cols_ref.3, s32[8]{0:T(128)} %bitcast.17, bf16[8,16,256,256]{3,2,1,0:T(8,128)(2,1)} %a_ref.3, bf16[64,256,256]{2,1,0:T(8,128)(2,1)} %bitcast.14), custom_call_target="tpu_custom_call" | custom-call | tf_op jit(solution)/shard_map/pallas_call | solution.py:66
  119.9 17.9 %all_to_all.26 = bf16[4,512,256]{2,1,0:T(8,128)(2,1)S(1)} all-to-all(bf16[4,512,256]{2,1,0:T(8,128)(2,1)} %bitcast.15), channel_id=1, replica_groups=mesh['row'=4,'col'=32] {'row'}, dimensions={0} | all-to-all | bytes 2097152 | tf_op jit(solution)/shard_map/all_to_all | solution.py:116
  137.8 0.3 reduce_sum.53
  138.1 0.0 copy-done
  138.1 0.0 copy-done.3
  138.1 0.0 copy-done.4
  138.1 1.1 convert_reduce_fusion
  139.2 0.3 fusion
  139.6 0.3 convolution_convert_fusion
  139.9 0.1 broadcast_in_dim.10
  140.0 29.6 %all_to_all.27 = bf16[4,1088,256]{2,1,0:T(8,128)(2,1)S(1)} all-to-all(bf16[4,1088,256]{2,1,0:T(8,128)(2,1)S(1)} %broadcast_in_dim.10), channel_id=1, replica_groups=mesh['row'=4,'col'=32] {'row'}, dimensions={0} | all-to-all | bytes 4456448 | tf_op jit(solution)/shard_map/all_to_all | solution.py:164
  169.6 0.2 add_reduce_fusion
  169.8 0.1 subtract_convert_fusion
  169.9 1.1 slice.32
  171.0 15.0 %shard_map.103 = bf16[64,256,256]{2,1,0:T(8,128)(2,1)} custom-call(s32[8,16]{1,0:T(8,128)} %cols_ref.3, s32[8]{0:T(128)} %bitcast.18, bf16[8,16,256,256]{3,2,1,0:T(8,128)(2,1)} %a_ref.3, bf16[8,256,256]{2,1,0:T(8,128)(2,1)} %bitcast.16), custom_call_target="tpu_custom_call" | custom-call | tf_op jit(solution)/shard_map/pallas_call | solution.py:89
  186.0 4.7 %pad_maximum_fusion = bf16[32,530,256]{2,1,0:T(8,128)(2,1)S(1)} fusion(bf16[32,9,256]{2,1,0:T(8,128)(2,1)S(1)} %get-tuple-element.4, bf16[32,9,256]{2,1,0:T(8,128)(2,1)S(1)} %get-tuple-element.5, bf16[32,512,256]{2,1,0:T(8,128)(2,1)} %bitcast.13), kind=kLoop, calls=%fused_computation | loop fusion | flops 26050560 | bytes 17367040 | tf_op jit(solution)/shard_map/concatenate | solution.py:179
  190.7 0.0 copy-start.1
  190.7 106.9 %all_to_all.28 = bf16[32,530,256]{2,1,0:T(8,128)(2,1)S(1)} all-to-all(bf16[32,530,256]{2,1,0:T(8,128)(2,1)S(1)} %pad_maximum_fusion), channel_id=1, replica_groups=mesh['row'=4,'col'=32] {'col'}, dimensions={0} | all-to-all | bytes 17367040 | tf_op jit(solution)/shard_map/all_to_all | solution.py:182
  297.6 0.0 copy-start.2
  297.6 3.4 %copy-done.2 = bf16[32,530,256]{2,1,0:T(8,128)(2,1)} copy-done((bf16[32,530,256]{2,1,0:T(8,128)(2,1)}, bf16[32,530,256]{2,1,0:T(8,128)(2,1)S(1)}, u32[]{:S(2)}) %copy-start.2) | copy-done | bytes 8683544
  301.0 0.1 add_reduce_fusion.1
  301.1 0.9 broadcast_in_dim.11
  302.0 7.8 %all-to-all-start.4 = ((f32[32,9,256]{2,1,0:T(8,128)}), f32[32,9,256]{2,1,0:T(8,128)S(1)}, u32[]{:S(2)}, u32[]{:S(2)}) async-start(f32[32,9,256]{2,1,0:T(8,128)} %broadcast_in_dim.11), calls=%async_computation.4 | async-start | bytes 1048576 | tf_op jit(solution)/shard_map/all_to_all | solution.py:188
  309.8 5.5 %slice_reduce_fusion = bf16[512,256]{1,0:T(8,128)(2,1)} fusion(bf16[32,530,256]{2,1,0:T(8,128)(2,1)} %copy-done.2), kind=kLoop, calls=%fused_computation.1 | loop fusion | flops 4063232 | bytes 8650752 | tf_op jit(solution)/shard_map/reduce_sum | solution.py:183
  315.3 4.5 %all-to-all-done.4 = f32[32,9,256]{2,1,0:T(8,128)S(1)} async-done(((f32[32,9,256]{2,1,0:T(8,128)}), f32[32,9,256]{2,1,0:T(8,128)S(1)}, u32[]{:S(2)}, u32[]{:S(2)}) %all-to-all-start.4) | async-done | bytes 294944 | tf_op jit(solution)/shard_map/all_to_all | solution.py:188
  319.8 0.1 reshape.23
  319.9 0.6 slice.39
  320.4 0.7 slice.38
  321.2 0.0 copy-done.1
  (5 shorter events, 0.1 us)
Async XLA Ops:
  0.6 137.4 %copy-start = (bf16[256,256]{1,0:T(8,128)(2,1)S(1)}, bf16[256,256]{1,0:T(8,128)(2,1)}, u32[]{:S(2)}) copy-start(bf16[256,256]{1,0:T(8,128)(2,1)} %param.11) | copy-start | bytes 393220
  107.6 30.5 %copy-start.3 = (bf16[512,256]{1,0:T(8,128)(2,1)S(1)}, bf16[512,256]{1,0:T(8,128)(2,1)}, u32[]{:S(2)}) copy-start(bf16[512,256]{1,0:T(8,128)(2,1)} %param.13) | copy-start | bytes 786436
  107.6 30.5 %copy-start.4 = (f32[256]{0:T(256)S(1)}, f32[256]{0:T(256)}, u32[]{:S(2)}) copy-start(f32[256]{0:T(256)} %param.12) | copy-start | bytes 3076
  190.7 130.4 %copy-start.1 = (bf16[256,256]{1,0:T(8,128)(2,1)S(1)}, bf16[256,256]{1,0:T(8,128)(2,1)}, u32[]{:S(2)}) copy-start(bf16[256,256]{1,0:T(8,128)(2,1)} %param.11) | copy-start | bytes 393220
  297.6 3.4 %copy-start.2 = (bf16[32,530,256]{2,1,0:T(8,128)(2,1)}, bf16[32,530,256]{2,1,0:T(8,128)(2,1)S(1)}, u32[]{:S(2)}) copy-start(bf16[32,530,256]{2,1,0:T(8,128)(2,1)S(1)} %all_to_all.28) | copy-start | bytes 26050564
  302.0 17.8 %all-to-all-start.4 = ((f32[32,9,256]{2,1,0:T(8,128)}), f32[32,9,256]{2,1,0:T(8,128)S(1)}, u32[]{:S(2)}, u32[]{:S(2)}) async-start(f32[32,9,256]{2,1,0:T(8,128)} %broadcast_in_dim.11), calls=%async_computation.4 | async-start | bytes 1048576 | tf_op jit(solution)/shard_map/all_to_all | solution.py:188

commit v12 on v11

--- a/solution.py
+++ b/solution.py
@@ -133,12 +133,6 @@
     return (output, weight_grad, bias_grad, hidden_grad)
 
 
-def split_wide(v):
-    high = v.astype(jnp.bfloat16)
-    low = (v - high.astype(jnp.float32)).astype(jnp.bfloat16)
-    return high, low
-
-
 def per_device(features, tile_values, tile_cols, tile_counts, weight, bias, cotangent):
     node_dev, width = features.shape
     row_tiles, slot_count, tile_size, _ = tile_values.shape
@@ -159,32 +153,23 @@
     rows = terms.shape[0]
     piece = -(-rows // n_col)
     terms = jnp.concatenate([terms, jnp.zeros((piece * n_col - rows, width), jnp.float32)])
-    high, low = split_wide(terms)
-    payload = jnp.concatenate([hidden_grad, high, low])
+    payload = jnp.concatenate([hidden_grad, terms.astype(jnp.bfloat16)])
     got = lax.all_to_all(
         jnp.broadcast_to(payload[None], (n_row,) + payload.shape), "row", 0, 0, tiled=True
     )
     grad_block = got[:, :node_dev].reshape(n_row * node_dev, width)
-    kept = piece * n_col
-    row_sum = (
-        got[:, node_dev : node_dev + kept].astype(jnp.float32)
-        + got[:, node_dev + kept :].astype(jnp.float32)
-    ).sum(axis=0)
+    row_sum = got[:, node_dev:].astype(jnp.float32).sum(axis=0)
     grad_tiles = grad_block.reshape(row_tiles, tile_size, width)
 
     summed = aggregate_transposed(tile_values, tile_cols, live_counts, grad_tiles, column_tiles)
     parts = summed.reshape(n_col, -1, width)
     chunk = parts.shape[1]
-    high, low = split_wide(row_sum)
     payload = jnp.concatenate(
-        [parts, high.reshape(n_col, piece, width), low.reshape(n_col, piece, width)], axis=1
+        [parts, row_sum.astype(jnp.bfloat16).reshape(n_col, piece, width)], axis=1
     )
     got = lax.all_to_all(payload, "col", 0, 0, tiled=True)
     feature_grad = got[:, :chunk].astype(jnp.float32).sum(axis=0).astype(jnp.bfloat16)
-    own_piece = (
-        got[:, chunk : chunk + piece].astype(jnp.float32)
-        + got[:, chunk + piece :].astype(jnp.float32)
-    ).sum(axis=0)
+    own_piece = got[:, chunk:].astype(jnp.float32).sum(axis=0)
     total = lax.all_to_all(
         jnp.broadcast_to(own_piece[None], (n_col, piece, width)), "col", 0, 0, tiled=True
     ).reshape(n_col * piece, width)

time: 327 us -> 317 us (0.969)
  blocking collectives: 259 us -> 252 us
    all_to_all x1, blocking collectives: 29.6 us -> 23.2 us  [per_device(): lax.all_to_all(jnp.broadcast_to(payload[None], (n_row,) + payload.shape),...]
where the time goes in v12:
time: 317 us; the launch traced here: 313 us
  blocking collectives  252 us (79%)
  Pallas kernels  27.2 us (9%)
  other arithmetic  10.2 us (3%)
  local copies, waits for them, and re-layouts  8.79 us (3%)
  starting transfers between devices  7.72 us (2%)
  waiting for transfers between devices  4.31 us (1%)
    all_to_all x1, blocking collectives, per_device(): got = lax.all_to_all(payload, 'col', 0, 0, tiled=True)  106 us
    all_to_all x1, blocking collectives, gather_over(): got = lax.all_to_all(spread, axis, 0, 0, tiled=True)  105 us
    all_to_all x1, blocking collectives, per_device(): lax.all_to_all(jnp.broadcast_to(payload[None], (n_row,) + payload.shape),...  23.2 us
    all_to_all x1, blocking collectives, sum_scatter_over(): got = lax.all_to_all(parts, axis, 0, 0, tiled=True)  17.9 us
    pallas_call x1, Pallas kernels, aggregate_transposed(): pl.pallas_call(backward_kernel, out_shape=jax.ShapeDtypeStruct((col_tiles...  15 us
    pallas_call x1, Pallas kernels, aggregate(): pl.pallas_call(forward_kernel, out_shape=jax.ShapeDtypeStruct((row_tiles,...  12.3 us
    all_to_all x1, starting transfers between devices, per_device(): lax.all_to_all(jnp.broadcast_to(own_piece[None], (n_col, piece, width)),...  7.72 us
  transfers between devices with their start and end apart: 1, of which 1 were waited for; matrix products, arithmetic and copies ran while one was open for 2% of the time, Pallas kernels for 0%

profile of v12, /device:TPU:66, one launch (start us, length us, event | category | flops | bytes accessed | tf_op | source)
XLA Modules:
  0.0 312.6 jit_solution(10965353520925745791)
XLA Ops:
  0.6 0.0 copy-start
  0.6 1.9 broadcast_in_dim.8
  2.6 105.0 %all_to_all.25 = bf16[32,512,256]{2,1,0:T(8,128)(2,1)} all-to-all(bf16[32,512,256]{2,1,0:T(8,128)(2,1)S(1)} %broadcast_in_dim.8), channel_id=1, replica_groups=mesh['row'=4,'col'=32] {'col'}, dimensions={0} | all-to-all | bytes 16777216 | tf_op jit(solution)/shard_map/all_to_all | solution.py:109
  107.6 0.0 copy-start.3
  107.6 0.0 copy-start.4
  107.6 12.3 %shard_map.102 = bf16[8,256,256]{2,1,0:T(8,128)(2,1)} custom-call(s32[8,16]{1,0:T(8,128)} %cols_ref.3, s32[8]{0:T(128)} %bitcast.17, bf16[8,16,256,256]{3,2,1,0:T(8,128)(2,1)} %a_ref.3, bf16[64,256,256]{2,1,0:T(8,128)(2,1)} %bitcast.14), custom_call_target="tpu_custom_call" | custom-call | tf_op jit(solution)/shard_map/pallas_call | solution.py:66
  119.9 17.9 %all_to_all.26 = bf16[4,512,256]{2,1,0:T(8,128)(2,1)S(1)} all-to-all(bf16[4,512,256]{2,1,0:T(8,128)(2,1)} %bitcast.15), channel_id=1, replica_groups=mesh['row'=4,'col'=32] {'row'}, dimensions={0} | all-to-all | bytes 2097152 | tf_op jit(solution)/shard_map/all_to_all | solution.py:116
  137.8 0.3 reduce_sum.54
  138.1 0.0 copy-done
  138.1 0.0 copy-done.3
  138.1 0.0 copy-done.4
  138.1 1.1 convert_reduce_fusion.1
  139.2 0.3 fusion.3
  139.5 0.3 convolution_convert_fusion
  139.8 0.1 broadcast_in_dim.10
  139.9 23.2 %all_to_all.27 = bf16[4,800,256]{2,1,0:T(8,128)(2,1)S(1)} all-to-all(bf16[4,800,256]{2,1,0:T(8,128)(2,1)S(1)} %broadcast_in_dim.10), channel_id=1, replica_groups=mesh['row'=4,'col'=32] {'row'}, dimensions={0} | all-to-all | bytes 3276800 | tf_op jit(solution)/shard_map/all_to_all | solution.py:157
  163.2 0.1 slice_reduce_fusion.1
  163.2 0.1 reshape.22
  163.3 1.1 slice.24
  164.5 15.0 %shard_map.103 = bf16[64,256,256]{2,1,0:T(8,128)(2,1)} custom-call(s32[8,16]{1,0:T(8,128)} %cols_ref.3, s32[8]{0:T(128)} %bitcast.18, bf16[8,16,256,256]{3,2,1,0:T(8,128)(2,1)} %a_ref.3, bf16[8,256,256]{2,1,0:T(8,128)(2,1)} %bitcast.16), custom_call_target="tpu_custom_call" | custom-call | tf_op jit(solution)/shard_map/pallas_call | solution.py:89
  179.4 4.3 %pad_maximum_fusion = bf16[32,521,256]{2,1,0:T(8,128)(2,1)S(1)} fusion(bf16[32,9,256]{2,1,0:T(8,128)(2,1)S(1)} %reshape.22, bf16[32,512,256]{2,1,0:T(8,128)(2,1)} %bitcast.13), kind=kLoop, calls=%fused_computation | loop fusion | flops 17072128 | bytes 17072128 | tf_op jit(solution)/shard_map/concatenate | solution.py:167
  183.7 0.0 copy-start.1
  183.7 105.8 %all_to_all.28 = bf16[32,521,256]{2,1,0:T(8,128)(2,1)S(1)} all-to-all(bf16[32,521,256]{2,1,0:T(8,128)(2,1)S(1)} %pad_maximum_fusion), channel_id=1, replica_groups=mesh['row'=4,'col'=32] {'col'}, dimensions={0} | all-to-all | bytes 17072128 | tf_op jit(solution)/shard_map/all_to_all | solution.py:170
  289.5 0.0 copy-start.2
  289.5 3.3 %copy-done.2 = bf16[32,521,256]{2,1,0:T(8,128)(2,1)} copy-done((bf16[32,521,256]{2,1,0:T(8,128)(2,1)}, bf16[32,521,256]{2,1,0:T(8,128)(2,1)S(1)}, u32[]{:S(2)}) %copy-start.2) | copy-done | bytes 8536088
  292.8 0.1 convert_reduce_fusion
  292.9 0.9 broadcast_in_dim.11
  293.8 7.7 %all-to-all-start.4 = ((f32[32,9,256]{2,1,0:T(8,128)}), f32[32,9,256]{2,1,0:T(8,128)S(1)}, u32[]{:S(2)}, u32[]{:S(2)}) async-start(f32[32,9,256]{2,1,0:T(8,128)} %broadcast_in_dim.11), calls=%async_computation.4 | async-start | bytes 1048576 | tf_op jit(solution)/shard_map/all_to_all | solution.py:173
  301.5 5.5 %slice_reduce_fusion = bf16[512,256]{1,0:T(8,128)(2,1)} fusion(bf16[32,521,256]{2,1,0:T(8,128)(2,1)} %copy-done.2), kind=kLoop, calls=%fused_computation.1 | loop fusion | flops 4063232 | bytes 8650752 | tf_op jit(solution)/shard_map/reduce_sum | solution.py:171
  307.0 4.3 %all-to-all-done.4 = f32[32,9,256]{2,1,0:T(8,128)S(1)} async-done(((f32[32,9,256]{2,1,0:T(8,128)}), f32[32,9,256]{2,1,0:T(8,128)S(1)}, u32[]{:S(2)}, u32[]{:S(2)}) %all-to-all-start.4) | async-done | bytes 294944 | tf_op jit(solution)/shard_map/all_to_all | solution.py:173
  311.3 0.1 reshape.23
  311.3 0.6 slice.29
  311.9 0.7 slice.28
  312.6 0.0 copy-done.1
  (2 shorter events, 0.1 us)
Async XLA Ops:
  0.6 137.4 %copy-start = (bf16[256,256]{1,0:T(8,128)(2,1)S(1)}, bf16[256,256]{1,0:T(8,128)(2,1)}, u32[]{:S(2)}) copy-start(bf16[256,256]{1,0:T(8,128)(2,1)} %param.11) | copy-start | bytes 393220
  107.6 30.5 %copy-start.3 = (bf16[512,256]{1,0:T(8,128)(2,1)S(1)}, bf16[512,256]{1,0:T(8,128)(2,1)}, u32[]{:S(2)}) copy-start(bf16[512,256]{1,0:T(8,128)(2,1)} %param.13) | copy-start | bytes 786436
  107.6 30.5 %copy-start.4 = (f32[256]{0:T(256)S(1)}, f32[256]{0:T(256)}, u32[]{:S(2)}) copy-start(f32[256]{0:T(256)} %param.12) | copy-start | bytes 3076
  183.7 128.9 %copy-start.1 = (bf16[256,256]{1,0:T(8,128)(2,1)S(1)}, bf16[256,256]{1,0:T(8,128)(2,1)}, u32[]{:S(2)}) copy-start(bf16[256,256]{1,0:T(8,128)(2,1)} %param.11) | copy-start | bytes 393220
  289.5 3.3 %copy-start.2 = (bf16[32,521,256]{2,1,0:T(8,128)(2,1)}, bf16[32,521,256]{2,1,0:T(8,128)(2,1)S(1)}, u32[]{:S(2)}) copy-start(bf16[32,521,256]{2,1,0:T(8,128)(2,1)S(1)} %all_to_all.28) | copy-start | bytes 25608196
  293.8 17.5 %all-to-all-start.4 = ((f32[32,9,256]{2,1,0:T(8,128)}), f32[32,9,256]{2,1,0:T(8,128)S(1)}, u32[]{:S(2)}, u32[]{:S(2)}) async-start(f32[32,9,256]{2,1,0:T(8,128)} %broadcast_in_dim.11), calls=%async_computation.4 | async-start | bytes 1048576 | tf_op jit(solution)/shard_map/all_to_all | solution.py:173

commit v13 on v12

--- a/solution.py
+++ b/solution.py
@@ -28,7 +28,7 @@
         o_ref[u] = acc.astype(o_ref.dtype)
 
 
-def backward_kernel(cols_ref, counts_ref, a_ref, g_ref, o_ref, acc_ref):
+def backward_kernel(cols_ref, counts_ref, a_ref, g_ref, w_ref, o_ref, acc_ref):
     step = pl.program_id(0)
     group, slots = a_ref.shape[:2]
     last = acc_ref.shape[0] - 1
@@ -53,11 +53,16 @@
 
     @pl.when(step == pl.num_programs(0) - 1)
     def _():
+        tile = acc_ref.shape[1]
+        per = o_ref.shape[1] // tile
+
         def put(j, carry):
-            o_ref[j] = acc_ref[j].astype(o_ref.dtype)
+            at = pl.multiple_of((j % per) * tile, tile)
+            o_ref[j // per, pl.ds(at, tile)] = acc_ref[j].astype(o_ref.dtype)
             return carry
 
         lax.fori_loop(0, acc_ref.shape[0], put, 0)
+        o_ref[:, pl.ds(per * tile, w_ref.shape[1])] = w_ref[...]
 
 
 def aggregate(tile_values, cols, counts, x_tiles):
@@ -83,24 +88,26 @@
     )(cols, counts, tile_values, x_tiles)
 
 
-def aggregate_transposed(tile_values, cols, counts, g_tiles, col_tiles):
+def aggregate_transposed(tile_values, cols, counts, g_tiles, pieces, col_tiles, chunk):
     row_tiles, slots, tile, _ = tile_values.shape
     width = g_tiles.shape[-1]
+    n_col, piece, _ = pieces.shape
     return pl.pallas_call(
         backward_kernel,
-        out_shape=jax.ShapeDtypeStruct((col_tiles, tile, width), jnp.bfloat16),
+        out_shape=jax.ShapeDtypeStruct((n_col, chunk + piece, width), jnp.bfloat16),
         grid_spec=pltpu.PrefetchScalarGridSpec(
             num_scalar_prefetch=2,
             grid=(row_tiles // GROUP,),
             in_specs=[
                 pl.BlockSpec((GROUP, slots, tile, tile), lambda t, c, n: (t, 0, 0, 0)),
                 pl.BlockSpec((GROUP, tile, width), lambda t, c, n: (t, 0, 0)),
+                pl.BlockSpec((n_col, piece, width), lambda t, c, n: (0, 0, 0)),
             ],
-            out_specs=pl.BlockSpec((col_tiles, tile, width), lambda t, c, n: (0, 0, 0)),
+            out_specs=pl.BlockSpec((n_col, chunk + piece, width), lambda t, c, n: (0, 0, 0)),
             scratch_shapes=[pltpu.VMEM((col_tiles, tile, width), jnp.float32)],
         ),
         compiler_params=pltpu.CompilerParams(vmem_limit_bytes=VMEM_LIMIT),
-    )(cols, counts, tile_values, g_tiles)
+    )(cols, counts, tile_values, g_tiles, pieces)
 
 
 def gather_over(x, axis):
@@ -161,11 +168,10 @@
     row_sum = got[:, node_dev:].astype(jnp.float32).sum(axis=0)
     grad_tiles = grad_block.reshape(row_tiles, tile_size, width)
 
-    summed = aggregate_transposed(tile_values, tile_cols, live_counts, grad_tiles, column_tiles)
-    parts = summed.reshape(n_col, -1, width)
-    chunk = parts.shape[1]
-    payload = jnp.concatenate(
-        [parts, row_sum.astype(jnp.bfloat16).reshape(n_col, piece, width)], axis=1
+    chunk = column_tiles * tile_size // n_col
+    pieces = row_sum.astype(jnp.bfloat16).reshape(n_col, piece, width)
+    payload = aggregate_transposed(
+        tile_values, tile_cols, live_counts, grad_tiles, pieces, column_tiles, chunk
     )
     got = lax.all_to_all(payload, "col", 0, 0, tiled=True)
     feature_grad = got[:, :chunk].astype(jnp.float32).sum(axis=0).astype(jnp.bfloat16)

time: 317 us -> 315 us (level)
  other arithmetic: 10.2 us -> 5.91 us
    concatenate x1 -> x0, other arithmetic: 4.25 us -> none  [per_device(): jnp.concatenate([parts, row_sum.astype(jnp.bfloat16).reshape(n_col, piece...]
where the time goes in v13:
time: 315 us; the launch traced here: 309 us
  blocking collectives  252 us (80%)
  Pallas kernels  27.6 us (9%)
  local copies, waits for them, and re-layouts  9.47 us (3%)
  starting transfers between devices  7.72 us (2%)
  other arithmetic  5.91 us (2%)
  waiting for transfers between devices  4.31 us (1%)
    all_to_all x1, blocking collectives, per_device(): got = lax.all_to_all(payload, 'col', 0, 0, tiled=True)  106 us
    all_to_all x1, blocking collectives, gather_over(): got = lax.all_to_all(spread, axis, 0, 0, tiled=True)  105 us
    all_to_all x1, blocking collectives, per_device(): lax.all_to_all(jnp.broadcast_to(payload[None], (n_row,) + payload.shape),...  23.2 us
    all_to_all x1, blocking collectives, sum_scatter_over(): got = lax.all_to_all(parts, axis, 0, 0, tiled=True)  17.9 us
    pallas_call x1, Pallas kernels, aggregate_transposed(): pl.pallas_call(backward_kernel, out_shape=jax.ShapeDtypeStruct((n_col, ch...  15.4 us
    pallas_call x1, Pallas kernels, aggregate(): pl.pallas_call(forward_kernel, out_shape=jax.ShapeDtypeStruct((row_tiles,...  12.3 us
    all_to_all x1, starting transfers between devices, per_device(): lax.all_to_all(jnp.broadcast_to(own_piece[None], (n_col, piece, width)),...  7.72 us
  transfers between devices with their start and end apart: 1, of which 1 were waited for; matrix products, arithmetic and copies ran while one was open for 2% of the time, Pallas kernels for 0%

profile of v13, /device:TPU:66, one launch (start us, length us, event | category | flops | bytes accessed | tf_op | source)
XLA Modules:
  0.0 309.5 jit_solution(4620224669443498182)
XLA Ops:
  0.6 0.0 copy-start
  0.6 1.9 broadcast_in_dim.8
  2.6 105.0 %all_to_all.25 = bf16[32,512,256]{2,1,0:T(8,128)(2,1)} all-to-all(bf16[32,512,256]{2,1,0:T(8,128)(2,1)S(1)} %broadcast_in_dim.8), channel_id=1, replica_groups=mesh['row'=4,'col'=32] {'col'}, dimensions={0} | all-to-all | bytes 16777216 | tf_op jit(solution)/shard_map/all_to_all | solution.py:116
  107.6 0.0 copy-start.2
  107.6 0.0 copy-start.3
  107.6 12.3 %shard_map.102 = bf16[8,256,256]{2,1,0:T(8,128)(2,1)} custom-call(s32[8,16]{1,0:T(8,128)} %cols_ref.3, s32[8]{0:T(128)} %bitcast.15, bf16[8,16,256,256]{3,2,1,0:T(8,128)(2,1)} %a_ref.3, bf16[64,256,256]{2,1,0:T(8,128)(2,1)} %bitcast.12), custom_call_target="tpu_custom_call" | custom-call | tf_op jit(solution)/shard_map/pallas_call | solution.py:71
  119.8 17.9 %all_to_all.26 = bf16[4,512,256]{2,1,0:T(8,128)(2,1)S(1)} all-to-all(bf16[4,512,256]{2,1,0:T(8,128)(2,1)} %bitcast.14), channel_id=1, replica_groups=mesh['row'=4,'col'=32] {'row'}, dimensions={0} | all-to-all | bytes 2097152 | tf_op jit(solution)/shard_map/all_to_all | solution.py:123
  137.8 0.3 reduce_sum.54
  138.1 0.0 copy-done
  138.1 0.0 copy-done.2
  138.1 0.0 copy-done.3
  138.1 1.1 convert_reduce_fusion.1
  139.2 0.3 fusion.3
  139.5 0.3 convolution_convert_fusion
  139.8 0.1 broadcast_in_dim.10
  139.9 23.2 %all_to_all.27 = bf16[4,800,256]{2,1,0:T(8,128)(2,1)S(1)} all-to-all(bf16[4,800,256]{2,1,0:T(8,128)(2,1)S(1)} %broadcast_in_dim.10), channel_id=1, replica_groups=mesh['row'=4,'col'=32] {'row'}, dimensions={0} | all-to-all | bytes 3276800 | tf_op jit(solution)/shard_map/all_to_all | solution.py:164
  163.1 0.1 slice_reduce_fusion.1
  163.2 0.8 reshape.18.w_ref
  164.0 1.1 slice.24
  165.1 15.4 %shard_map.103 = bf16[32,521,256]{2,1,0:T(8,128)(2,1)} custom-call(s32[8,16]{1,0:T(8,128)} %cols_ref.3, s32[8]{0:T(128)} %bitcast.16, bf16[8,16,256,256]{3,2,1,0:T(8,128)(2,1)} %a_ref.3, bf16[8,256,256]{2,1,0:T(8,128)(2,1)} %bitcast.13, bf16[32,9,256]{2,1,0:T(8,128)(2,1)} %reshape.18.w_ref), custom_call_target="tpu_custom_call" | custom-call | tf_op jit(solution)/shard_map/pallas_call | solution.py:95
  180.5 105.9 %all_to_all.28 = bf16[32,521,256]{2,1,0:T(8,128)(2,1)S(1)} all-to-all(bf16[32,521,256]{2,1,0:T(8,128)(2,1)} %shard_map.103), channel_id=1, replica_groups=mesh['row'=4,'col'=32] {'col'}, dimensions={0} | all-to-all | bytes 17072128 | tf_op jit(solution)/shard_map/all_to_all | solution.py:176
  286.4 0.0 copy-start.1
  286.4 3.3 %copy-done.1 = bf16[32,521,256]{2,1,0:T(8,128)(2,1)} copy-done((bf16[32,521,256]{2,1,0:T(8,128)(2,1)}, bf16[32,521,256]{2,1,0:T(8,128)(2,1)S(1)}, u32[]{:S(2)}) %copy-start.1) | copy-done | bytes 8536088
  289.7 0.1 convert_reduce_fusion
  289.8 0.9 broadcast_in_dim.11
  290.7 7.7 %all-to-all-start.4 = ((f32[32,9,256]{2,1,0:T(8,128)}), f32[32,9,256]{2,1,0:T(8,128)S(1)}, u32[]{:S(2)}, u32[]{:S(2)}) async-start(f32[32,9,256]{2,1,0:T(8,128)} %broadcast_in_dim.11), calls=%async_computation.4 | async-start | bytes 1048576 | tf_op jit(solution)/shard_map/all_to_all | solution.py:179
  298.4 5.5 %slice_reduce_fusion = bf16[512,256]{1,0:T(8,128)(2,1)} fusion(bf16[32,521,256]{2,1,0:T(8,128)(2,1)} %copy-done.1), kind=kLoop, calls=%fused_computation | loop fusion | flops 4063232 | bytes 8650752 | tf_op jit(solution)/shard_map/reduce_sum | solution.py:177
  303.8 4.3 %all-to-all-done.4 = f32[32,9,256]{2,1,0:T(8,128)S(1)} async-done(((f32[32,9,256]{2,1,0:T(8,128)}), f32[32,9,256]{2,1,0:T(8,128)S(1)}, u32[]{:S(2)}, u32[]{:S(2)}) %all-to-all-start.4) | async-done | bytes 294944 | tf_op jit(solution)/shard_map/all_to_all | solution.py:179
  308.2 0.1 reshape.19
  308.2 0.6 slice.29
  308.8 0.7 slice.28
  (2 shorter events, 0.1 us)
Async XLA Ops:
  0.6 137.4 %copy-start = (bf16[256,256]{1,0:T(8,128)(2,1)S(1)}, bf16[256,256]{1,0:T(8,128)(2,1)}, u32[]{:S(2)}) copy-start(bf16[256,256]{1,0:T(8,128)(2,1)} %param.11) | copy-start | bytes 393220
  107.6 30.5 %copy-start.2 = (bf16[512,256]{1,0:T(8,128)(2,1)S(1)}, bf16[512,256]{1,0:T(8,128)(2,1)}, u32[]{:S(2)}) copy-start(bf16[512,256]{1,0:T(8,128)(2,1)} %param.13) | copy-start | bytes 786436
  107.6 30.5 %copy-start.3 = (f32[256]{0:T(256)S(1)}, f32[256]{0:T(256)}, u32[]{:S(2)}) copy-start(f32[256]{0:T(256)} %param.12) | copy-start | bytes 3076
  286.4 3.3 %copy-start.1 = (bf16[32,521,256]{2,1,0:T(8,128)(2,1)}, bf16[32,521,256]{2,1,0:T(8,128)(2,1)S(1)}, u32[]{:S(2)}) copy-start(bf16[32,521,256]{2,1,0:T(8,128)(2,1)S(1)} %all_to_all.28) | copy-start | bytes 25608196
  290.7 17.5 %all-to-all-start.4 = ((f32[32,9,256]{2,1,0:T(8,128)}), f32[32,9,256]{2,1,0:T(8,128)S(1)}, u32[]{:S(2)}, u32[]{:S(2)}) async-start(f32[32,9,256]{2,1,0:T(8,128)} %broadcast_in_dim.11), calls=%async_computation.4 | async-start | bytes 1048576 | tf_op jit(solution)/shard_map/all_to_all | solution.py:179

commit v14 on v13

--- a/solution.py
+++ b/solution.py
@@ -124,6 +124,27 @@
     return got.astype(jnp.float32).sum(axis=0)
 
 
+def sum_kernel(x_ref, o_ref):
+    o_ref[...] = x_ref[0].astype(jnp.float32)
+
+    def add(i, carry):
+        o_ref[...] += x_ref[i].astype(jnp.float32)
+        return carry
+
+    lax.fori_loop(1, x_ref.shape[0], add, 0)
+
+
+def sum_parts(parts):
+    count, rows, width = parts.shape
+    return pl.pallas_call(
+        sum_kernel,
+        out_shape=jax.ShapeDtypeStruct((rows, width), jnp.float32),
+        in_specs=[pl.BlockSpec(memory_space=pltpu.VMEM)],
+        out_specs=pl.BlockSpec(memory_space=pltpu.VMEM),
+        compiler_params=pltpu.CompilerParams(vmem_limit_bytes=VMEM_LIMIT),
+    )(parts)
+
+
 def dense_part(hidden, weight, bias, cotangent):
     preact = jnp.dot(hidden, weight, preferred_element_type=jnp.float32) + bias
     output = jax.nn.silu(preact).astype(jnp.bfloat16)
@@ -174,8 +195,9 @@
         tile_values, tile_cols, live_counts, grad_tiles, pieces, column_tiles, chunk
     )
     got = lax.all_to_all(payload, "col", 0, 0, tiled=True)
-    feature_grad = got[:, :chunk].astype(jnp.float32).sum(axis=0).astype(jnp.bfloat16)
-    own_piece = got[:, chunk:].astype(jnp.float32).sum(axis=0)
+    col_sum = sum_parts(got)
+    feature_grad = col_sum[:chunk].astype(jnp.bfloat16)
+    own_piece = col_sum[chunk:]
     total = lax.all_to_all(
         jnp.broadcast_to(own_piece[None], (n_col, piece, width)), "col", 0, 0, tiled=True
     ).reshape(n_col * piece, width)

time: 315 us -> 319 us (1.013)
  Pallas kernels: 27.6 us -> 33.4 us
  other arithmetic: 5.91 us -> 0.39 us
  waiting for transfers between devices: 4.31 us -> 8.53 us
    pallas_call x0 -> x1, Pallas kernels: none -> 5.82 us  [sum_parts(): pl.pallas_call(sum_kernel, out_shape=jax.ShapeDtypeStruct((rows, width),...]
    reduce_sum x2 -> x0, other arithmetic: 5.52 us -> none  [the longest x1 5.46 us: per_device(): got[:, :chunk].astype(jnp.float32).sum(axis=0).astype(jnp.bfloat16)]
    all_to_all x1, waiting for transfers between devices: 4.31 us -> 8.53 us  [per_device(): lax.all_to_all(jnp.broadcast_to(own_piece[None], (n_col, piece, width)),...]
    unnamed x8 -> x6, local copies, waits for them, and re-layouts: 3.31 us -> 0.02 us
  transfers between devices with their start and end apart: 1 -> 1, of which waited for: 1 -> 1; matrix products, arithmetic and copies ran while one was open for 2% -> 1% of each run, Pallas kernels for 0% -> 0%
where the time goes in v14:
time: 319 us; the launch traced here: 314 us
  blocking collectives  253 us (79%)
  Pallas kernels  33.4 us (10%)
  local copies, waits for them, and re-layouts  8.64 us (3%)
  waiting for transfers between devices  8.53 us (3%)
  starting transfers between devices  7.93 us (2%)
    all_to_all x1, blocking collectives, per_device(): got = lax.all_to_all(payload, 'col', 0, 0, tiled=True)  107 us
    all_to_all x1, blocking collectives, gather_over(): got = lax.all_to_all(spread, axis, 0, 0, tiled=True)  105 us
    all_to_all x1, blocking collectives, per_device(): lax.all_to_all(jnp.broadcast_to(payload[None], (n_row,) + payload.shape),...  23.2 us
    all_to_all x1, blocking collectives, sum_scatter_over(): got = lax.all_to_all(parts, axis, 0, 0, tiled=True)  17.9 us
    pallas_call x1, Pallas kernels, aggregate_transposed(): pl.pallas_call(backward_kernel, out_shape=jax.ShapeDtypeStruct((n_col, ch...  15.4 us
    pallas_call x1, Pallas kernels, aggregate(): pl.pallas_call(forward_kernel, out_shape=jax.ShapeDtypeStruct((row_tiles,...  12.3 us
    all_to_all x1, waiting for transfers between devices, per_device(): lax.all_to_all(jnp.broadcast_to(own_piece[None], (n_col, piece, width)),...  8.53 us
    all_to_all x1, starting transfers between devices, per_device(): lax.all_to_all(jnp.broadcast_to(own_piece[None], (n_col, piece, width)),...  7.93 us
  transfers between devices with their start and end apart: 1, of which 1 were waited for; matrix products, arithmetic and copies ran while one was open for 1% of the time, Pallas kernels for 0%

profile of v14, /device:TPU:66, one launch (start us, length us, event | category | flops | bytes accessed | tf_op | source)
XLA Modules:
  0.0 314.4 jit_solution(3760898282349831141)
XLA Ops:
  0.6 0.0 copy-start
  0.6 1.9 broadcast_in_dim.8
  2.6 105.0 %all_to_all.25 = bf16[32,512,256]{2,1,0:T(8,128)(2,1)} all-to-all(bf16[32,512,256]{2,1,0:T(8,128)(2,1)S(1)} %broadcast_in_dim.8), channel_id=1, replica_groups=mesh['row'=4,'col'=32] {'col'}, dimensions={0} | all-to-all | bytes 16777216 | tf_op jit(solution)/shard_map/all_to_all | solution.py:116
  107.6 0.0 copy-start.1
  107.6 0.0 copy-start.2
  107.6 12.3 %shard_map.102 = bf16[8,256,256]{2,1,0:T(8,128)(2,1)} custom-call(s32[8,16]{1,0:T(8,128)} %cols_ref.3, s32[8]{0:T(128)} %bitcast.15, bf16[8,16,256,256]{3,2,1,0:T(8,128)(2,1)} %a_ref.3, bf16[64,256,256]{2,1,0:T(8,128)(2,1)} %bitcast.12), custom_call_target="tpu_custom_call" | custom-call | tf_op jit(solution)/shard_map/pallas_call | solution.py:71
  119.8 17.9 %all_to_all.26 = bf16[4,512,256]{2,1,0:T(8,128)(2,1)S(1)} all-to-all(bf16[4,512,256]{2,1,0:T(8,128)(2,1)} %bitcast.14), channel_id=1, replica_groups=mesh['row'=4,'col'=32] {'row'}, dimensions={0} | all-to-all | bytes 2097152 | tf_op jit(solution)/shard_map/all_to_all | solution.py:123
  137.8 0.3 reduce_sum.33
  138.1 0.0 copy-done
  138.1 0.0 copy-done.1
  138.1 0.0 copy-done.2
  138.1 1.1 convert_reduce_fusion
  139.2 0.3 fusion.3
  139.5 0.3 convolution_convert_fusion
  139.8 0.1 broadcast_in_dim.10
  139.9 23.2 %all_to_all.27 = bf16[4,800,256]{2,1,0:T(8,128)(2,1)S(1)} all-to-all(bf16[4,800,256]{2,1,0:T(8,128)(2,1)S(1)} %broadcast_in_dim.10), channel_id=1, replica_groups=mesh['row'=4,'col'=32] {'row'}, dimensions={0} | all-to-all | bytes 3276800 | tf_op jit(solution)/shard_map/all_to_all | solution.py:185
  163.1 0.1 slice_reduce_fusion
  163.2 0.8 reshape.18.w_ref
  164.0 1.1 slice.25
  165.1 15.4 %shard_map.103 = bf16[32,521,256]{2,1,0:T(8,128)(2,1)} custom-call(s32[8,16]{1,0:T(8,128)} %cols_ref.3, s32[8]{0:T(128)} %bitcast.16, bf16[8,16,256,256]{3,2,1,0:T(8,128)(2,1)} %a_ref.3, bf16[8,256,256]{2,1,0:T(8,128)(2,1)} %bitcast.13, bf16[32,9,256]{2,1,0:T(8,128)(2,1)} %reshape.18.w_ref), custom_call_target="tpu_custom_call" | custom-call | tf_op jit(solution)/shard_map/pallas_call | solution.py:95
  180.5 106.9 %all_to_all.28.x_ref = bf16[32,521,256]{2,1,0:T(8,128)(2,1)} all-to-all(bf16[32,521,256]{2,1,0:T(8,128)(2,1)} %shard_map.103), channel_id=1, replica_groups=mesh['row'=4,'col'=32] {'col'}, dimensions={0} | all-to-all | bytes 17072128 | tf_op jit(solution)/shard_map/all_to_all | solution.py:197
  287.4 5.8 %shard_map.104 = f32[521,256]{1,0:T(8,128)} custom-call(bf16[32,521,256]{2,1,0:T(8,128)(2,1)} %all_to_all.28.x_ref), custom_call_target="tpu_custom_call" | custom-call | tf_op jit(solution)/shard_map/pallas_call | solution.py:139
  293.2 0.7 slice.28
  293.9 0.9 broadcast_in_dim.11
  294.8 7.9 %all-to-all-start.4 = ((f32[32,9,256]{2,1,0:T(8,128)}), f32[32,9,256]{2,1,0:T(8,128)S(1)}, u32[]{:S(2)}, u32[]{:S(2)}) async-start(f32[32,9,256]{2,1,0:T(8,128)} %broadcast_in_dim.11), calls=%async_computation.4 | async-start | bytes 1048576 | tf_op jit(solution)/shard_map/all_to_all | solution.py:201
  302.7 1.8 slice.33
  304.5 8.5 %all-to-all-done.4 = f32[32,9,256]{2,1,0:T(8,128)S(1)} async-done(((f32[32,9,256]{2,1,0:T(8,128)}), f32[32,9,256]{2,1,0:T(8,128)S(1)}, u32[]{:S(2)}, u32[]{:S(2)}) %all-to-all-start.4) | async-done | bytes 294944 | tf_op jit(solution)/shard_map/all_to_all | solution.py:201
  313.0 0.1 reshape.19
  313.1 0.6 slice.30
  313.7 0.7 slice.29
  (2 shorter events, 0.1 us)
Async XLA Ops:
  0.6 137.4 %copy-start = (bf16[256,256]{1,0:T(8,128)(2,1)S(1)}, bf16[256,256]{1,0:T(8,128)(2,1)}, u32[]{:S(2)}) copy-start(bf16[256,256]{1,0:T(8,128)(2,1)} %param.11) | copy-start | bytes 393220
  107.6 30.5 %copy-start.1 = (bf16[512,256]{1,0:T(8,128)(2,1)S(1)}, bf16[512,256]{1,0:T(8,128)(2,1)}, u32[]{:S(2)}) copy-start(bf16[512,256]{1,0:T(8,128)(2,1)} %param.13) | copy-start | bytes 786436
  107.6 30.5 %copy-start.2 = (f32[256]{0:T(256)S(1)}, f32[256]{0:T(256)}, u32[]{:S(2)}) copy-start(f32[256]{0:T(256)} %param.12) | copy-start | bytes 3076
  294.8 18.2 %all-to-all-start.4 = ((f32[32,9,256]{2,1,0:T(8,128)}), f32[32,9,256]{2,1,0:T(8,128)S(1)}, u32[]{:S(2)}, u32[]{:S(2)}) async-start(f32[32,9,256]{2,1,0:T(8,128)} %broadcast_in_dim.11), calls=%async_computation.4 | async-start | bytes 1048576 | tf_op jit(solution)/shard_map/all_to_all | solution.py:201
